TPU v7x, 32 devices: a whole 2x2x4 slice. The times are simulated.
32 devices in a mesh: scen: 8 (over z, y), rows: 2 (over x), section: 2 (over core).
Axes of the slice: x: 2, y: 2, z: 4, core: 2. Of those that a mesh axis runs over, the one named last changes fastest.
Arguments:
- lp_blocks: bfloat16 [192, 2, 4, 2, 128, 128], P('scen', 'rows', 'section'), may hold values from -0.1875 to 0.1875
- block_columns: int32 [192, 2, 4, 2], P('scen', None, 'section'), may hold values from 0 to 175
- scenario_nodes: int32 [3, 192], P(None, 'scen'), may hold values from 0 to 511, as said below
- scenario_weights: float32 [192], P('scen'), may hold values from 0.5 to 4.5
- cost: bfloat16 [192, 4, 22528], P('scen', 'section'), may hold values from -6 to 6
- bounds_rhs: float32 [192, 256], P('scen', 'rows'), may hold values from -6 to 6
- primal_start: bfloat16 [192, 4, 22528], P('scen', 'section'), may hold values from 0 to 2
- dual_start: float32 [192, 256], P('scen', 'rows'), may hold values from 0 to 1
- multiplier_start: float32 [192, 4, 512], P('scen', 'section'), may hold values from -3 to 3
- consensus_start: float32 [585, 512], replicated, may hold values from 0 to 2
Outputs:
- primal: float32 [192, 4, 22528], P('scen', 'section')
- dual: float32 [192, 256], P('scen', 'rows')
- multiplier: float32 [192, 4, 512], P('scen', 'section')
- penalty: float32 [], replicated
Inputs may be any that keep to these rules, and one draw needn't show every extreme that they name: `scenario_nodes`: node ids never fall from one scenario to the next at any section; the section-three node is the section-four node // 8 and the section-two node the section-three node // 8; the first scenario lies in node 0 and the last in node 511 of section four.
All inputs are finite; a program needn't handle non-finite values.
Results may differ from a plain program's by a relative error of at most 0.0018.
Values sent between devices are 32-bit elements; how exact they have to be, the bound alone decides.
No kernel may reach another device: no remote copies, remote signals or barrier semaphores. Data moves between devices by JAX's collectives and lax.ppermute only.
A program may use at most 128 MiB of HBM per device.

v0:
```python
import jax
import jax.numpy as jnp
from jax import lax
from jax.sharding import PartitionSpec as P

BLK = 128
CPS = 176
N1 = 8
SWEEPS = 2
N2 = 64
NODES = 585


TAU_STEP = 0.4
SIGMA_STEP = 0.4
RHO_START = 1.0
EPSILON = 1e-06


def averaged(node_table, node_mass):
    positive = node_mass > 0
    safe_mass = jnp.where(positive, node_mass, 1.0)
    return jnp.where(positive[:, None], node_table / safe_mass[:, None], 0.0)


def local(
    lp_blocks,
    block_columns,
    scenario_nodes,
    scenario_weights,
    cost,
    bounds_rhs,
    primal_start,
    dual_start,
    multiplier_start,
    consensus_start,
):
    scenario_count = cost.shape[0]
    local_sections = cost.shape[1]
    columns = cost.shape[2]
    hedged = multiplier_start.shape[2]
    row_blocks = dual_start.shape[1] // BLK
    section_index = lax.axis_index("section")
    row_index = lax.axis_index("rows")
    selector = (block_columns[..., None] == jnp.arange(CPS, dtype=jnp.int32)).astype(jnp.float32)
    local_selector = lax.dynamic_slice_in_dim(
        selector, row_index * row_blocks, row_blocks, 1
    ).astype(jnp.bfloat16)
    offsets = jnp.array([1, 1 + N1, 1 + N1 + N2], jnp.int32)
    node_rows = jnp.concatenate(
        [jnp.zeros((1, scenario_count), jnp.int32), scenario_nodes + offsets[:, None]], axis=0
    )
    local_rows = lax.dynamic_slice_in_dim(
        node_rows, section_index * local_sections, local_sections, 0
    )
    membership = (
        local_rows[:, None, :] == jnp.arange(NODES, dtype=jnp.int32)[None, :, None]
    ).astype(jnp.float32)
    cost_full = cost.astype(jnp.float32)

    def spread(table):
        return jnp.einsum("jns,nc->sjc", membership, table, precision=lax.Precision.HIGHEST)

    penalty = jnp.asarray(RHO_START, jnp.float32)
    primal = primal_start.astype(jnp.float32)
    dual, multiplier, previous = (dual_start, multiplier_start, consensus_start)
    for sweep_index in range(SWEEPS):
        anchors = spread(previous)
        dual_half = dual.reshape(scenario_count, row_blocks, BLK).astype(jnp.bfloat16)
        pieces = jnp.einsum(
            "srjnab,sra->srjnb", lp_blocks, dual_half, preferred_element_type=jnp.float32
        )
        gathered = lax.all_gather(pieces, "rows", axis=1, tiled=True)
        placed = jnp.einsum(
            "srjnc,srjnb->sjcb", selector, gathered, precision=lax.Precision.HIGHEST
        )
        adjoint = placed.reshape(scenario_count, local_sections, columns)
        hedge_term = multiplier + penalty * (primal[:, :, :hedged] - anchors)
        hedge_full = jnp.pad(hedge_term, ((0, 0), (0, 0), (0, columns - hedged)))
        primal_next = jnp.maximum(primal - TAU_STEP * (cost_full + adjoint + hedge_full), 0.0)
        step_half = (2.0 * primal_next - primal).astype(jnp.bfloat16)
        blocks = step_half.reshape(scenario_count, local_sections, CPS, BLK)
        picked = jnp.einsum(
            "srjnc,sjcb->srjnb", local_selector, blocks, preferred_element_type=jnp.float32
        ).astype(jnp.bfloat16)
        image = lax.psum(
            jnp.einsum("srjnab,srjnb->sra", lp_blocks, picked, preferred_element_type=jnp.float32),
            "section",
        )
        dual_next = jnp.maximum(
            dual + SIGMA_STEP * (image.reshape(scenario_count, -1) - bounds_rhs), 0.0
        )
        hedged_next = primal_next[:, :, :hedged]
        weighted = scenario_weights[:, None, None] * hedged_next
        node_table, node_mass = lax.psum(
            (
                jnp.einsum("jns,sjc->nc", membership, weighted, precision=lax.Precision.HIGHEST),
                jnp.einsum(
                    "jns,s->n", membership, scenario_weights, precision=lax.Precision.HIGHEST
                ),
            ),
            "scen",
        )
        consensus = averaged(node_table, node_mass)
        new_anchors = spread(consensus)
        gap_local = jnp.sum(scenario_weights[:, None, None] * (hedged_next - new_anchors) ** 2)
        drift_local = jnp.sum(scenario_weights[:, None, None] * (new_anchors - anchors) ** 2)
        primal_gap, drift_gap = lax.psum((gap_local, drift_local), ("scen", "section"))
        multiplier = multiplier + penalty * (hedged_next - new_anchors)
        penalty = penalty * jnp.sqrt(primal_gap / (drift_gap + EPSILON))
        primal, dual, previous = (primal_next, dual_next, consensus)
    return (primal, dual, multiplier, penalty)


def solution(mesh):
    in_specs = (
        P("scen", "rows", "section", None, None, None),
        P("scen", None, "section", None),
        P(None, "scen"),
        P("scen"),
        P("scen", "section", None),
        P("scen", "rows"),
        P("scen", "section", None),
        P("scen", "rows"),
        P("scen", "section", None),
        P(),
    )
    out_specs = (P("scen", "section", None), P("scen", "rows"), P("scen", "section", None), P())
    return jax.shard_map(local, mesh=mesh, in_specs=in_specs, out_specs=out_specs, check_vma=False)
```

profile of v0, /device:TPU:0, one launch (start us, length us, event | category | flops | bytes accessed | tf_op | source)
XLA Modules:
  0.0 297.4 jit_solution(1320190035164285401)
XLA Ops:
  8.1 1.0 copy-done
  9.7 5.7 %all-gather = f32[24,4,2,128]{3,0,2,1:T(8,128)S(1)} all-gather(f32[24,2,2,128]{3,0,2,1:T(8,128)S(1)} %bitcast.114), channel_id=2, replica_groups=mesh['scen'=8,'rows'=2,'section'=2] {'rows'}, dimensions={1}, use_global_device_ids=true | all-gather | bytes 147456 | tf_op jit(solution)/shard_map/all_gather | solution.py:73
  15.4 3.8 %fusion.53 = f32[24,2,176,128,1]{3,2,1,0,4:T(8,128)S(1)} fusion(f32[24,2,2,2,128]{4,0,3,2,1:T(8,128)S(1)} %bitcast.113, s32[24,2,2,2]{3,2,0,1:T(2,128)S(1)} %copy.45), kind=kOutput, calls=%fused_computation.58 | convolution fusion | flops 51938304 | bytes 4424448 | tf_op jit(solution)/shard_map/srjnc,srjnb->sjcb/dot_general | solution.py:74
  19.2 2.4 copy.119
  21.6 5.4 %reshape.65 = f32[24,2,22528]{2,0,1:T(8,128)} reshape(f32[24,2,176,128]{3,2,0,1:T(8,128)} %bitcast.103) | data formatting | bytes 8650752 | tf_op jit(solution)/shard_map/reshape | solution.py:77
  26.9 4.4 %copy_convert_fusion = f32[24,2,22528]{2,0,1:T(8,128)} fusion(bf16[24,2,22528]{2,1,0:T(2,128)(2,1)} %param.17), kind=kLoop, calls=%fused_computation.26 | loop fusion | flops 1081344 | bytes 6488064 | tf_op jit(solution)/shard_map/convert_element_type | solution.py:65
  31.4 1.9 fusion.50
  33.3 5.4 %subtract_convert_fusion.1 = (bf16[24,2,22528]{2,0,1:T(8,128)(2,1)}, f32[24,2,22528]{2,0,1:T(8,128)S(1)}) fusion(bf16[24,2,22528]{2,1,0:T(2,128)(2,1)} %param.17, f32[24,2,512]{2,0,1:T(8,128)S(1)} %get-tuple-element.29, f32[24,2,22528]{2,0,1:T(8,128)} %reshape.65, bf16[24,2,22528]{2,1,0:T(2,128)(2,1)} %param.15), kind=kLoop, calls=%fused_computation.13 | loop fusion | flops 10813440 | bytes 15237120 | tf_op jit(solution)/shard_map/convert_element_type | solution.py:81
  38.7 2.0 copy-done.1
  40.7 1.8 convolution_bitcast_fusion.1
  42.8 3.3 %copy.72 = bf16[6,8,176,128]{3,2,1,0:T(8,128)(2,1)} copy(bf16[6,8,176,128]{3,1,2,0:T(8,128)(2,1)} %bitcast.106) | data formatting | bytes 4325376
  46.1 2.3 fusion.40
  49.3 3.3 %psum.66 = f32[24,128]{1,0:T(8,128)S(1)} all-reduce(f32[24,128]{1,0:T(8,128)S(1)} %bitcast.117), channel_id=1, replica_groups=mesh['scen'=8,'rows'=2,'section'=2] {'section'}, use_global_device_ids=true, to_apply=%region_0.1 | all-reduce | flops 3072 | bytes 24576 | tf_op jit(solution)/shard_map/psum | solution.py:86
  53.2 5.1 %all-gather.1 = f32[24,4,2,128]{3,0,2,1:T(8,128)S(1)} all-gather(f32[24,2,2,128]{3,0,2,1:T(8,128)S(1)} %bitcast.115), channel_id=3, replica_groups=mesh['scen'=8,'rows'=2,'section'=2] {'rows'}, dimensions={1}, use_global_device_ids=true | all-gather | bytes 147456 | tf_op jit(solution)/shard_map/all_gather | solution.py:73
  58.3 3.8 %fusion.51 = f32[24,2,176,128,1]{3,2,1,0,4:T(8,128)S(1)} fusion(f32[24,2,2,2,128]{4,0,3,2,1:T(8,128)S(1)} %bitcast.112, s32[24,2,2,2]{3,2,0,1:T(2,128)S(1)} %copy.45), kind=kOutput, calls=%fused_computation.56 | convolution fusion | flops 51938304 | bytes 4424448 | tf_op jit(solution)/shard_map/srjnc,srjnb->sjcb/dot_general | solution.py:74
  62.1 2.4 copy.118
  64.5 5.4 %reshape.70 = f32[24,2,22528]{2,0,1:T(8,128)} reshape(f32[24,2,176,128]{3,2,0,1:T(8,128)} %bitcast.104) | data formatting | bytes 8650752 | tf_op jit(solution)/shard_map/reshape | solution.py:77
  70.2 22.1 %psum.67 = f32[585]{0:T(1024)S(1)} all-reduce(f32[585]{0:T(1024)S(1)} %convolution_reduce_fusion), channel_id=1, replica_groups=mesh['scen'=8,'rows'=2,'section'=2] {'scen'}, use_global_device_ids=true, to_apply=%region_2.3 | all-reduce | flops 585 | bytes 4680 | tf_op jit(solution)/shard_map/psum | solution.py:95
  92.3 33.4 %all-reduce.8.cloned.1.call-done = f32[585,512]{1,0:T(8,128)} async-done(((f32[585,512]{1,0:T(8,128)}), f32[585,512]{1,0:T(8,128)}) %all-reduce.8.cloned.1.call-update) | async-done | bytes 1198096 | tf_op jit(solution)/shard_map/psum | solution.py:95
  125.8 2.1 fusion.25
  127.8 1.6 multiply_reduce_fusion.2
  129.4 31.8 %all-reduce.4 = (f32[]{:T(128)}, f32[]{:T(128)}) all-reduce(f32[]{:T(128)} %get-tuple-element.19, f32[]{:T(128)} %get-tuple-element.18), channel_id=1, replica_groups=mesh['scen'=8,'rows'=2,'section'=2] {'scen','section'}, use_global_device_ids=true, to_apply=%region_5.6 | all-reduce | flops 2 | bytes 16 | tf_op jit(solution)/shard_map/psum | solution.py:108
  162.6 0.9 multiply_add_fusion.1
  163.5 5.7 %subtract_convert_fusion = (bf16[24,2,22528]{2,0,1:T(8,128)(2,1)}, f32[24,2,22528]{2,0,1:T(8,128)S(1)}) fusion(f32[24,2,22528]{2,0,1:T(8,128)} %copy-done.1, f32[24,2,512]{2,0,1:T(8,128)S(1)} %multiply_add_fusion.1, f32[24,2,22528]{2,0,1:T(8,128)} %reshape.70, bf16[24,2,22528]{2,1,0:T(2,128)(2,1)} %param.15), kind=kLoop, calls=%fused_computation.12 | loop fusion | flops 9732096 | bytes 17399808 | tf_op jit(solution)/shard_map/convert_element_type | solution.py:81
  169.3 2.0 copy-done.2
  171.3 1.8 convolution_bitcast_fusion
  173.1 7.8 %copy.54 = f32[24,2,22528]{2,1,0:T(2,128)} copy(f32[24,2,22528]{2,0,1:T(8,128)} %copy-done.2) | data formatting | bytes 8650752
  183.4 3.3 %psum.71 = f32[24,128]{1,0:T(8,128)S(1)} all-reduce(f32[24,128]{1,0:T(8,128)S(1)} %bitcast.118), channel_id=1, replica_groups=mesh['scen'=8,'rows'=2,'section'=2] {'section'}, use_global_device_ids=true, to_apply=%region_8.9 | all-reduce | flops 3072 | bytes 24576 | tf_op jit(solution)/shard_map/psum | solution.py:86
  187.3 64.4 %all-reduce.10.cloned.1.call-done = f32[585,512]{1,0:T(8,128)} async-done(((f32[585,512]{1,0:T(8,128)}), f32[585,512]{1,0:T(8,128)}) %all-reduce.10.cloned.1.call-update) | async-done | bytes 1198096 | tf_op jit(solution)/shard_map/psum | solution.py:95
  251.7 2.1 fusion.22
  253.8 1.7 multiply_reduce_fusion
  256.2 31.9 %all-reduce.3 = (f32[]{:T(128)}, f32[]{:T(128)}) all-reduce(f32[]{:T(128)} %get-tuple-element.17, f32[]{:T(128)} %get-tuple-element.16), channel_id=1, replica_groups=mesh['scen'=8,'rows'=2,'section'=2] {'scen','section'}, use_global_device_ids=true, to_apply=%region_11.12 | all-reduce | flops 2 | bytes 16 | tf_op jit(solution)/shard_map/psum | solution.py:108
  (52 shorter events, 7.5 us)
Async XLA Ops:
  7.2 1.9 copy-start
  7.2 2.4 copy-start.12
  7.2 118.6 %all-reduce.8.cloned.1.call-start = ((), (), s32[]{:S(2)}) async-start(), calls=%async_computation | async-start | bytes 2424832 | tf_op jit(solution)/shard_map/psum | solution.py:95
  26.9 4.4 %copy-start.13 = (s32[3,24]{1,0:T(4,128)S(1)}, s32[3,24]{1,0:T(4,128)}, u32[]{:S(2)}) copy-start(s32[3,24]{1,0:T(4,128)} %param.13) | copy-start | bytes 868
  26.9 4.4 %copy-start.14 = (s32[3]{0:T(128)S(1)}, s32[3]{0:T(128)}, u32[]{:S(2)}) copy-start(s32[3]{0:T(128)} %constant.8.clone) | copy-start | bytes 40
  26.9 4.5 %copy-start.4 = (f32[24,2,512]{2,1,0:T(2,128)S(1)}, f32[24,2,512]{2,1,0:T(2,128)}, u32[]{:S(2)}) copy-start(f32[24,2,512]{2,1,0:T(2,128)} %param.19) | copy-start | bytes 294916
  33.3 7.4 %copy-start.10 = (f32[24]{0:T(128)S(1)}, f32[24]{0:T(128)}, u32[]{:S(2)}) copy-start(f32[24]{0:T(128)} %param.14) | copy-start | bytes 292
  38.7 2.0 copy-start.1
  42.5 209.2 %all-reduce.10.cloned.1.call-start = ((), (), s32[]{:S(2)}) async-start(), calls=%async_computation.1 | async-start | bytes 2424832 | tf_op jit(solution)/shard_map/psum | solution.py:95
  42.8 5.6 %copy-start.6 = (pred[24,2,2,2,176]{4,3,2,0,1:T(4,128)(4,1)}, pred[24,2,2,2,176]{4,3,2,0,1:T(4,128)(4,1)S(1)}, u32[]{:S(2)}) copy-start(pred[24,2,2,2,176]{4,3,2,0,1:T(4,128)(4,1)S(1)} %iota_compare_fusion) | copy-start | bytes 101380
  46.1 6.5 %copy-start.5 = (f32[24,128]{1,0:T(8,128)S(1)}, f32[24,128]{1,0:T(8,128)}, u32[]{:S(2)}) copy-start(f32[24,128]{1,0:T(8,128)} %param.18) | copy-start | bytes 36868
  46.1 6.5 %copy-start.8 = (f32[24,128]{1,0:T(8,128)S(1)}, f32[24,128]{1,0:T(8,128)}, u32[]{:S(2)}) copy-start(f32[24,128]{1,0:T(8,128)} %param.16) | copy-start | bytes 36868
  64.5 5.5 %copy-start.11 = (f32[24]{0:T(128)S(1)}, f32[24]{0:T(128)}, u32[]{:S(2)}) copy-start(f32[24]{0:T(128)} %param.14) | copy-start | bytes 292
  169.3 2.0 copy-start.2
  173.1 7.8 %copy-start.3 = (bf16[24,2,22528]{2,0,1:T(8,128)(2,1)S(1)}, bf16[24,2,22528]{2,0,1:T(8,128)(2,1)}, u32[]{:S(2)}) copy-start(bf16[24,2,22528]{2,0,1:T(8,128)(2,1)} %get-tuple-element.24) | copy-start | bytes 6488068
  180.9 0.9 copy-start.7
  181.8 4.9 %copy-start.9 = (f32[24,128]{1,0:T(8,128)S(1)}, f32[24,128]{1,0:T(8,128)}, u32[]{:S(2)}) copy-start(f32[24,128]{1,0:T(8,128)} %param.16) | copy-start | bytes 36868
Sparse Core Ops, SparseCore 0:
  42.7 83.0 all-reduce.7
  173.3 78.4 all-reduce.9
where the time goes:
time: 298 us; the launch traced here: 297 us
  blocking collectives  103 us (35%)
  waiting for transfers between devices  97.9 us (33%)
  local copies, waits for them, and re-layouts  33.3 us (11%)
  matrix products  23.3 us (8%)
  other arithmetic  21.6 us (7%)
  between operations  18.1 us (6%)
    psum x2, waiting for transfers between devices, local(): lax.psum((jnp.einsum('jns,sjc->nc', membership, weighted, precision=lax.P...  97.8 us
    psum x2, blocking collectives, local(): lax.psum((gap_local, drift_local), ('scen', 'section'))  63.7 us
    psum x1, blocking collectives, local(): lax.psum((jnp.einsum('jns,sjc->nc', membership, weighted, precision=lax.P...  22.1 us
    unnamed x35, local copies, waits for them, and re-layouts  17.8 us
    convert_element_type x2, other arithmetic, local(): step_half = (2.0 * primal_next - primal).astype(jnp.bfloat16)  11.1 us
    reshape x2, local copies, waits for them, and re-layouts, local(): adjoint = placed.reshape(scenario_count, local_sections, columns)  10.8 us
    all_gather x2, blocking collectives, local(): gathered = lax.all_gather(pieces, 'rows', axis=1, tiled=True)  10.8 us
    dot_general x2, matrix products, local(): jnp.einsum('srjnc,srjnb->sjcb', selector, gathered, precision=lax.Precisi...  7.67 us
  transfers between devices with their start and end apart: 2, of which 2 were waited for; matrix products, arithmetic and copies ran while one was open for 10% of the time, Pallas kernels for 0%

commit v1 on v0

v1 whole, which is shorter than its diff:
```python
import functools

import jax
import jax.numpy as jnp
from jax import lax
from jax.experimental import pallas as pl
from jax.experimental.pallas import tpu as pltpu
from jax.sharding import PartitionSpec as P

BLK = 128
N1 = 8
N2 = 64
SWEEPS = 2
TAU_STEP = 0.4
SIGMA_STEP = 0.4
RHO_START = 1.0
EPSILON = 1e-06
MIB = 1 << 20
F32 = jnp.float32
BF16 = jnp.bfloat16
HIGHEST = lax.Precision.HIGHEST

VMEM = pl.BlockSpec(memory_space=pltpu.VMEM)
SMEM = pl.BlockSpec(memory_space=pltpu.SMEM)


def params(mib):
    return pltpu.CompilerParams(vmem_limit_bytes=mib * MIB)


def shape(*dims, dtype=F32):
    return jax.ShapeDtypeStruct(dims, dtype)


def write_pieces(lp_ref, dual, out_ref, S, J, NZ):
    for s in range(S):
        row = dual[s : s + 1, :].astype(BF16)
        for j in range(J):
            for n in range(NZ):
                y = jnp.dot(row, lp_ref[s, j * NZ + n], preferred_element_type=F32)
                out_ref[pl.ds((n * J + j) * S + s, 1), :] = y


def write_image(lp_ref, step_ref, own, image_ref, S, J, NZ):
    Q = J * S
    for s in range(S):
        total = None
        for j in range(J):
            for n in range(NZ):
                x = step_ref[pl.ds((own * NZ + n) * Q + j * S + s, 1), :].astype(BF16)
                y = lax.dot_general(
                    x,
                    lp_ref[s, j * NZ + n],
                    (((1,), (1,)), ((), ())),
                    preferred_element_type=F32,
                )
                total = y if total is None else total + y
        image_ref[pl.ds(s, 1), :] = total


def pieces_kernel(S, J, NZ, lp_ref, dual_ref, out_ref):
    write_pieces(lp_ref, dual_ref[...], out_ref, S, J, NZ)


def dual_kernel(S, J, NZ, lp_ref, dual_ref, rhs_ref, image_ref, image2_ref, next_ref, out_ref):
    image = image_ref[...] + image2_ref[...]
    dual = jnp.maximum(dual_ref[...] + SIGMA_STEP * (image - rhs_ref[...]), 0.0)
    next_ref[...] = dual
    write_pieces(lp_ref, dual, out_ref, S, J, NZ)


def setup_kernel(
    S,
    J,
    R,
    NZ,
    HB,
    cols_ref,
    nodes_ref,
    weights_ref,
    primal_ref,
    cost_ref,
    mult_ref,
    table_ref,
    pp_ref,
    pc_ref,
    hp_ref,
    hc_ref,
    cb_ref,
    ml_ref,
    an_ref,
    id_ref,
    wb_ref,
    ts_ref,
    idx_sc,
    pp_sc,
    pc_sc,
    hp_sc,
    hc_sc,
):
    K, Q = R * NZ, J * S
    section = lax.axis_index("section")
    rows = primal_ref.shape[1]
    nodes = table_ref.shape[0]
    for s in range(S):
        for j in range(J):
            for k in range(K):
                c = cols_ref[s, k // NZ, j, k % NZ]
                idx_sc[pl.ds((s * K + k) * J + j, 1), :] = jnp.full(
                    (1, BLK), c * J + j, jnp.int32
                )
    for j in range(J):
        g = section * J + j
        level = jnp.maximum(g - 1, 0)
        off = jnp.where(g == 0, 0, jnp.where(g == 1, 1, jnp.where(g == 2, 1 + N1, 1 + N1 + N2)))
        keep = jnp.where(g == 0, 0, 1)
        for s in range(S):
            node = nodes_ref[level, s] * keep + off
            q = j * S + s
            id_ref[pl.ds(q, 1), :] = jnp.full((1, BLK), node, jnp.int32).astype(F32)
            wb_ref[pl.ds(q, 1), :] = jnp.full((1, BLK), weights_ref[s], F32)
            line = table_ref[pl.ds(node, 1), :]
            for h in range(HB):
                an_ref[pl.ds(h * Q + q, 1), :] = line[:, h * BLK : (h + 1) * BLK]
    tiles = -(-rows // BLK)
    lane = lax.broadcasted_iota(jnp.int32, (K * J, BLK), 1)
    for s in range(S):
        want = idx_sc[pl.ds(s * K * J, K * J), :]
        pick = jnp.concatenate(
            [(want == lane + t * BLK).astype(F32).astype(BF16) for t in range(tiles)], axis=1
        )[:, :rows]
        pp_sc[pl.ds(s * K * J, K * J), :] = jnp.dot(pick, primal_ref[s], preferred_element_type=F32)
        pc_sc[pl.ds(s * K * J, K * J), :] = jnp.dot(pick, cost_ref[s], preferred_element_type=F32)
        hp_sc[pl.ds(s * HB * J, HB * J), :] = primal_ref[s, : HB * J, :].astype(F32)
        hc_sc[pl.ds(s * HB * J, HB * J), :] = cost_ref[s, : HB * J, :].astype(F32)
    for j in range(J):
        for k in range(K):
            src, dst = pl.ds(k * J + j, S, stride=K * J), pl.ds(k * Q + j * S, S)
            pp_ref[dst, :] = pp_sc[src, :]
            pc_ref[dst, :] = pc_sc[src, :]
            cb_ref[dst, :] = (idx_sc[src, :] - j).astype(F32)
        for h in range(HB):
            src, dst = pl.ds(h * J + j, S, stride=HB * J), pl.ds(h * Q + j * S, S)
            hp_ref[dst, :] = hp_sc[src, :]
            hc_ref[dst, :] = hc_sc[src, :]
            ml_ref[dst, :] = mult_ref[src, :]
    rest = table_ref[...]
    for part in range(3):
        high = rest.astype(BF16)
        ts_ref[part, :nodes, :] = high
        rest = rest - high.astype(F32)
    ts_ref[:, nodes:, :] = jnp.zeros_like(ts_ref[:, nodes:, :])


def total(x):
    return jnp.sum(x, axis=(0, 1), keepdims=True)


def primal_step(
    S, J, R, NZ, HB, own, pieces_ref, other_refs, p_ref, pc_ref, h_ref, hc_ref, cb_ref, hedge, all_sc
):
    K, Q = R * NZ, J * S
    for shift in range(R):
        src = pieces_ref if shift == 0 else other_refs[shift - 1]
        at = lax.rem(own + shift, R) * (NZ * Q)
        all_sc[pl.ds(pl.multiple_of(at, 8), NZ * Q), :] = src[...]
    slot = lambda ref, k: ref[k * Q : (k + 1) * Q, :]
    cols = [slot(cb_ref, k) for k in range(K)]
    parts = [slot(all_sc, k) for k in range(K)]
    placed, hedged = [], []
    for k in range(K):
        add = None
        for m in range(K):
            term = parts[m] if m == k else jnp.where(cols[m] == cols[k], parts[m], 0.0)
            add = term if add is None else add + term
        for h in range(HB):
            add = add + jnp.where(cols[k] == float(h * J), hedge[h], 0.0)
        placed.append(
            jnp.maximum(slot(p_ref, k) - TAU_STEP * (slot(pc_ref, k) + add), 0.0)
        )
    for h in range(HB):
        add = None
        for m in range(K):
            term = jnp.where(cols[m] == float(h * J), parts[m], 0.0)
            add = term if add is None else add + term
        add = add + hedge[h]
        hedged.append(jnp.maximum(slot(h_ref, h) - TAU_STEP * (slot(hc_ref, h) + add), 0.0))
    return placed, hedged


def finish_step(
    S, J, R, NZ, HB, own, lp_ref, p_ref, placed, hedged, anchors, ids, wb, p_out, h_out, mu_ref, image_ref, send_ref, step_sc, send_sc
):
    K, Q = R * NZ, J * S
    for k in range(K):
        p_out[k * Q : (k + 1) * Q, :] = placed[k]
        step_sc[k * Q : (k + 1) * Q, :] = 2.0 * placed[k] - p_ref[k * Q : (k + 1) * Q, :]
    for h in range(HB):
        h_out[h * Q : (h + 1) * Q, :] = hedged[h]
    across = jnp.transpose(ids)[0:1, :Q]
    same = (jnp.broadcast_to(ids[:, :1], (Q, Q)) == across).astype(F32)
    sums = jnp.dot(
        same,
        jnp.concatenate([wb * x for x in hedged] + [wb], axis=1),
        precision=HIGHEST,
        preferred_element_type=F32,
    )
    mass = sums[:, HB * BLK :]
    inner = []
    for j in range(J):
        mine = ids[j * S : (j + 1) * S]
        inner.append((mine != mine[:1]) & (mine != mine[S - 1 :]))
    inner = jnp.concatenate([x.astype(F32) for x in inner], axis=0)
    gap, drift = jnp.zeros((Q, BLK), F32), jnp.zeros((Q, BLK), F32)
    for h in range(HB):
        mu = sums[:, h * BLK : (h + 1) * BLK] / mass
        mu_ref[h * Q : (h + 1) * Q, :] = mu
        gap = gap + wb * (hedged[h] - mu) ** 2
        drift = drift + (wb * inner) * (mu - anchors[h]) ** 2
    lane = lax.broadcasted_iota(jnp.int32, (1, BLK), 1)
    note = jnp.zeros((1, BLK), F32)
    for j in range(J):
        a, b = j * S, j * S + S - 1
        fresh = ids[b : b + 1] != ids[a : a + 1]
        for f in range(2):
            e = f * J + j
            at = b if f else a
            for h in range(HB):
                line = sums[at : at + 1, h * BLK : (h + 1) * BLK]
                send_sc[pl.ds(e * HB + h, 1), :] = jnp.where(fresh, line, 0.0) if f else line
            name, weight = ids[at : at + 1], mass[at : at + 1]
            if f:
                name, weight = jnp.where(fresh, name, -1.0), jnp.where(fresh, weight, 0.0)
            note = jnp.where(lane == e, name, note)
            note = jnp.where(lane == 2 * J + e, weight, note)
    note = jnp.where(lane == 4 * J, total(gap), note)
    note = jnp.where(lane == 4 * J + 1, total(drift), note)
    at = 2 * J * HB
    send_sc[pl.ds(at, 1), :] = note
    send_sc[pl.ds(at + 1, send_sc.shape[0] - at - 1), :] = jnp.zeros(
        (send_sc.shape[0] - at - 1, BLK), F32
    )
    message = send_sc[...]
    for d in range(send_ref.shape[0]):
        send_ref[d] = message
    write_image(lp_ref, step_sc, own, image_ref, S, J, NZ)


def first_kernel(
    S, J, R, NZ, HB, lp_ref, pp_ref, pc_ref, hp_ref, hc_ref, cb_ref, ml_ref, an_ref, id_ref, wb_ref, pieces_ref, *rest
):
    other_refs = rest[: R - 1]
    p_out, h_out, mu_ref, image_ref, send_ref, all_sc, step_sc, send_sc = rest[R - 1 :]
    Q = J * S
    own = lax.axis_index("rows")
    slot = lambda ref, k: ref[k * Q : (k + 1) * Q, :]
    anchors = [slot(an_ref, h) for h in range(HB)]
    hedge = [
        slot(ml_ref, h) + RHO_START * (slot(hp_ref, h) - anchors[h]) for h in range(HB)
    ]
    placed, hedged = primal_step(
        S, J, R, NZ, HB, own, pieces_ref, other_refs, pp_ref, pc_ref, hp_ref, hc_ref, cb_ref, hedge, all_sc
    )
    finish_step(
        S, J, R, NZ, HB, own, lp_ref, pp_ref, placed, hedged, anchors, id_ref[...], wb_ref[...], p_out, h_out, mu_ref, image_ref, send_ref, step_sc, send_sc
    )


def read_nodes(J, HB, got_ref, ids, devices):
    step = got_ref.shape[0] // devices
    E = 2 * J
    sums = [
        jnp.concatenate(
            [got_ref[pl.ds(e * HB + h, devices, stride=step), :] for e in range(E)], axis=0
        )
        for h in range(HB)
    ]
    notes = got_ref[pl.ds(E * HB, devices, stride=step), :]
    wide = lambda at: jnp.broadcast_to(notes[:, at : at + 1], (devices, BLK))
    names = jnp.concatenate([wide(e) for e in range(E)], axis=0)
    weight = jnp.concatenate([wide(E + e) for e in range(E)], axis=0)
    every = jnp.concatenate([ids, names], axis=0)
    across = jnp.transpose(names)[0:1, :]
    count = E * devices
    same = (jnp.broadcast_to(every[:, :1], (every.shape[0], count)) == across).astype(F32)
    totals = jnp.dot(
        same,
        jnp.concatenate(sums + [weight], axis=1),
        precision=HIGHEST,
        preferred_element_type=F32,
    )
    mass = totals[:, HB * BLK :]
    positive = mass > 0
    safe = jnp.where(positive, mass, 1.0)
    means = [
        jnp.where(positive, totals[:, h * BLK : (h + 1) * BLK] / safe, 0.0) for h in range(HB)
    ]
    own_safe = jnp.where(weight > 0, weight, 1.0)
    gap = total(notes[:, 2 * E : 2 * E + 1])
    drift = total(notes[:, 2 * E + 1 : 2 * E + 2])
    rows = ids.shape[0]
    spread = jnp.zeros((count, BLK), F32)
    for h in range(HB):
        spread = spread + weight * (sums[h] / own_safe - means[h][rows:]) ** 2
    gap = gap + total(spread)
    return positive[:rows], [m[:rows] for m in means], [m[rows:] for m in means], names, weight, gap, drift


def moved(weight, means, before):
    change = jnp.zeros_like(weight)
    for mean, old in zip(means, before):
        change = change + weight * (mean - old) ** 2
    return total(change)


def second_kernel(
    S, J, R, NZ, HB, devices, lp_ref, pp_ref, pc_ref, hp_ref, hc_ref, cb_ref, ml_ref, mu_ref, id_ref, wb_ref, ts_ref, got_ref, pieces_ref, *rest
):
    other_refs = rest[: R - 1]
    p_out, h_out, mu_out, image_ref, send_ref, ml_out, pen_ref, ent_ref, all_sc, step_sc, send_sc = rest[R - 1 :]
    Q = J * S
    own = lax.axis_index("rows")
    slot = lambda ref, k: ref[k * Q : (k + 1) * Q, :]
    ids = id_ref[...]
    shared, means, entry_means, names, weight, gap, drift = read_nodes(J, HB, got_ref, ids, devices)
    nodes = ts_ref.shape[1]
    where = lax.broadcasted_iota(jnp.int32, (names.shape[0], nodes), 1).astype(F32)
    pick = (jnp.broadcast_to(names[:, :1], where.shape) == where).astype(F32).astype(BF16)
    old = None
    for part in range(3):
        y = jnp.dot(pick, ts_ref[part], preferred_element_type=F32)
        old = y if old is None else old + y
    drift = drift + moved(weight, entry_means, [old[:, h * BLK : (h + 1) * BLK] for h in range(HB)])
    penalty = RHO_START * jnp.sqrt(gap / (drift + EPSILON))
    pen_ref[...] = jnp.broadcast_to(penalty, pen_ref.shape)
    anchors, hedge = [], []
    for h in range(HB):
        ent_ref[h] = entry_means[h]
        anchor = jnp.where(shared, means[h], slot(mu_ref, h))
        left = slot(hp_ref, h) - anchor
        mult = slot(ml_ref, h) + RHO_START * left
        ml_out[h * Q : (h + 1) * Q, :] = mult
        anchors.append(anchor)
        hedge.append(mult + penalty * left)
    placed, hedged = primal_step(
        S, J, R, NZ, HB, own, pieces_ref, other_refs, pp_ref, pc_ref, hp_ref, hc_ref, cb_ref, hedge, all_sc
    )
    finish_step(
        S, J, R, NZ, HB, own, lp_ref, pp_ref, placed, hedged, anchors, ids, wb_ref[...], p_out, h_out, mu_out, image_ref, send_ref, step_sc, send_sc
    )


def last_kernel(
    S, J, HB, devices, got_ref, id_ref, ent_ref, mu_ref, h_ref, ml_ref, pen_ref, dual_ref, rhs_ref, image_ref, image2_ref, dual_out, ml_out, pen_out
):
    Q = J * S
    image = image_ref[...] + image2_ref[...]
    dual_out[...] = jnp.maximum(dual_ref[...] + SIGMA_STEP * (image - rhs_ref[...]), 0.0)
    shared, means, entry_means, names, weight, gap, drift = read_nodes(
        J, HB, got_ref, id_ref[...], devices
    )
    drift = drift + moved(weight, entry_means, [ent_ref[h] for h in range(HB)])
    penalty = pen_ref[0:1, 0:1]
    pen_out[...] = penalty * jnp.sqrt(gap / (drift + EPSILON))
    for h in range(HB):
        anchor = jnp.where(shared, means[h], mu_ref[h * Q : (h + 1) * Q, :])
        mult = ml_ref[h * Q : (h + 1) * Q, :] + penalty * (h_ref[h * Q : (h + 1) * Q, :] - anchor)
        for j in range(J):
            ml_out[pl.ds(h * J + j, S, stride=HB * J), :] = mult[j * S : (j + 1) * S]


def bulk_kernel(S, J, R, NZ, HB, SB, cols_ref, primal_ref, cost_ref, p_ref, h_ref, out_ref):
    K, Q = R * NZ, J * S
    first = pl.program_id(0) * SB
    for i in range(SB):
        move = TAU_STEP * cost_ref[i].astype(F32)
        x = primal_ref[i].astype(F32)
        for _ in range(SWEEPS):
            x = jnp.maximum(x - move, 0.0)
        out_ref[i] = x
        s = first + i
        for j in range(J):
            for k in range(K):
                c = cols_ref[s, k // NZ, j, k % NZ]
                out_ref[i, pl.ds(c * J + j, 1), :] = p_ref[pl.ds(k * Q + j * S + s, 1), :]
            for h in range(HB):
                out_ref[i, pl.ds(h * J + j, 1), :] = h_ref[pl.ds(h * Q + j * S + s, 1), :]


def local(
    sizes,
    lp_blocks,
    block_columns,
    scenario_nodes,
    scenario_weights,
    cost,
    bounds_rhs,
    primal_start,
    dual_start,
    multiplier_start,
    consensus_start,
):
    scens, R, sections = sizes
    S, J, columns = cost.shape
    NZ = lp_blocks.shape[3]
    hedged = multiplier_start.shape[2]
    HB, C = hedged // BLK, columns // BLK
    K, Q = R * NZ, J * S
    nodes = consensus_start.shape[0]
    devices = scens * sections
    padded = -(-nodes // 16) * 16
    message = -(-(2 * J * HB + 1) // 8) * 8
    static = (S, J, R, NZ, HB)

    def interleave(x):
        return x.reshape(S, J, -1, BLK).transpose(0, 2, 1, 3).reshape(S, -1, BLK)

    def uninterleave(x):
        return x.reshape(S, -1, J, BLK).transpose(0, 2, 1, 3).reshape(S, J, -1)

    lp = lp_blocks.reshape(S, J * NZ, BLK, BLK)
    primal, price = interleave(primal_start), interleave(cost)
    mult = interleave(multiplier_start).reshape(S * HB * J, BLK)

    def from_rows(x):
        return [
            lax.ppermute(x, "rows", [((i + q) % R, i) for i in range(R)]) for q in range(1, R)
        ]

    def from_section(x):
        return lax.ppermute(x, "section", [(i, (i + 1) % sections) for i in range(sections)])

    def exchange(x):
        return lax.all_to_all(x, ("scen", "section"), 0, 0).reshape(-1, BLK)

    pieces = pl.pallas_call(
        functools.partial(pieces_kernel, S, J, NZ),
        out_shape=shape(NZ * Q, BLK),
        in_specs=[VMEM] * 2,
        out_specs=VMEM,
        compiler_params=params(16),
        name="pieces",
    )(lp, dual_start)
    others = from_rows(pieces)

    pp, pc, hp, hc, cb, ml, an, ids, wb, ts = pl.pallas_call(
        functools.partial(setup_kernel, *static),
        out_shape=[shape(K * Q, BLK)] * 2
        + [shape(HB * Q, BLK)] * 2
        + [shape(K * Q, BLK)]
        + [shape(HB * Q, BLK)] * 2
        + [shape(Q, BLK)] * 2
        + [shape(3, padded, hedged, dtype=BF16)],
        in_specs=[SMEM] * 3 + [VMEM] * 4,
        out_specs=[VMEM] * 10,
        scratch_shapes=[pltpu.VMEM((S * K * J, BLK), jnp.int32)]
        + [pltpu.VMEM((S * K * J, BLK), F32)] * 2
        + [pltpu.VMEM((S * HB * J, BLK), F32)] * 2,
        compiler_params=params(24),
        name="setup",
    )(block_columns, scenario_nodes, scenario_weights, primal, price, mult, consensus_start)

    step_out = [
        shape(K * Q, BLK),
        shape(HB * Q, BLK),
        shape(HB * Q, BLK),
        shape(S, BLK),
        shape(devices, message, BLK),
    ]
    step_scratch = [
        pltpu.VMEM((K * Q, BLK), F32),
        pltpu.VMEM((K * Q, BLK), F32),
        pltpu.VMEM((message, BLK), F32),
    ]
    p1, h1, mu1, image1, send1 = pl.pallas_call(
        functools.partial(first_kernel, *static),
        out_shape=step_out,
        in_specs=[VMEM] * (11 + R - 1),
        out_specs=[VMEM] * 5,
        scratch_shapes=step_scratch,
        compiler_params=params(16),
        name="first",
    )(lp, pp, pc, hp, hc, cb, ml, an, ids, wb, pieces, *others)
    got1 = exchange(send1)
    image1b = from_section(image1)

    dual1, pieces2 = pl.pallas_call(
        functools.partial(dual_kernel, S, J, NZ),
        out_shape=[shape(S, BLK), shape(NZ * Q, BLK)],
        in_specs=[VMEM] * 5,
        out_specs=[VMEM] * 2,
        compiler_params=params(16),
        name="dual",
    )(lp, dual_start, bounds_rhs, image1, image1b)
    others2 = from_rows(pieces2)

    p2, h2, mu2, image2, send2, ml1, pen1, ent1 = pl.pallas_call(
        functools.partial(second_kernel, *static, devices),
        out_shape=step_out
        + [shape(HB * Q, BLK), shape(8, BLK), shape(HB, 2 * J * devices, BLK)],
        in_specs=[VMEM] * (13 + R - 1),
        out_specs=[VMEM] * 8,
        scratch_shapes=step_scratch,
        compiler_params=params(20),
        name="second",
    )(lp, p1, pc, h1, hc, cb, ml, mu1, ids, wb, ts, got1, pieces2, *others2)
    got2 = exchange(send2)
    image2b = from_section(image2)

    SB = 4 if S % 4 == 0 else 1
    block = lambda rows: pl.BlockSpec((SB, rows, BLK), lambda i: (i, 0, 0))
    out = pl.pallas_call(
        functools.partial(bulk_kernel, *static, SB),
        out_shape=shape(S, C * J, BLK),
        grid=(S // SB,),
        in_specs=[SMEM, block(C * J), block(C * J), VMEM, VMEM],
        out_specs=block(C * J),
        compiler_params=params(16),
        name="bulk",
    )(block_columns, primal, price, p2, h2)

    dual2, ml2, pen2 = pl.pallas_call(
        functools.partial(last_kernel, S, J, HB, devices),
        out_shape=[shape(S, BLK), shape(S * HB * J, BLK), shape(1, 1)],
        in_specs=[VMEM] * 11,
        out_specs=[VMEM] * 3,
        compiler_params=params(16),
        name="last",
    )(got2, ids, ent1, mu2, h2, ml1, pen1, dual1, bounds_rhs, image2, image2b)

    return (
        uninterleave(out),
        dual2,
        uninterleave(ml2.reshape(S, HB * J, BLK)),
        pen2.reshape(()),
    )


def solution(mesh):
    sizes = tuple(mesh.shape[a] for a in ("scen", "rows", "section"))
    in_specs = (
        P("scen", "rows", "section", None, None, None),
        P("scen", None, "section", None),
        P(None, "scen"),
        P("scen"),
        P("scen", "section", None),
        P("scen", "rows"),
        P("scen", "section", None),
        P("scen", "rows"),
        P("scen", "section", None),
        P(),
    )
    out_specs = (P("scen", "section", None), P("scen", "rows"), P("scen", "section", None), P())
    return jax.shard_map(
        functools.partial(local, sizes),
        mesh=mesh,
        in_specs=in_specs,
        out_specs=out_specs,
        check_vma=False,
    )
```

time: 298 us -> 68.7 us (0.23)
  blocking collectives: 103 us -> 0 us
  waiting for transfers between devices: 97.9 us -> 5.28 us
  matrix products: 23.3 us -> 0 us
  other arithmetic: 21.6 us -> 0 us
  between operations: 18.1 us -> 0.85 us
  Pallas kernels: 0 us -> 16 us
  starting transfers between devices: 0.08 us -> 14.7 us
    psum x2 -> x0, waiting for transfers between devices: 97.8 us -> none  [local(): lax.psum((jnp.einsum('jns,sjc->nc', membership, weighted, precision=lax.P...]
    psum x5 -> x0, blocking collectives: 92.4 us -> none  [the longest x2 63.7 us: local(): lax.psum((gap_local, drift_local), ('scen', 'section'))]
    dot_general x12 -> x0, matrix products: 19.2 us -> none  [the longest x2 7.67 us: local(): jnp.einsum('srjnc,srjnb->sjcb', selector, gathered, precision=lax.Precisi...]
    convert_element_type x5 -> x0, other arithmetic: 16.4 us -> none  [the longest x2 11.1 us: local(): step_half = (2.0 * primal_next - primal).astype(jnp.bfloat16)]
    pallas_call x0 -> x7, Pallas kernels: none -> 16 us  [the longest x1 4.73 us: local(): pl.pallas_call(functools.partial(bulk_kernel, *static, SB), out_shape=sha...]
    unnamed x35 -> x97, local copies, waits for them, and re-layouts: 17.8 us -> 30.9 us
    reshape x2 -> x0, local copies, waits for them, and re-layouts: 10.8 us -> none  [local(): adjoint = placed.reshape(scenario_count, local_sections, columns)]
    all_gather x2 -> x0, blocking collectives: 10.8 us -> none  [local(): gathered = lax.all_gather(pieces, 'rows', axis=1, tiled=True)]
  transfers between devices with their start and end apart: 2 -> 6, of which waited for: 2 -> 3; matrix products, arithmetic and copies ran while one was open for 10% -> 0% of each run, Pallas kernels for 0% -> 13%
where the time goes in v1:
time: 68.7 us; the launch traced here: 67.7 us
  local copies, waits for them, and re-layouts  30.9 us (45%)
  Pallas kernels  16 us (23%)
  starting transfers between devices  14.7 us (21%)
  waiting for transfers between devices  5.28 us (8%)
  between operations  0.85 us (1%)
    unnamed x97, local copies, waits for them, and re-layouts  30.9 us
    all_to_all x2, starting transfers between devices, exchange(): return lax.all_to_all(x, ('scen', 'section'), 0, 0).reshape(-1, BLK)  10.4 us
    pallas_call x1, Pallas kernels, local(): pl.pallas_call(functools.partial(bulk_kernel, *static, SB), out_shape=sha...  4.73 us
    ppermute x2, starting transfers between devices, from_rows(): lax.ppermute(x, 'rows', [((i + q) % R, i) for i in range(R)])  3.51 us
    pallas_call x1, Pallas kernels, local(): pl.pallas_call(functools.partial(second_kernel, *static, devices), out_sh...  3.22 us
    ppermute x2, waiting for transfers between devices, from_rows(): lax.ppermute(x, 'rows', [((i + q) % R, i) for i in range(R)])  2.94 us
    pallas_call x1, Pallas kernels, local(): pl.pallas_call(functools.partial(setup_kernel, *static), out_shape=[shape...  2.85 us
    pallas_call x1, Pallas kernels, local(): pl.pallas_call(functools.partial(first_kernel, *static), out_shape=step_o...  2.02 us
  transfers between devices with their start and end apart: 6, of which 3 were waited for; matrix products, arithmetic and copies ran while one was open for 0% of the time, Pallas kernels for 13%

profile of v1, /device:TPU:0, one launch (start us, length us, event | category | flops | bytes accessed | tf_op | source)
XLA Modules:
  0.0 67.7 jit_solution(12585334038496566851)
XLA Ops:
  0.7 1.9 %copy-done = bf16[24,1,2,2,128,128]{5,4,3,2,1,0:T(8,128)(2,1)S(1)} copy-done((bf16[24,1,2,2,128,128]{5,4,3,2,1,0:T(8,128)(2,1)S(1)}, bf16[24,1,2,2,128,128]{5,4,3,2,1,0:T(8,128)(2,1)}, u32[]{:S(2)}) %copy-start) | copy-done | bytes 3145752
  2.5 0.7 %copy-done.38 = f32[24,128]{1,0:T(8,128)S(1)} copy-done((f32[24,128]{1,0:T(8,128)S(1)}, f32[24,128]{1,0:T(8,128)}, u32[]{:S(2)}) %copy-start.38) | copy-done | bytes 12312
  3.3 0.9 %pieces.1.pieces_ref = f32[96,128]{1,0:T(8,128)S(1)} custom-call(bf16[24,4,128,128]{3,2,1,0:T(8,128)(2,1)S(1)} %bitcast.29, f32[24,128]{1,0:T(8,128)S(1)} %copy-done.38), custom_call_target="tpu_custom_call" | custom-call | tf_op jit(solution)/shard_map/pieces/pallas_call | solution.py:436
  4.2 3.0 %collective-permute-start = (f32[96,128]{1,0:T(8,128)S(1)}, f32[96,128]{1,0:T(8,128)S(1)}, u32[]{:S(2)}, u32[]{:S(2)}) collective-permute-start(f32[96,128]{1,0:T(8,128)S(1)} %pieces.1.pieces_ref), channel_id=1, source_target_pairs={{2,0},{0,2},{3,1},{1,3},{6,4},{4,6},{7,5},{5,7},{10,8},{8,10},{11,... | collective-permute-start | bytes 147464 | tf_op jit(solution)/shard_map/ppermute | solution.py:427
  7.3 1.6 %copy-done.2 = bf16[24,2,22528]{2,1,0:T(2,128)(2,1)S(1)} copy-done((bf16[24,2,22528]{2,1,0:T(2,128)(2,1)S(1)}, bf16[24,2,22528]{2,1,0:T(2,128)(2,1)}, u32[]{:S(2)}) %copy-start.2) | copy-done | bytes 2162712
  8.9 1.6 %copy-done.4 = bf16[24,2,22528]{2,1,0:T(2,128)(2,1)S(1)} copy-done((bf16[24,2,22528]{2,1,0:T(2,128)(2,1)S(1)}, bf16[24,2,22528]{2,1,0:T(2,128)(2,1)}, u32[]{:S(2)}) %copy-start.4) | copy-done | bytes 2162712
  10.5 1.3 %copy-done.8 = f32[585,512]{1,0:T(8,128)S(1)} copy-done((f32[585,512]{1,0:T(8,128)S(1)}, f32[585,512]{1,0:T(8,128)}, u32[]{:S(2)}) %copy-start.8) | copy-done | bytes 1198104
  11.8 2.9 %setup.1 = (f32[192,128]{1,0:T(8,128)S(1)}, f32[192,128]{1,0:T(8,128)S(1)}, f32[192,128]{1,0:T(8,128)S(1)}, f32[192,128]{1,0:T(8,128)S(1)}, f32[192,128]{1,0:T(8...) custom-call(s32[24,2,2,2]{3,2,1,0:T(2,128)S(1)} %copy.18.cols_ref, ...), custom_call_target="tpu_custom_call" | custom-call | tf_op jit(solution)/shard_map/setup/pallas_call | solution.py:446
  14.7 1.2 %copy-done.6 = bf16[3,592,512]{2,1,0:T(8,128)(2,1)} copy-done((bf16[3,592,512]{2,1,0:T(8,128)(2,1)}, bf16[3,592,512]{2,1,0:T(8,128)(2,1)S(1)}, u32[]{:S(2)}) %copy-start.6) | copy-done | bytes 1818648
  15.9 2.0 %first.1 = (f32[192,128]{1,0:T(8,128)S(1)}, f32[192,128]{1,0:T(8,128)S(1)}, f32[192,128]{1,0:T(8,128)S(1)}, f32[24,128]{1,0:T(8,128)S(1)}, f32[16,24,128]{2,1,0:T(8,128)S(1)}) custom-call(bf16[24,4,128,128]{3,2,1,0:T(8,128)(2,1)S(1)} %bitcast.30, f32[192,128]{1,0:T(8,128)S(1)} %get-tuple-element.32.pp_ref, f32[192,128]{1,0:T(8,128)S(1)} %get-tuple-element.33.pc_ref, ...), custom_call_target="tpu_custom_call" | custom-call | tf_op jit(solution)/shard_map/first/pallas_call | solution.py:475
  21.2 5.9 %all-to-all-start = ((f32[16,24,128]{2,1,0:T(8,128)}), f32[16,24,128]{2,1,0:T(8,128)S(1)}, u32[]{:S(2)}, u32[]{:S(2)}) async-start(f32[16,24,128]{2,1,0:T(8,128)} %copy-done.18), calls=%async_computation | async-start | bytes 393216 | tf_op jit(solution)/shard_map/all_to_all | solution.py:434
  27.6 0.8 %collective-permute-done.1.image2_ref = f32[24,128]{1,0:T(8,128)S(1)} collective-permute-done((f32[24,128]{1,0:T(8,128)S(1)}, f32[24,128]{1,0:T(8,128)S(1)}, u32[]{:S(2)}, u32[]{:S(2)}) %collective-permute-start.1) | collective-permute-done | bytes 12320 | tf_op jit(solution)/shard_map/ppermute | solution.py:431
  28.4 0.9 %dual.1 = (f32[24,128]{1,0:T(8,128)S(1)}, f32[96,128]{1,0:T(8,128)S(1)}) custom-call(bf16[24,4,128,128]{3,2,1,0:T(8,128)(2,1)S(1)} %bitcast.31, f32[24,128]{1,0:T(8,128)S(1)} %copy-done.39, f32[24,128]{1,0:T(8,128)S(1)} %copy-done.40, f32[24,128]{1,0:T(8,128)S(1)} %get-tuple-element.46.image_ref, f32[24,128]{1,0:T(8,128)S(1)} %collective-permute-done.1.image2_ref), custom_call_target="tpu_custom_call" | custom-call | tf_op jit(solution)/shard_map/dual/pallas_call | solution.py:487
  31.1 2.9 %collective-permute-done.2.rest_0_ = f32[96,128]{1,0:T(8,128)S(1)} collective-permute-done((f32[96,128]{1,0:T(8,128)S(1)}, f32[96,128]{1,0:T(8,128)S(1)}, u32[]{:S(2)}, u32[]{:S(2)}) %collective-permute-start.2) | collective-permute-done | bytes 49184 | tf_op jit(solution)/shard_map/ppermute | solution.py:427
  34.7 1.5 %all-to-all-done = f32[16,24,128]{2,1,0:T(8,128)S(1)} async-done(((f32[16,24,128]{2,1,0:T(8,128)}), f32[16,24,128]{2,1,0:T(8,128)S(1)}, u32[]{:S(2)}, u32[]{:S(2)}) %all-to-all-start) | async-done | bytes 196640 | tf_op jit(solution)/shard_map/all_to_all | solution.py:434
  36.2 1.5 %copy-done.7 = bf16[3,592,512]{2,1,0:T(8,128)(2,1)S(1)} copy-done((bf16[3,592,512]{2,1,0:T(8,128)(2,1)S(1)}, bf16[3,592,512]{2,1,0:T(8,128)(2,1)}, u32[]{:S(2)}) %copy-start.7) | copy-done | bytes 1818648
  37.7 0.9 %copy-done.10 = f32[192,128]{1,0:T(8,128)S(1)} copy-done((f32[192,128]{1,0:T(8,128)S(1)}, f32[192,128]{1,0:T(8,128)}, u32[]{:S(2)}) %copy-start.10) | copy-done | bytes 98328
  38.6 0.9 %copy-done.12 = f32[192,128]{1,0:T(8,128)S(1)} copy-done((f32[192,128]{1,0:T(8,128)S(1)}, f32[192,128]{1,0:T(8,128)}, u32[]{:S(2)}) %copy-start.12) | copy-done | bytes 98328
  39.5 0.9 %copy-done.14 = f32[192,128]{1,0:T(8,128)S(1)} copy-done((f32[192,128]{1,0:T(8,128)S(1)}, f32[192,128]{1,0:T(8,128)}, u32[]{:S(2)}) %copy-start.14) | copy-done | bytes 98328
  40.4 0.9 %copy-done.16 = f32[192,128]{1,0:T(8,128)S(1)} copy-done((f32[192,128]{1,0:T(8,128)S(1)}, f32[192,128]{1,0:T(8,128)}, u32[]{:S(2)}) %copy-start.16) | copy-done | bytes 98328
  41.2 0.9 %copy-done.29 = f32[192,128]{1,0:T(8,128)S(1)} copy-done((f32[192,128]{1,0:T(8,128)S(1)}, f32[192,128]{1,0:T(8,128)}, u32[]{:S(2)}) %copy-start.29) | copy-done | bytes 98328
  42.1 0.9 %copy-done.31 = f32[192,128]{1,0:T(8,128)S(1)} copy-done((f32[192,128]{1,0:T(8,128)S(1)}, f32[192,128]{1,0:T(8,128)}, u32[]{:S(2)}) %copy-start.31) | copy-done | bytes 98328
  43.0 0.9 %copy-done.33 = f32[192,128]{1,0:T(8,128)S(1)} copy-done((f32[192,128]{1,0:T(8,128)S(1)}, f32[192,128]{1,0:T(8,128)}, u32[]{:S(2)}) %copy-start.33) | copy-done | bytes 98328
  43.9 0.8 %copy-done.35 = f32[96,128]{1,0:T(8,128)S(1)} copy-done((f32[96,128]{1,0:T(8,128)S(1)}, f32[96,128]{1,0:T(8,128)}, u32[]{:S(2)}) %copy-start.35) | copy-done | bytes 49176
  44.7 0.8 %copy-done.37 = f32[96,128]{1,0:T(8,128)S(1)} copy-done((f32[96,128]{1,0:T(8,128)S(1)}, f32[96,128]{1,0:T(8,128)}, u32[]{:S(2)}) %copy-start.37) | copy-done | bytes 49176
  45.5 3.2 %second.1 = (f32[192,128]{1,0:T(8,128)S(1)}, f32[192,128]{1,0:T(8,128)S(1)}, f32[192,128]{1,0:T(8,128)S(1)}, f32[24,128]{1,0:T(8,128)S(1)}, f32[16,24,128]{2,1,0...) custom-call(bf16[24,4,128,128]{3,2,1,0:T(8,128)(2,1)S(1)} %bitcast.32, ...), custom_call_target="tpu_custom_call" | custom-call | tf_op jit(solution)/shard_map/second/pallas_call | solution.py:497
  52.6 4.4 %all-to-all-start.1 = ((f32[16,24,128]{2,1,0:T(8,128)}), f32[16,24,128]{2,1,0:T(8,128)S(1)}, u32[]{:S(2)}, u32[]{:S(2)}) async-start(f32[16,24,128]{2,1,0:T(8,128)} %copy-done.17), calls=%async_computation.1 | async-start | bytes 393216 | tf_op jit(solution)/shard_map/all_to_all | solution.py:434
  57.5 1.6 %copy-done.3 = bf16[24,2,22528]{2,1,0:T(2,128)(2,1)S(1)} copy-done((bf16[24,2,22528]{2,1,0:T(2,128)(2,1)S(1)}, bf16[24,2,22528]{2,1,0:T(2,128)(2,1)}, u32[]{:S(2)}) %copy-start.3) | copy-done | bytes 2162712
  59.1 1.6 %copy-done.5 = bf16[24,2,22528]{2,1,0:T(2,128)(2,1)S(1)} copy-done((bf16[24,2,22528]{2,1,0:T(2,128)(2,1)S(1)}, bf16[24,2,22528]{2,1,0:T(2,128)(2,1)}, u32[]{:S(2)}) %copy-start.5) | copy-done | bytes 2162712
  60.7 0.9 %copy-done.22 = f32[192,128]{1,0:T(8,128)S(1)} copy-done((f32[192,128]{1,0:T(8,128)S(1)}, f32[192,128]{1,0:T(8,128)}, u32[]{:S(2)}) %copy-start.22) | copy-done | bytes 98328
  61.6 4.7 %bulk.1 = f32[24,352,128]{2,1,0:T(8,128)} custom-call(s32[24,2,2,2]{3,2,1,0:T(2,128)S(1)} %copy.18.cols_ref, bf16[24,352,128]{2,1,0:T(8,128)(2,1)S(1)} %bitcast.34, bf16[24,352,128]{2,1,0:T(8,128)(2,1)S(1)} %bitcast.36, f32[192,128]{1,0:T(8,128)S(1)} %copy-done.22, f32[192,128]{1,0:T(8,128)S(1)} %get-tuple-element.49.h_ref), custom_call_target="tpu_custom_call" | custom-call | tf_op jit(solution)/shard_map/bulk/pallas_call | solution.py:512
  66.4 1.3 %last.1 = (f32[24,128]{1,0:T(8,128)}, f32[192,128]{1,0:T(8,128)}, f32[1,1]{1,0:T(1,128)}) custom-call(f32[384,128]{1,0:T(8,128)S(1)} %bitcast.38, f32[48,128]{1,0:T(8,128)S(1)} %get-tuple-element.39.id_ref, f32[4,64,128]{2,1,0:T(8,128)S(1)} %copy-done.20, f32[192,128]{1,0:T(8,128)S(1)} %copy-done.24, f32[192,128]{1,0:T(8,128)S(1)} %get-tuple-element.49.h_ref, ...), custom_call_target="tpu_custom_call" | custom-call | tf_op jit(solution)/shard_map/last/pallas_call | solution.py:522
  (84 shorter events, 10.5 us)
Async XLA Ops:
  0.6 6.6 %copy-start.46 = (f32[24]{0:T(128)S(1)}, f32[24]{0:T(128)}, u32[]{:S(2)}) copy-start(f32[24]{0:T(128)} %weights_ref.1) | copy-start | bytes 292
  0.6 1.9 %copy-start = (bf16[24,1,2,2,128,128]{5,4,3,2,1,0:T(8,128)(2,1)S(1)}, bf16[24,1,2,2,128,128]{5,4,3,2,1,0:T(8,128)(2,1)}, u32[]{:S(2)}) copy-start(bf16[24,1,2,2,128,128]{5,4,3,2,1,0:T(8,128)(2,1)} %param.10) | copy-start | bytes 9437188
  3.2 3.9 %copy-start.47 = (s32[24,2,2,2]{0,3,2,1:T(2,128)S(1)}, s32[24,2,2,2]{0,3,2,1:T(2,128)}, u32[]{:S(2)}) copy-start(s32[24,2,2,2]{0,3,2,1:T(2,128)} %param.11) | copy-start | bytes 2308
  3.2 4.0 %copy-start.27 = (f32[24,2,512]{2,1,0:T(2,128)S(1)}, f32[24,2,512]{2,1,0:T(2,128)}, u32[]{:S(2)}) copy-start(f32[24,2,512]{2,1,0:T(2,128)} %param.18) | copy-start | bytes 294916
  3.2 4.0 %copy-start.45 = (s32[3,24]{1,0:T(4,128)S(1)}, s32[3,24]{1,0:T(4,128)}, u32[]{:S(2)}) copy-start(s32[3,24]{1,0:T(4,128)} %nodes_ref.1) | copy-start | bytes 868
  4.2 11.7 %collective-permute-start = (f32[96,128]{1,0:T(8,128)S(1)}, f32[96,128]{1,0:T(8,128)S(1)}, u32[]{:S(2)}, u32[]{:S(2)}) collective-permute-start(f32[96,128]{1,0:T(8,128)S(1)} %pieces.1.pieces_ref), channel_id=1, source_target_pairs={{2,0},{0,2},{3,1},{1,3},{6,4},{4,6},{7,5},{5,7},{10,8},{8,10},{11,... | collective-permute-start | bytes 147464 | tf_op jit(solution)/shard_map/ppermute | solution.py:427
  7.3 1.6 %copy-start.2 = (bf16[24,2,22528]{2,1,0:T(2,128)(2,1)S(1)}, bf16[24,2,22528]{2,1,0:T(2,128)(2,1)}, u32[]{:S(2)}) copy-start(bf16[24,2,22528]{2,1,0:T(2,128)(2,1)} %param.16) | copy-start | bytes 6488068
  8.9 1.6 %copy-start.4 = (bf16[24,2,22528]{2,1,0:T(2,128)(2,1)S(1)}, bf16[24,2,22528]{2,1,0:T(2,128)(2,1)}, u32[]{:S(2)}) copy-start(bf16[24,2,22528]{2,1,0:T(2,128)(2,1)} %param.14) | copy-start | bytes 6488068
  10.5 1.3 %copy-start.8 = (f32[585,512]{1,0:T(8,128)S(1)}, f32[585,512]{1,0:T(8,128)}, u32[]{:S(2)}) copy-start(f32[585,512]{1,0:T(8,128)} %table_ref.1) | copy-start | bytes 3594244
  11.8 4.1 %copy-start.1 = (bf16[24,1,2,2,128,128]{5,4,3,2,1,0:T(8,128)(2,1)S(1)}, bf16[24,1,2,2,128,128]{5,4,3,2,1,0:T(8,128)(2,1)}, u32[]{:S(2)}) copy-start(bf16[24,1,2,2,128,128]{5,4,3,2,1,0:T(8,128)(2,1)} %param.10) | copy-start | bytes 9437188
  14.7 1.2 %copy-start.6 = (bf16[3,592,512]{2,1,0:T(8,128)(2,1)}, bf16[3,592,512]{2,1,0:T(8,128)(2,1)S(1)}, u32[]{:S(2)}) copy-start(bf16[3,592,512]{2,1,0:T(8,128)(2,1)S(1)} %get-tuple-element.44.ts_ref) | copy-start | bytes 5455876
  15.9 2.1 %copy-start.11 = (f32[192,128]{1,0:T(8,128)}, f32[192,128]{1,0:T(8,128)S(1)}, u32[]{:S(2)}) copy-start(f32[192,128]{1,0:T(8,128)S(1)} %get-tuple-element.35.hc_ref) | copy-start | bytes 294916
  15.9 2.1 %copy-start.13 = (f32[192,128]{1,0:T(8,128)}, f32[192,128]{1,0:T(8,128)S(1)}, u32[]{:S(2)}) copy-start(f32[192,128]{1,0:T(8,128)S(1)} %get-tuple-element.36.cb_ref) | copy-start | bytes 294916
  15.9 2.1 %copy-start.15 = (f32[192,128]{1,0:T(8,128)}, f32[192,128]{1,0:T(8,128)S(1)}, u32[]{:S(2)}) copy-start(f32[192,128]{1,0:T(8,128)S(1)} %get-tuple-element.37.ml_ref) | copy-start | bytes 294916
  15.9 12.5 %copy-start.39 = (f32[24,128]{1,0:T(8,128)S(1)}, f32[24,128]{1,0:T(8,128)}, u32[]{:S(2)}) copy-start(f32[24,128]{1,0:T(8,128)} %dual_ref.3) | copy-start | bytes 36868
  15.9 12.5 %copy-start.40 = (f32[24,128]{1,0:T(8,128)S(1)}, f32[24,128]{1,0:T(8,128)}, u32[]{:S(2)}) copy-start(f32[24,128]{1,0:T(8,128)} %rhs_ref.3) | copy-start | bytes 36868
  21.2 14.9 %all-to-all-start = ((f32[16,24,128]{2,1,0:T(8,128)}), f32[16,24,128]{2,1,0:T(8,128)S(1)}, u32[]{:S(2)}, u32[]{:S(2)}) async-start(f32[16,24,128]{2,1,0:T(8,128)} %copy-done.18), calls=%async_computation | async-start | bytes 393216 | tf_op jit(solution)/shard_map/all_to_all | solution.py:434
  27.2 1.2 %collective-permute-start.1 = (f32[24,128]{1,0:T(8,128)S(1)}, f32[24,128]{1,0:T(8,128)S(1)}, u32[]{:S(2)}, u32[]{:S(2)}) collective-permute-start(f32[24,128]{1,0:T(8,128)S(1)} %get-tuple-element.46.image_ref), channel_id=1, source_target_pairs={{0,1},{1,0},{2,3},{3,2},{4,5},{5,4},{6,7},{7,6},{8,9},{9,8},{10,11... | collective-permute-start | bytes 36872 | tf_op jit(solution)/shard_map/ppermute | solution.py:431
  30.0 4.1 %collective-permute-start.2 = (f32[96,128]{1,0:T(8,128)S(1)}, f32[96,128]{1,0:T(8,128)S(1)}, u32[]{:S(2)}, u32[]{:S(2)}) collective-permute-start(f32[96,128]{1,0:T(8,128)S(1)} %get-tuple-element.47.pieces_ref), channel_id=1, source_target_pairs={{2,0},{0,2},{3,1},{1,3},{6,4},{4,6},{7,5},{5,7},{10,8},{8,10},{11,... | collective-permute-start | bytes 147464 | tf_op jit(solution)/shard_map/ppermute | solution.py:427
  36.2 1.5 %copy-start.7 = (bf16[3,592,512]{2,1,0:T(8,128)(2,1)S(1)}, bf16[3,592,512]{2,1,0:T(8,128)(2,1)}, u32[]{:S(2)}) copy-start(bf16[3,592,512]{2,1,0:T(8,128)(2,1)} %copy-done.6) | copy-start | bytes 5455876
  37.7 0.9 %copy-start.10 = (f32[192,128]{1,0:T(8,128)S(1)}, f32[192,128]{1,0:T(8,128)}, u32[]{:S(2)}) copy-start(f32[192,128]{1,0:T(8,128)} %copy-done.9) | copy-start | bytes 294916
  38.6 0.9 %copy-start.12 = (f32[192,128]{1,0:T(8,128)S(1)}, f32[192,128]{1,0:T(8,128)}, u32[]{:S(2)}) copy-start(f32[192,128]{1,0:T(8,128)} %copy-done.11) | copy-start | bytes 294916
  43.0 0.9 %copy-start.33 = (f32[192,128]{1,0:T(8,128)S(1)}, f32[192,128]{1,0:T(8,128)}, u32[]{:S(2)}) copy-start(f32[192,128]{1,0:T(8,128)} %copy-done.32) | copy-start | bytes 294916
  52.6 13.7 %all-to-all-start.1 = ((f32[16,24,128]{2,1,0:T(8,128)}), f32[16,24,128]{2,1,0:T(8,128)S(1)}, u32[]{:S(2)}, u32[]{:S(2)}) async-start(f32[16,24,128]{2,1,0:T(8,128)} %copy-done.17), calls=%async_computation.1 | async-start | bytes 393216 | tf_op jit(solution)/shard_map/all_to_all | solution.py:434
  57.1 9.3 %collective-permute-start.3 = (f32[24,128]{1,0:T(8,128)}, f32[24,128]{1,0:T(8,128)S(1)}, u32[]{:S(2)}, u32[]{:S(2)}) collective-permute-start(f32[24,128]{1,0:T(8,128)} %copy-done.43), channel_id=1, source_target_pairs={{0,1},{1,0},{2,3},{3,2},{4,5},{5,4},{6,7},{7,6},{8,9},{9,8},{10,11... | collective-permute-start | bytes 36872 | tf_op jit(solution)/shard_map/ppermute | solution.py:431
  57.5 1.6 %copy-start.3 = (bf16[24,2,22528]{2,1,0:T(2,128)(2,1)S(1)}, bf16[24,2,22528]{2,1,0:T(2,128)(2,1)}, u32[]{:S(2)}) copy-start(bf16[24,2,22528]{2,1,0:T(2,128)(2,1)} %param.16) | copy-start | bytes 6488068
  59.1 1.6 %copy-start.5 = (bf16[24,2,22528]{2,1,0:T(2,128)(2,1)S(1)}, bf16[24,2,22528]{2,1,0:T(2,128)(2,1)}, u32[]{:S(2)}) copy-start(bf16[24,2,22528]{2,1,0:T(2,128)(2,1)} %param.14) | copy-start | bytes 6488068
  61.6 4.8 %copy-start.20 = (f32[4,64,128]{2,1,0:T(8,128)S(1)}, f32[4,64,128]{2,1,0:T(8,128)}, u32[]{:S(2)}) copy-start(f32[4,64,128]{2,1,0:T(8,128)} %copy-done.19) | copy-start | bytes 393220
  61.6 4.8 %copy-start.24 = (f32[192,128]{1,0:T(8,128)S(1)}, f32[192,128]{1,0:T(8,128)}, u32[]{:S(2)}) copy-start(f32[192,128]{1,0:T(8,128)} %copy-done.23) | copy-start | bytes 294916
  61.6 4.8 %copy-start.26 = (f32[192,128]{1,0:T(8,128)S(1)}, f32[192,128]{1,0:T(8,128)}, u32[]{:S(2)}) copy-start(f32[192,128]{1,0:T(8,128)} %copy-done.25) | copy-start | bytes 294916
  61.6 4.8 %copy-start.42 = (f32[24,128]{1,0:T(8,128)S(1)}, f32[24,128]{1,0:T(8,128)}, u32[]{:S(2)}) copy-start(f32[24,128]{1,0:T(8,128)} %copy-done.41) | copy-start | bytes 36868
  61.6 4.8 %copy-start.44 = (f32[24,128]{1,0:T(8,128)S(1)}, f32[24,128]{1,0:T(8,128)}, u32[]{:S(2)}) copy-start(f32[24,128]{1,0:T(8,128)} %copy-done.43) | copy-start | bytes 36868
  (22 other events, 15.7 us)

commit v2 on v1

v2 whole, which is shorter than its diff:
```python
import functools

import jax
import jax.numpy as jnp
from jax import lax
from jax.experimental import pallas as pl
from jax.experimental.pallas import tpu as pltpu
from jax.sharding import PartitionSpec as P

BLK = 128
N1 = 8
N2 = 64
SWEEPS = 2
TAU_STEP = 0.4
SIGMA_STEP = 0.4
RHO_START = 1.0
EPSILON = 1e-06
F32 = jnp.float32
BF16 = jnp.bfloat16
HIGHEST = lax.Precision.HIGHEST

VMEM = pl.BlockSpec(memory_space=pltpu.VMEM)
SMEM = pl.BlockSpec(memory_space=pltpu.SMEM)
HBM = pl.BlockSpec(memory_space=pltpu.HBM)


def params(mib=16):
    return pltpu.CompilerParams(vmem_limit_bytes=mib << 20)


def in_vmem(x):
    return pltpu.with_memory_space_constraint(x, pltpu.VMEM)


def in_hbm(x):
    return pltpu.with_memory_space_constraint(x, pltpu.HBM)


def shape(*dims):
    return jax.ShapeDtypeStruct(dims, F32)


def near(*dims):
    return pltpu.VMEM(dims, F32)


def cut(src_ref, dst_ref, sems, parts):
    step = src_ref.shape[0] // parts
    at = [pl.ds(i * step, step) for i in range(parts)]
    return [
        pltpu.make_async_copy(src_ref.at[a], dst_ref.at[a], sems.at[i]) for i, a in enumerate(at)
    ]


def write_pieces(lp_ref, dual, out_ref, S, J, NZ, before=lambda s: None):
    for s in range(S):
        before(s)
        row = dual[s : s + 1, :].astype(BF16)
        for j in range(J):
            for n in range(NZ):
                y = jnp.dot(row, lp_ref[s, j * NZ + n], preferred_element_type=F32)
                out_ref[pl.ds((n * J + j) * S + s, 1), :] = y


def image_kernel(S, J, NZ, lp_ref, step_ref, image_ref):
    for s in range(S):
        total = None
        for j in range(J):
            for n in range(NZ):
                x = step_ref[pl.ds((n * J + j) * S + s, 1), :].astype(BF16)
                y = lax.dot_general(
                    x,
                    lp_ref[s, j * NZ + n],
                    (((1,), (1,)), ((), ())),
                    preferred_element_type=F32,
                )
                total = y if total is None else total + y
        image_ref[pl.ds(s, 1), :] = total


def pieces_kernel(
    S, J, NZ, lp_hbm, dual_hbm, primal_hbm, out_ref, lp_ref, primal_ref, sems, dual_ref, sem, primal_sem
):
    parts = sems.shape[0]
    dual_copy = pltpu.make_async_copy(dual_hbm, dual_ref, sem)
    dual_copy.start()
    copies = cut(lp_hbm, lp_ref, sems, parts)
    for copy in copies:
        copy.start()
    primal_copy = pltpu.make_async_copy(primal_hbm, primal_ref, primal_sem)
    primal_copy.start()
    dual_copy.wait()

    def before(s):
        if s % (S // parts) == 0:
            copies[s // (S // parts)].wait()

    write_pieces(lp_ref, dual_ref[...], out_ref, S, J, NZ, before)
    primal_copy.wait()


def dual_kernel(S, J, NZ, lp_ref, dual_ref, rhs_ref, image_ref, image2_ref, next_ref, out_ref):
    image = image_ref[...] + image2_ref[...]
    dual = jnp.maximum(dual_ref[...] + SIGMA_STEP * (image - rhs_ref[...]), 0.0)
    next_ref[...] = dual
    write_pieces(lp_ref, dual, out_ref, S, J, NZ)


def setup_kernel(
    S,
    J,
    R,
    NZ,
    HB,
    cols_ref,
    nodes_ref,
    weights_ref,
    primal_ref,
    cost_hbm,
    mult_ref,
    table_hbm,
    pp_ref,
    pc_ref,
    hp_ref,
    hc_ref,
    cb_ref,
    ml_ref,
    an_ref,
    id_ref,
    wb_ref,
    cost_ref,
    idx_sc,
    pp_sc,
    pc_sc,
    hp_sc,
    hc_sc,
    table_ref,
    cost_sem,
    table_sem,
):
    K, Q = R * NZ, J * S
    cost_copy = pltpu.make_async_copy(cost_hbm, cost_ref, cost_sem)
    cost_copy.start()
    table_copy = pltpu.make_async_copy(table_hbm, table_ref, table_sem)
    table_copy.start()
    section = lax.axis_index("section")
    rows = primal_ref.shape[1]
    for s in range(S):
        for j in range(J):
            for k in range(K):
                c = cols_ref[k // NZ, j, k % NZ, s]
                idx_sc[pl.ds((s * K + k) * J + j, 1), :] = jnp.full(
                    (1, BLK), c * J + j, jnp.int32
                )
    nodes_of = []
    for j in range(J):
        g = section * J + j
        level = jnp.maximum(g - 1, 0)
        off = jnp.where(g == 0, 0, jnp.where(g == 1, 1, jnp.where(g == 2, 1 + N1, 1 + N1 + N2)))
        keep = jnp.where(g == 0, 0, 1)
        for s in range(S):
            node = nodes_ref[level, s] * keep + off
            q = j * S + s
            id_ref[pl.ds(q, 1), :] = jnp.full((1, BLK), node, jnp.int32).astype(F32)
            wb_ref[pl.ds(q, 1), :] = jnp.full((1, BLK), weights_ref[s], F32)
            nodes_of.append(node)
    tiles = -(-rows // BLK)
    lane = lax.broadcasted_iota(jnp.int32, (K * J, BLK), 1)

    def gather(source_ref, placed_ref, hedged_ref):
        for s in range(S):
            want = idx_sc[pl.ds(s * K * J, K * J), :]
            pick = jnp.concatenate(
                [(want == lane + t * BLK).astype(F32).astype(BF16) for t in range(tiles)], axis=1
            )[:, :rows]
            placed_ref[pl.ds(s * K * J, K * J), :] = jnp.dot(
                pick, source_ref[s], preferred_element_type=F32
            )
            hedged_ref[pl.ds(s * HB * J, HB * J), :] = source_ref[s, : HB * J, :].astype(F32)

    gather(primal_ref, pp_sc, hp_sc)
    for j in range(J):
        for k in range(K):
            src, dst = pl.ds(k * J + j, S, stride=K * J), pl.ds(k * Q + j * S, S)
            pp_ref[dst, :] = pp_sc[src, :]
            cb_ref[dst, :] = (idx_sc[src, :] - j).astype(F32)
        for h in range(HB):
            src, dst = pl.ds(h * J + j, S, stride=HB * J), pl.ds(h * Q + j * S, S)
            hp_ref[dst, :] = hp_sc[src, :]
            ml_ref[dst, :] = mult_ref[src, :]
    cost_copy.wait()
    gather(cost_ref, pc_sc, hc_sc)
    for j in range(J):
        for k in range(K):
            src, dst = pl.ds(k * J + j, S, stride=K * J), pl.ds(k * Q + j * S, S)
            pc_ref[dst, :] = pc_sc[src, :]
        for h in range(HB):
            src, dst = pl.ds(h * J + j, S, stride=HB * J), pl.ds(h * Q + j * S, S)
            hc_ref[dst, :] = hc_sc[src, :]
    table_copy.wait()
    for q, node in enumerate(nodes_of):
        line = table_ref[pl.ds(node, 1), :]
        for h in range(HB):
            an_ref[pl.ds(h * Q + q, 1), :] = line[:, h * BLK : (h + 1) * BLK]


def total(x):
    return jnp.sum(x, axis=(0, 1), keepdims=True)


def primal_step(
    S, J, R, NZ, HB, own, pieces_ref, other_refs, p_ref, pc_ref, h_ref, hc_ref, cb_ref, hedge, all_sc
):
    K, Q = R * NZ, J * S
    for shift in range(R):
        src = pieces_ref if shift == 0 else other_refs[shift - 1]
        at = lax.rem(own + shift, R) * (NZ * Q)
        all_sc[pl.ds(pl.multiple_of(at, 8), NZ * Q), :] = src[...]
    slot = lambda ref, k: ref[k * Q : (k + 1) * Q, :]
    cols = [slot(cb_ref, k) for k in range(K)]
    parts = [slot(all_sc, k) for k in range(K)]
    placed, hedged = [], []
    for k in range(K):
        add = None
        for m in range(K):
            term = parts[m] if m == k else jnp.where(cols[m] == cols[k], parts[m], 0.0)
            add = term if add is None else add + term
        for h in range(HB):
            add = add + jnp.where(cols[k] == float(h * J), hedge[h], 0.0)
        placed.append(
            jnp.maximum(slot(p_ref, k) - TAU_STEP * (slot(pc_ref, k) + add), 0.0)
        )
    for h in range(HB):
        add = None
        for m in range(K):
            term = jnp.where(cols[m] == float(h * J), parts[m], 0.0)
            add = term if add is None else add + term
        add = add + hedge[h]
        hedged.append(jnp.maximum(slot(h_ref, h) - TAU_STEP * (slot(hc_ref, h) + add), 0.0))
    return placed, hedged


def finish_step(
    S, J, R, NZ, HB, own, p_ref, placed, hedged, anchors, with_anchors, ids, wb, p_out, h_out, mu_ref, send_ref, step_ref
):
    K, Q = R * NZ, J * S
    for k in range(K):
        p_out[k * Q : (k + 1) * Q, :] = placed[k]
    mine = pl.ds(pl.multiple_of(own * (NZ * Q), 8), NZ * Q)
    step_ref[...] = 2.0 * p_out[mine, :] - p_ref[mine, :]
    for h in range(HB):
        h_out[h * Q : (h + 1) * Q, :] = hedged[h]
    across = jnp.transpose(ids)[0:1, :Q]
    same = (jnp.broadcast_to(ids[:, :1], (Q, Q)) == across).astype(F32)
    sums = jnp.dot(
        same,
        jnp.concatenate([wb * x for x in hedged] + [wb], axis=1),
        precision=HIGHEST,
        preferred_element_type=F32,
    )
    mass = sums[:, HB * BLK :]
    inner = []
    for j in range(J):
        mine = ids[j * S : (j + 1) * S]
        inner.append((mine != mine[:1]) & (mine != mine[S - 1 :]))
    inner = jnp.concatenate([x.astype(F32) for x in inner], axis=0)
    gap, drift = jnp.zeros((Q, BLK), F32), jnp.zeros((Q, BLK), F32)
    for h in range(HB):
        mu = sums[:, h * BLK : (h + 1) * BLK] / mass
        mu_ref[h * Q : (h + 1) * Q, :] = mu
        gap = gap + wb * (hedged[h] - mu) ** 2
        drift = drift + (wb * inner) * (mu - anchors[h]) ** 2
    lane = lax.broadcasted_iota(jnp.int32, (1, BLK), 1)
    note = jnp.zeros((1, BLK), F32)
    for j in range(J):
        a, b = j * S, j * S + S - 1
        fresh = ids[b : b + 1] != ids[a : a + 1]
        for f in range(2):
            e = f * J + j
            at = b if f else a
            for h in range(HB):
                line = sums[at : at + 1, h * BLK : (h + 1) * BLK]
                send_ref[pl.ds(e * HB + h, 1), :] = jnp.where(fresh, line, 0.0) if f else line
            name, weight = ids[at : at + 1], mass[at : at + 1]
            if f:
                name, weight = jnp.where(fresh, name, -1.0), jnp.where(fresh, weight, 0.0)
            note = jnp.where(lane == e, name, note)
            note = jnp.where(lane == 2 * J + e, weight, note)
    note = jnp.where(lane == 4 * J, total(gap), note)
    note = jnp.where(lane == 4 * J + 1, total(drift), note)
    if with_anchors:
        for j in range(J):
            for f in range(2):
                at = j * S + (S - 1) * f
                for h in range(HB):
                    send_ref[pl.ds(2 * J * HB + 1 + (f * J + j) * HB + h, 1), :] = anchors[h][at : at + 1]
    at = 2 * J * HB * (2 if with_anchors else 1)
    send_ref[pl.ds(2 * J * HB, 1), :] = note
    send_ref[pl.ds(at + 1, send_ref.shape[0] - at - 1), :] = jnp.zeros(
        (send_ref.shape[0] - at - 1, BLK), F32
    )


def first_kernel(
    S, J, R, NZ, HB, pp_ref, pc_ref, hp_ref, hc_ref, cb_ref, ml_ref, an_ref, id_ref, wb_ref, pieces_ref, *rest
):
    other_refs = rest[: R - 1]
    p_out, h_out, mu_ref, send_ref, step_ref, all_sc = rest[R - 1 :]
    Q = J * S
    own = lax.axis_index("rows")
    slot = lambda ref, k: ref[k * Q : (k + 1) * Q, :]
    anchors = [slot(an_ref, h) for h in range(HB)]
    hedge = [
        slot(ml_ref, h) + RHO_START * (slot(hp_ref, h) - anchors[h]) for h in range(HB)
    ]
    placed, hedged = primal_step(
        S, J, R, NZ, HB, own, pieces_ref, other_refs, pp_ref, pc_ref, hp_ref, hc_ref, cb_ref, hedge, all_sc
    )
    finish_step(
        S, J, R, NZ, HB, own, pp_ref, placed, hedged, anchors, True, id_ref[...], wb_ref[...], p_out, h_out, mu_ref, send_ref, step_ref
    )


def read_nodes(J, HB, got_ref, ids, devices):
    step = got_ref.shape[0] // devices
    E = 2 * J
    sums = [
        jnp.concatenate(
            [got_ref[pl.ds(e * HB + h, devices, stride=step), :] for e in range(E)], axis=0
        )
        for h in range(HB)
    ]
    notes = got_ref[pl.ds(E * HB, devices, stride=step), :]
    wide = lambda at: jnp.broadcast_to(notes[:, at : at + 1], (devices, BLK))
    names = jnp.concatenate([wide(e) for e in range(E)], axis=0)
    weight = jnp.concatenate([wide(E + e) for e in range(E)], axis=0)
    every = jnp.concatenate([ids, names], axis=0)
    across = jnp.transpose(names)[0:1, :]
    count = E * devices
    same = (jnp.broadcast_to(every[:, :1], (every.shape[0], count)) == across).astype(F32)
    totals = jnp.dot(
        same,
        jnp.concatenate(sums + [weight], axis=1),
        precision=HIGHEST,
        preferred_element_type=F32,
    )
    mass = totals[:, HB * BLK :]
    positive = mass > 0
    safe = jnp.where(positive, mass, 1.0)
    means = [
        jnp.where(positive, totals[:, h * BLK : (h + 1) * BLK] / safe, 0.0) for h in range(HB)
    ]
    own_safe = jnp.where(weight > 0, weight, 1.0)
    gap = total(notes[:, 2 * E : 2 * E + 1])
    drift = total(notes[:, 2 * E + 1 : 2 * E + 2])
    before = [
        jnp.concatenate(
            [
                got_ref[pl.ds(E * HB + 1 + e * HB + h, devices, stride=step), :]
                for e in range(E)
            ],
            axis=0,
        )
        for h in range(HB)
    ] if step > 2 * E * HB else None
    rows = ids.shape[0]
    spread = jnp.zeros((count, BLK), F32)
    for h in range(HB):
        spread = spread + weight * (sums[h] / own_safe - means[h][rows:]) ** 2
    gap = gap + total(spread)
    return positive[:rows], [m[:rows] for m in means], [m[rows:] for m in means], before, weight, gap, drift


def moved(weight, means, before):
    change = jnp.zeros_like(weight)
    for mean, old in zip(means, before):
        change = change + weight * (mean - old) ** 2
    return total(change)


def put_sums(gap, drift, out_ref):
    lane = lax.broadcasted_iota(jnp.int32, out_ref.shape, 1)
    out_ref[...] = jnp.where(lane == 0, gap, drift)


def scaled(penalty, own_ref, other_refs):
    sums = own_ref[...]
    for ref in other_refs:
        sums = sums + ref[...]
    return penalty * jnp.sqrt(sums[0:1, 0:1] / (sums[0:1, 1:2] + EPSILON))


def nodes_kernel(
    S, J, HB, devices, got_ref, id_ref, mu_ref, h_ref, ml_ref, an_out, ml_out, ent_ref, sums_ref
):
    Q = J * S
    shared, means, entry_means, before, weight, gap, drift = read_nodes(
        J, HB, got_ref, id_ref[...], devices
    )
    put_sums(gap, drift + moved(weight, entry_means, before), sums_ref)
    for h in range(HB):
        at = pl.ds(h * Q, Q)
        ent_ref[h] = entry_means[h]
        anchor = jnp.where(shared, means[h], mu_ref[at, :])
        an_out[at, :] = anchor
        ml_out[at, :] = ml_ref[at, :] + RHO_START * (h_ref[at, :] - anchor)


def second_kernel(
    S, J, R, NZ, HB, pp_ref, pc_ref, hp_ref, hc_ref, cb_ref, ml_ref, an_ref, id_ref, wb_ref, sums_ref, sums2_ref, pieces_ref, *rest
):
    other_refs = rest[: R - 1]
    p_out, h_out, mu_out, send_ref, step_ref, pen_ref, all_sc = rest[R - 1 :]
    Q = J * S
    own = lax.axis_index("rows")
    slot = lambda ref, k: ref[k * Q : (k + 1) * Q, :]
    penalty = scaled(RHO_START, sums_ref, [sums2_ref])
    pen_ref[...] = jnp.broadcast_to(penalty, pen_ref.shape)
    anchors = [slot(an_ref, h) for h in range(HB)]
    hedge = [slot(ml_ref, h) + penalty * (slot(hp_ref, h) - anchors[h]) for h in range(HB)]
    placed, hedged = primal_step(
        S, J, R, NZ, HB, own, pieces_ref, other_refs, pp_ref, pc_ref, hp_ref, hc_ref, cb_ref, hedge, all_sc
    )
    finish_step(
        S, J, R, NZ, HB, own, pp_ref, placed, hedged, anchors, False, id_ref[...], wb_ref[...], p_out, h_out, mu_out, send_ref, step_ref
    )


def last_kernel(
    S, J, HB, devices, got_ref, id_ref, ent_ref, mu_ref, h_ref, ml_ref, pen_ref, ml_out, sums_ref
):
    Q = J * S
    shared, means, entry_means, before, weight, gap, drift = read_nodes(
        J, HB, got_ref, id_ref[...], devices
    )
    drift = drift + moved(weight, entry_means, [ent_ref[h] for h in range(HB)])
    put_sums(gap, drift, sums_ref)
    penalty = pen_ref[0:1, 0:1]
    for h in range(HB):
        at = pl.ds(h * Q, Q)
        anchor = jnp.where(shared, means[h], mu_ref[at, :])
        ml_out[at, :] = ml_ref[at, :] + penalty * (h_ref[at, :] - anchor)


def order_kernel(S, J, HB, ml_ref, out_ref):
    for h in range(HB):
        for j in range(J):
            src = pl.ds(h * J * S + j * S, S)
            out_ref[pl.ds(h * J + j, S, stride=HB * J), :] = ml_ref[src, :]


def last_dual_kernel(dual_ref, rhs_ref, image_ref, image2_ref, out_ref):
    image = image_ref[...] + image2_ref[...]
    out_ref[...] = jnp.maximum(dual_ref[...] + SIGMA_STEP * (image - rhs_ref[...]), 0.0)


def penalty_kernel(pen_ref, sums_ref, sums2_ref, out_ref):
    out_ref[...] = scaled(pen_ref[0:1, 0:1], sums_ref, [sums2_ref])


def bulk_kernel(S, J, R, NZ, HB, first, count, parts, cols_ref, primal_ref, cost_ref, p_ref, h_ref, *rest):
    out_hbm, out_ref, sems = rest[-3:]
    K, Q = R * NZ, J * S
    step = count // parts
    copies = [
        pltpu.make_async_copy(
            out_ref.at[pl.ds(i * step, step)], out_hbm.at[pl.ds(first + i * step, step)], sems.at[i]
        )
        for i in range(parts)
    ]
    for i in range(count):
        s = first + i
        move = TAU_STEP * cost_ref[s].astype(F32)
        x = primal_ref[s].astype(F32)
        for _ in range(SWEEPS):
            x = jnp.maximum(x - move, 0.0)
        out_ref[i] = x
        for j in range(J):
            for k in range(K):
                c = cols_ref[k // NZ, j, k % NZ, s]
                out_ref[i, pl.ds(c * J + j, 1), :] = p_ref[pl.ds(k * Q + j * S + s, 1), :]
            for h in range(HB):
                out_ref[i, pl.ds(h * J + j, 1), :] = h_ref[pl.ds(h * Q + j * S + s, 1), :]
        if (i + 1) % step == 0:
            copies[i // step].start()
    for copy in copies:
        copy.wait()


def merge_kernel(apart, x_ref, y_ref, *rest):
    out_ref = rest[-1]
    rows = x_ref.shape[0]
    high = lax.rem(lax.axis_index("scen") // apart, 2)
    out_ref[pl.ds(pl.multiple_of(high * rows, 8), rows), :] = x_ref[...]
    out_ref[pl.ds(pl.multiple_of((1 - high) * rows, 8), rows), :] = y_ref[...]


def local(
    sizes,
    lp_blocks,
    block_columns,
    scenario_nodes,
    scenario_weights,
    cost,
    bounds_rhs,
    primal_start,
    dual_start,
    multiplier_start,
    consensus_start,
):
    scens, R, sections = sizes
    S, J, columns = cost.shape
    NZ = lp_blocks.shape[3]
    hedged = multiplier_start.shape[2]
    HB, C = hedged // BLK, columns // BLK
    K, Q = R * NZ, J * S
    devices = scens
    message = -(-(2 * J * HB + 1) // 8) * 8
    message1 = -(-(4 * J * HB + 1) // 8) * 8
    static = (S, J, R, NZ, HB)

    def interleave(x):
        return x.reshape(S, J, -1, BLK).transpose(0, 2, 1, 3).reshape(S, -1, BLK)

    def uninterleave(x):
        return x.reshape(S, -1, J, BLK).transpose(0, 2, 1, 3).reshape(S, J, -1)

    columns_of = block_columns.transpose(1, 2, 3, 0)
    lp = in_hbm(lp_blocks.reshape(S, J * NZ, BLK, BLK))
    primal, price = in_hbm(interleave(primal_start)), in_hbm(interleave(cost))
    mult = interleave(multiplier_start).reshape(S * HB * J, BLK)

    def from_rows(x):
        return [
            lax.ppermute(x, "rows", [((i + q) % R, i) for i in range(R)]) for q in range(1, R)
        ]

    def from_section(x):
        return lax.ppermute(x, "section", [(i, (i + 1) % sections) for i in range(sections)])

    def partner(x, apart):
        return lax.ppermute(x, "scen", [(i, i ^ apart) for i in range(scens)])

    def merge(x, y, apart, *after):
        return pl.pallas_call(
            functools.partial(merge_kernel, apart),
            out_shape=near(2 * x.shape[0], BLK),
            in_specs=[VMEM] * 2 + [HBM if far else VMEM for far, _ in after],
            out_specs=VMEM,
            compiler_params=params(4),
            name="merge",
        )(x, y, *[in_hbm(z) if far else z for far, z in after])

    def exchange(x, *work):
        if scens & (scens - 1):
            return lax.all_gather(x, "scen", axis=0, tiled=True)
        apart, turn = scens // 2, 0
        while apart:
            y = partner(x, apart)
            x = merge(x, y, apart, *(work[turn]() if turn < len(work) else ()))
            apart, turn = apart // 2, turn + 1
        return x

    def near_like(x):
        return pltpu.VMEM(x.shape, x.dtype)

    parts = max(p for p in (4, 3, 2, 1) if S % p == 0)
    pieces, lp, primal = pl.pallas_call(
        functools.partial(pieces_kernel, S, J, NZ),
        out_shape=[near(NZ * Q, BLK), near_like(lp), near_like(primal)],
        in_specs=[HBM] * 3,
        out_specs=[VMEM] * 3,
        scratch_shapes=[
            pltpu.SemaphoreType.DMA((parts,)),
            pltpu.VMEM(dual_start.shape, F32),
            pltpu.SemaphoreType.DMA,
            pltpu.SemaphoreType.DMA,
        ],
        compiler_params=params(16),
        name="pieces",
    )(lp, in_hbm(dual_start), primal)
    others = from_rows(pieces)

    pp, pc, hp, hc, cb, ml, an, ids, wb, price = pl.pallas_call(
        functools.partial(setup_kernel, *static),
        out_shape=[near(K * Q, BLK)] * 2
        + [near(HB * Q, BLK)] * 2
        + [near(K * Q, BLK)]
        + [near(HB * Q, BLK)] * 2
        + [near(Q, BLK)] * 2
        + [near_like(price)],
        in_specs=[SMEM] * 3 + [VMEM, HBM, VMEM, HBM],
        out_specs=[VMEM] * 10,
        scratch_shapes=[pltpu.VMEM((S * K * J, BLK), jnp.int32)]
        + [pltpu.VMEM((S * K * J, BLK), F32)] * 2
        + [pltpu.VMEM((S * HB * J, BLK), F32)] * 2
        + [pltpu.VMEM(consensus_start.shape, F32)]
        + [pltpu.SemaphoreType.DMA] * 2,
        compiler_params=params(16),
        name="setup",
    )(columns_of, scenario_nodes, scenario_weights, in_vmem(primal), price, mult, in_hbm(consensus_start))
    primal = in_vmem(primal)

    def step_out(rows):
        return [
            near(K * Q, BLK),
            near(HB * Q, BLK),
            near(HB * Q, BLK),
            near(rows, BLK),
            near(NZ * Q, BLK),
        ]

    def image_of(step):
        return pl.pallas_call(
            functools.partial(image_kernel, S, J, NZ),
            out_shape=near(S, BLK),
            in_specs=[VMEM] * 2,
            out_specs=VMEM,
            compiler_params=params(8),
            name="image",
        )(lp, step)

    scratch = [pltpu.VMEM((K * Q, BLK), F32)]
    p1, h1, mu1, send1, step1 = pl.pallas_call(
        functools.partial(first_kernel, *static),
        out_shape=step_out(message1),
        in_specs=[VMEM] * (10 + R - 1),
        out_specs=[VMEM] * 5,
        scratch_shapes=scratch,
        compiler_params=params(8),
        name="first",
    )(pp, pc, hp, hc, cb, ml, an, ids, wb, pieces, *others)
    made = {}

    def image_work():
        made["image"] = image_of(step1)
        return ((False, made["image"]),)

    def dual_work():
        made["dual"], made["pieces"] = pl.pallas_call(
            functools.partial(dual_kernel, S, J, NZ),
            out_shape=[near(S, BLK), near(NZ * Q, BLK)],
            in_specs=[VMEM] * 5,
            out_specs=[VMEM] * 2,
            compiler_params=params(8),
            name="dual",
        )(lp, dual_start, bounds_rhs, made["image"], from_section(made["image"]))
        return ((False, made["pieces"]),)

    got1 = exchange(send1, image_work, dual_work)
    dual1, pieces2 = made["dual"], made["pieces"]
    others2 = from_rows(pieces2)

    an1, ml1, ent1, sums1 = pl.pallas_call(
        functools.partial(nodes_kernel, S, J, HB, devices),
        out_shape=[near(HB * Q, BLK)] * 2 + [near(HB, 2 * J * devices, BLK), near(8, BLK)],
        in_specs=[VMEM] * 5,
        out_specs=[VMEM] * 4,
        compiler_params=params(8),
        name="nodes",
    )(got1, ids, mu1, h1, ml)
    sums1b = from_section(sums1)

    p2, h2, mu2, send2, step2, pen1 = pl.pallas_call(
        functools.partial(second_kernel, *static),
        out_shape=step_out(message) + [near(8, BLK)],
        in_specs=[VMEM] * (12 + R - 1),
        out_specs=[VMEM] * 6,
        scratch_shapes=scratch,
        compiler_params=params(8),
        name="second",
    )(p1, pc, h1, hc, cb, ml1, an1, ids, wb, sums1, sums1b, pieces2, *others2)
    half = S // 2

    def bulk(first, count, *into):
        cuts = max(p for p in (3, 2, 1) if count % p == 0)
        return pl.pallas_call(
            functools.partial(bulk_kernel, *static, first, count, cuts),
            out_shape=shape(S, C * J, BLK),
            in_specs=[SMEM] + [VMEM] * 4 + [HBM] * len(into),
            out_specs=HBM,
            scratch_shapes=[pltpu.VMEM((count, C * J, BLK), F32), pltpu.SemaphoreType.DMA((cuts,))],
            input_output_aliases={5: 0} if into else {},
            compiler_params=params(8),
            name="bulk",
        )(columns_of, primal, price, p2, h2, *into)

    def last_image_work():
        made["image"] = image_of(step2)
        return ((False, made["image"]),)

    def bulk_work():
        made["out"] = bulk(0, half)
        made["image2"] = from_section(made["image"])
        return ((True, made["out"]),)

    def rest_work():
        made["out"] = bulk(half, S - half, made["out"])
        made["dual"] = pl.pallas_call(
            last_dual_kernel,
            out_shape=shape(S, BLK),
            in_specs=[VMEM] * 4,
            out_specs=VMEM,
            compiler_params=params(4),
            name="last_dual",
        )(dual1, bounds_rhs, made["image"], made["image2"])
        return ((True, made["out"]), (True, made["dual"]))

    got2 = exchange(send2, last_image_work, bulk_work, rest_work)
    out, dual2 = made["out"], made["dual"]
    ml2, sums2 = pl.pallas_call(
        functools.partial(last_kernel, S, J, HB, devices),
        out_shape=[near(HB * Q, BLK), near(8, BLK)],
        in_specs=[VMEM] * 7,
        out_specs=[VMEM] * 2,
        compiler_params=params(8),
        name="last",
    )(got2, ids, ent1, mu2, h2, ml1, pen1)
    ml2 = pl.pallas_call(
        functools.partial(order_kernel, S, J, HB),
        out_shape=shape(S * HB * J, BLK),
        in_specs=[VMEM],
        out_specs=VMEM,
        compiler_params=params(4),
        name="order",
    )(ml2)
    pen2 = pl.pallas_call(
        penalty_kernel,
        out_shape=shape(1, 1),
        in_specs=[VMEM] * 3,
        out_specs=VMEM,
        compiler_params=params(4),
        name="penalty",
    )(pen1, sums2, from_section(sums2))

    return (
        uninterleave(out),
        dual2,
        uninterleave(ml2.reshape(S, HB * J, BLK)),
        pen2.reshape(()),
    )


def solution(mesh):
    sizes = tuple(mesh.shape[a] for a in ("scen", "rows", "section"))
    in_specs = (
        P("scen", "rows", "section", None, None, None),
        P("scen", None, "section", None),
        P(None, "scen"),
        P("scen"),
        P("scen", "section", None),
        P("scen", "rows"),
        P("scen", "section", None),
        P("scen", "rows"),
        P("scen", "section", None),
        P(),
    )
    out_specs = (P("scen", "section", None), P("scen", "rows"), P("scen", "section", None), P())
    return jax.shard_map(
        functools.partial(local, sizes),
        mesh=mesh,
        in_specs=in_specs,
        out_specs=out_specs,
        check_vma=False,
    )
```

time: 68.7 us -> 42.7 us (0.62); the launches traced: 67.7 us -> 42.6 us
  local copies, waits for them, and re-layouts: 30.9 us -> 0.03 us
  Pallas kernels: 16 us -> 19 us
  waiting for transfers between devices: 5.28 us -> 7.01 us
  starting transfers between devices: 14.7 us -> 15.7 us
    unnamed x97 -> x12, local copies, waits for them, and re-layouts: 30.9 us -> 0.03 us
    ppermute x0 -> x6, starting transfers between devices: none -> 11.6 us  [partner(): return lax.ppermute(x, 'scen', [(i, i ^ apart) for i in range(scens)])]
    all_to_all x2 -> x0, starting transfers between devices: 10.4 us -> none  [exchange(): return lax.all_to_all(x, ('scen', 'section'), 0, 0).reshape(-1, BLK)]
    pallas_call x5 -> x18, Pallas kernels: 12.6 us -> 17.8 us  [the longest x2 4.26 us: bulk(): pl.pallas_call(functools.partial(bulk_kernel, *static, first, count, cuts...]
    ppermute x0 -> x6, waiting for transfers between devices: none -> 3.17 us  [partner(): return lax.ppermute(x, 'scen', [(i, i ^ apart) for i in range(scens)])]
    ppermute x2 -> x4, waiting for transfers between devices: 0.84 us -> 3.4 us  [from_section(): lax.ppermute(x, 'section', [(i, (i + 1) % sections) for i in range(sectio...]
    ppermute x2, waiting for transfers between devices: 2.94 us -> 0.45 us  [from_rows(): lax.ppermute(x, 'rows', [((i + q) % R, i) for i in range(R)])]
    all_to_all x2 -> x0, waiting for transfers between devices: 1.5 us -> none  [exchange(): return lax.all_to_all(x, ('scen', 'section'), 0, 0).reshape(-1, BLK)]
  transfers between devices with their start and end apart: 6 -> 12, of which waited for: 3 -> 10; matrix products, arithmetic and copies ran while one was open for 0% -> 0% of each run, Pallas kernels for 13% -> 32%
where the time goes in v2:
time: 42.7 us; the launch traced here: 42.6 us
  Pallas kernels  19 us (44%)
  starting transfers between devices  15.7 us (37%)
  waiting for transfers between devices  7.01 us (16%)
  between operations  0.81 us (2%)
    ppermute x6, starting transfers between devices, partner(): return lax.ppermute(x, 'scen', [(i, i ^ apart) for i in range(scens)])  11.6 us
    pallas_call x2, Pallas kernels, bulk(): pl.pallas_call(functools.partial(bulk_kernel, *static, first, count, cuts...  4.26 us
    ppermute x2, starting transfers between devices, from_rows(): lax.ppermute(x, 'rows', [((i + q) % R, i) for i in range(R)])  3.81 us
    pallas_call x2, Pallas kernels, image_of(): pl.pallas_call(functools.partial(image_kernel, S, J, NZ), out_shape=near(...  3.46 us
    ppermute x4, waiting for transfers between devices, from_section(): lax.ppermute(x, 'section', [(i, (i + 1) % sections) for i in range(sectio...  3.4 us
    pallas_call x1, Pallas kernels, local(): pl.pallas_call(functools.partial(setup_kernel, *static), out_shape=[near(...  3.23 us
    ppermute x6, waiting for transfers between devices, partner(): return lax.ppermute(x, 'scen', [(i, i ^ apart) for i in range(scens)])  3.17 us
    pallas_call x1, Pallas kernels, local(): pl.pallas_call(functools.partial(pieces_kernel, S, J, NZ), out_shape=[nea...  2.8 us
  transfers between devices with their start and end apart: 12, of which 10 were waited for; matrix products, arithmetic and copies ran while one was open for 0% of the time, Pallas kernels for 32%

profile of v2, /device:TPU:0, one launch (start us, length us, event | category | flops | bytes accessed | tf_op | source)
XLA Modules:
  0.0 42.6 jit_solution(1875861562665155822)
XLA Ops:
  0.7 2.8 %pieces.1 = (f32[96,128]{1,0:T(8,128)S(1)}, bf16[24,4,128,128]{3,2,1,0:T(8,128)(2,1)S(1)}, bf16[24,352,128]{2,1,0:T(8,128)(2,1)S(1)}) custom-call(bf16[24,4,128,128]{3,2,1,0:T(8,128)(2,1)} %bitcast.33, f32[24,128]{1,0:T(8,128)} %dual_ref.1, bf16[24,352,128]{2,1,0:T(8,128)(2,1)} %bitcast.34), custom_call_target="tpu_custom_call" | custom-call | tf_op jit(solution)/shard_map/pieces/pallas_call | solution.py:568
  3.5 3.0 %collective-permute-start = (f32[96,128]{1,0:T(8,128)S(1)}, f32[96,128]{1,0:T(8,128)S(1)}, u32[]{:S(2)}, u32[]{:S(2)}) collective-permute-start(f32[96,128]{1,0:T(8,128)S(1)} %get-tuple-element.47.pieces_ref), channel_id=1, source_target_pairs={{2,0},{0,2},{3,1},{1,3},{6,4},{4,6},{7,5},{5,7},{10,8},{8,10},{11,... | collective-permute-start | bytes 147464 | tf_op jit(solution)/shard_map/ppermute | solution.py:535
  6.5 3.2 %setup.1 = (f32[192,128]{1,0:T(8,128)S(1)}, f32[192,128]{1,0:T(8,128)S(1)}, f32[192,128]{1,0:T(8,128)S(1)}, f32[192,128]{1,0:T(8,128)S(1)}, f32[192,128]{1,0:T(8...) custom-call(s32[2,2,2,24]{3,2,1,0:T(2,128)S(1)} %bitcast.29, ...), custom_call_target="tpu_custom_call" | custom-call | tf_op jit(solution)/shard_map/setup/pallas_call | solution.py:584
  9.8 0.6 %first.1 = (f32[192,128]{1,0:T(8,128)S(1)}, f32[192,128]{1,0:T(8,128)S(1)}, f32[192,128]{1,0:T(8,128)S(1)}, f32[40,128]{1,0:T(8,128)S(1)}, f32[96,128]{1,0:T(8,128)S(1)}) custom-call(f32[192,128]{1,0:T(8,128)S(1)} %get-tuple-element.38.pp_ref, f32[192,128]{1,0:T(8,128)S(1)} %get-tuple-element.39.pc_ref, f32[192,128]{1,0:T(8,128)S(1)} %get-tuple-element.40.hp_ref, ...), custom_call_target="tpu_custom_call" | custom-call | tf_op jit(solution)/shard_map/first/pallas_call | solution.py:624
  10.3 2.7 %collective-permute-start.1 = (f32[40,128]{1,0:T(8,128)S(1)}, f32[40,128]{1,0:T(8,128)S(1)}, u32[]{:S(2)}, u32[]{:S(2)}) collective-permute-start(f32[40,128]{1,0:T(8,128)S(1)} %get-tuple-element.50.x_ref), channel_id=1, source_target_pairs={{0,16},{4,20},{8,24},{12,28},{16,0},{20,4},{24,8},{28,12},{1,17},{... | collective-permute-start | bytes 61448 | tf_op jit(solution)/shard_map/ppermute | solution.py:542
  13.0 1.7 %image.2.rest_0_.image_ref = f32[24,128]{1,0:T(8,128)S(1)} custom-call(bf16[24,4,128,128]{3,2,1,0:T(8,128)(2,1)S(1)} %get-tuple-element.51.lp_ref, f32[96,128]{1,0:T(8,128)S(1)} %get-tuple-element.52.step_ref), custom_call_target="tpu_custom_call" | custom-call | tf_op jit(solution)/shard_map/image/pallas_call | solution.py:614
  14.7 0.4 collective-permute-done.1.y_ref
  15.1 1.6 %collective-permute-start.2 = (f32[80,128]{1,0:T(8,128)S(1)}, f32[80,128]{1,0:T(8,128)S(1)}, u32[]{:S(2)}, u32[]{:S(2)}) collective-permute-start(f32[80,128]{1,0:T(8,128)S(1)} %merge.6.x_ref), channel_id=1, source_target_pairs={{0,8},{4,12},{8,0},{12,4},{16,24},{20,28},{24,16},{28,20},{1,9},{5... | collective-permute-start | bytes 122888 | tf_op jit(solution)/shard_map/ppermute | solution.py:542
  16.7 1.2 %collective-permute-done.3.image2_ref = f32[24,128]{1,0:T(8,128)S(1)} collective-permute-done((f32[24,128]{1,0:T(8,128)S(1)}, f32[24,128]{1,0:T(8,128)S(1)}, u32[]{:S(2)}, u32[]{:S(2)}) %collective-permute-start.3) | collective-permute-done | bytes 12320 | tf_op jit(solution)/shard_map/ppermute | solution.py:539
  17.9 0.9 %dual.1 = (f32[24,128]{1,0:T(8,128)S(1)}, f32[96,128]{1,0:T(8,128)S(1)}) custom-call(bf16[24,4,128,128]{3,2,1,0:T(8,128)(2,1)S(1)} %get-tuple-element.51.lp_ref, f32[24,128]{1,0:T(8,128)S(1)} %copy-done.1, f32[24,128]{1,0:T(8,128)S(1)} %copy-done.2, f32[24,128]{1,0:T(8,128)S(1)} %image.2.rest_0_.image_ref, f32[24,128]{1,0:T(8,128)S(1)} %collective-permute-done.3.image2_ref), custom_call_target="tpu_custom_call" | custom-call | tf_op jit(solution)/shard_map/dual/pallas_call | solution.py:640
  18.8 0.3 collective-permute-done.2.y_ref
  19.1 1.6 %collective-permute-start.4 = (f32[160,128]{1,0:T(8,128)S(1)}, f32[160,128]{1,0:T(8,128)S(1)}, u32[]{:S(2)}, u32[]{:S(2)}) collective-permute-start(f32[160,128]{1,0:T(8,128)S(1)} %merge.7.x_ref), channel_id=1, source_target_pairs={{0,4},{4,0},{8,12},{12,8},{16,20},{20,16},{24,28},{28,24},{1,5},{5... | collective-permute-start | bytes 245768 | tf_op jit(solution)/shard_map/ppermute | solution.py:542
  20.7 0.8 %collective-permute-start.6 = (f32[96,128]{1,0:T(8,128)S(1)}, f32[96,128]{1,0:T(8,128)S(1)}, u32[]{:S(2)}, u32[]{:S(2)}) collective-permute-start(f32[96,128]{1,0:T(8,128)S(1)} %get-tuple-element.53.rest_0_.pieces_ref), channel_id=1, source_target_pairs={{2,0},{0,2},{3,1},{1,3},{6,4},{4,6},{7,5},{5,7},{10,8},{8,10},{11,... | collective-permute-start | bytes 147464 | tf_op jit(solution)/shard_map/ppermute | solution.py:535
  21.5 2.1 %collective-permute-done.4.y_ref = f32[160,128]{1,0:T(8,128)S(1)} collective-permute-done((f32[160,128]{1,0:T(8,128)S(1)}, f32[160,128]{1,0:T(8,128)S(1)}, u32[]{:S(2)}, u32[]{:S(2)}) %collective-permute-start.4) | collective-permute-done | bytes 81952 | tf_op jit(solution)/shard_map/ppermute | solution.py:542
  23.6 0.6 %nodes.1 = (f32[192,128]{1,0:T(8,128)S(1)}, f32[192,128]{1,0:T(8,128)S(1)}, f32[4,32,128]{2,1,0:T(8,128)S(1)}, f32[8,128]{1,0:T(8,128)S(1)}) custom-call(f32[320,128]{1,0:T(8,128)S(1)} %merge.8.got_ref, f32[48,128]{1,0:T(8,128)S(1)} %get-tuple-element.45.id_ref, f32[192,128]{1,0:T(8,128)S(1)} %get-tuple-element.54.mu_ref, ...), custom_call_target="tpu_custom_call" | custom-call | tf_op jit(solution)/shard_map/nodes/pallas_call | solution.py:654
  24.3 0.4 %collective-permute-done.6.rest_0_ = f32[96,128]{1,0:T(8,128)S(1)} collective-permute-done((f32[96,128]{1,0:T(8,128)S(1)}, f32[96,128]{1,0:T(8,128)S(1)}, u32[]{:S(2)}, u32[]{:S(2)}) %collective-permute-start.6) | collective-permute-done | bytes 49184 | tf_op jit(solution)/shard_map/ppermute | solution.py:535
  24.8 0.7 %collective-permute-done.5.sums2_ref = f32[8,128]{1,0:T(8,128)S(1)} collective-permute-done((f32[8,128]{1,0:T(8,128)S(1)}, f32[8,128]{1,0:T(8,128)S(1)}, u32[]{:S(2)}, u32[]{:S(2)}) %collective-permute-start.5) | collective-permute-done | bytes 4128 | tf_op jit(solution)/shard_map/ppermute | solution.py:539
  25.5 0.6 %second.1 = (f32[192,128]{1,0:T(8,128)S(1)}, f32[192,128]{1,0:T(8,128)S(1)}, f32[192,128]{1,0:T(8,128)S(1)}, f32[24,128]{1,0:T(8,128)S(1)}, f32[96,128]{1,0:T(8,128)S(1)}, /*index=5*/f32[8,128]{1,0:T(8,128)S(1)}) custom-call(f32[192,128]{1,0:T(8,128)S(1)} %get-tuple-element.48.pp_ref, f32[192,128]{1,0:T(8,128)S(1)} %get-tuple-element.39.pc_ref, ...), custom_call_target="tpu_custom_call" | custom-call | tf_op jit(solution)/shard_map/second/pallas_call | solution.py:664
  26.1 2.7 %collective-permute-start.8 = (f32[24,128]{1,0:T(8,128)S(1)}, f32[24,128]{1,0:T(8,128)S(1)}, u32[]{:S(2)}, u32[]{:S(2)}) collective-permute-start(f32[24,128]{1,0:T(8,128)S(1)} %get-tuple-element.62.x_ref), channel_id=1, source_target_pairs={{0,16},{4,20},{8,24},{12,28},{16,0},{20,4},{24,8},{28,12},{1,17},{... | collective-permute-start | bytes 36872 | tf_op jit(solution)/shard_map/ppermute | solution.py:542
  28.8 1.7 %image.3.image_ref.rest_0_ = f32[24,128]{1,0:T(8,128)S(1)} custom-call(bf16[24,4,128,128]{3,2,1,0:T(8,128)(2,1)S(1)} %get-tuple-element.51.lp_ref, f32[96,128]{1,0:T(8,128)S(1)} %get-tuple-element.61.step_ref), custom_call_target="tpu_custom_call" | custom-call | tf_op jit(solution)/shard_map/image/pallas_call | solution.py:614
  30.5 0.3 collective-permute-done.8.y_ref
  30.8 1.6 %collective-permute-start.9 = (f32[48,128]{1,0:T(8,128)S(1)}, f32[48,128]{1,0:T(8,128)S(1)}, u32[]{:S(2)}, u32[]{:S(2)}) collective-permute-start(f32[48,128]{1,0:T(8,128)S(1)} %merge.9.x_ref), channel_id=1, source_target_pairs={{0,8},{4,12},{8,0},{12,4},{16,24},{20,28},{24,16},{28,20},{1,9},{5... | collective-permute-start | bytes 73736 | tf_op jit(solution)/shard_map/ppermute | solution.py:542
  32.4 2.1 %bulk.2.rest_0_ = f32[24,352,128]{2,1,0:T(8,128)} custom-call(s32[2,2,2,24]{3,2,1,0:T(2,128)S(1)} %bitcast.30, bf16[24,352,128]{2,1,0:T(8,128)(2,1)S(1)} %get-tuple-element.36.primal_ref, bf16[24,352,128]{2,1,0:T(8,128)(2,1)S(1)} %get-tuple-element.37.cost_ref, f32[192,128]{1,0:T(8,128)S(1)} %get-tuple-element.58.p_ref, f32[192,128]{1,0:T(8,128)S(1)} %get-tuple-element.59.h_ref), custom_call_target="tpu_custom_call" | custom-call | tf_op jit(solution)/shard_map/bulk/pallas_call | solution.py:677
  34.6 1.5 %collective-permute-start.10 = (f32[96,128]{1,0:T(8,128)S(1)}, f32[96,128]{1,0:T(8,128)S(1)}, u32[]{:S(2)}, u32[]{:S(2)}) collective-permute-start(f32[96,128]{1,0:T(8,128)S(1)} %merge.10.x_ref), channel_id=1, source_target_pairs={{0,4},{4,0},{8,12},{12,8},{16,20},{20,16},{24,28},{28,24},{1,5},{5... | collective-permute-start | bytes 147464 | tf_op jit(solution)/shard_map/ppermute | solution.py:542
  36.2 1.2 %collective-permute-done.7.image2_ref = f32[24,128]{1,0:T(8,128)S(1)} collective-permute-done((f32[24,128]{1,0:T(8,128)S(1)}, f32[24,128]{1,0:T(8,128)S(1)}, u32[]{:S(2)}, u32[]{:S(2)}) %collective-permute-start.7) | collective-permute-done | bytes 12320 | tf_op jit(solution)/shard_map/ppermute | solution.py:539
  37.3 0.6 %last_dual.1.rest_1_ = f32[24,128]{1,0:T(8,128)} custom-call(f32[24,128]{1,0:T(8,128)S(1)} %get-tuple-element.60.dual_ref, f32[24,128]{1,0:T(8,128)S(1)} %copy-done.2, f32[24,128]{1,0:T(8,128)S(1)} %image.3.image_ref.rest_0_, f32[24,128]{1,0:T(8,128)S(1)} %collective-permute-done.7.image2_ref), custom_call_target="tpu_custom_call" | custom-call | tf_op jit(solution)/shard_map/last_dual/pallas_call | solution.py:699
  37.9 2.1 %bulk.3.rest_0_ = f32[24,352,128]{2,1,0:T(8,128)} custom-call(s32[2,2,2,24]{3,2,1,0:T(2,128)S(1)} %bitcast.31, bf16[24,352,128]{2,1,0:T(8,128)(2,1)S(1)} %get-tuple-element.36.primal_ref, bf16[24,352,128]{2,1,0:T(8,128)(2,1)S(1)} %get-tuple-element.37.cost_ref, f32[192,128]{1,0:T(8,128)S(1)} %get-tuple-element.58.p_ref, ...), custom_call_target="tpu_custom_call", output_to_operand_aliasing={{}: (5, {})} | custom-call | tf_op jit(solution)/shard_map/bulk/pallas_call | solution.py:677
  40.1 0.6 %last.1 = (f32[192,128]{1,0:T(8,128)S(1)}, f32[8,128]{1,0:T(8,128)S(1)}) custom-call(f32[192,128]{1,0:T(8,128)S(1)} %merge.11.got_ref, f32[48,128]{1,0:T(8,128)S(1)} %get-tuple-element.45.id_ref, f32[4,32,128]{2,1,0:T(8,128)S(1)} %get-tuple-element.63.ent_ref, f32[192,128]{1,0:T(8,128)S(1)} %get-tuple-element.64.mu_ref, ...), custom_call_target="tpu_custom_call" | custom-call | tf_op jit(solution)/shard_map/last/pallas_call | solution.py:711
  40.7 0.2 collective-permute-start.11
  41.0 0.7 %order.1 = f32[192,128]{1,0:T(8,128)} custom-call(f32[192,128]{1,0:T(8,128)S(1)} %get-tuple-element.66.ml_ref), custom_call_target="tpu_custom_call" | custom-call | tf_op jit(solution)/shard_map/order/pallas_call | solution.py:719
  41.6 0.3 collective-permute-done.11.sums2_ref
  42.0 0.6 %penalty.1 = f32[1,1]{1,0:T(1,128)} custom-call(f32[8,128]{1,0:T(8,128)S(1)} %get-tuple-element.65.pen_ref, f32[8,128]{1,0:T(8,128)S(1)} %get-tuple-element.67.sums_ref, f32[8,128]{1,0:T(8,128)S(1)} %collective-permute-done.11.sums2_ref), custom_call_target="tpu_custom_call" | custom-call | tf_op jit(solution)/shard_map/penalty/pallas_call | solution.py:727
  (24 shorter events, 0.3 us)
Async XLA Ops:
  0.6 5.9 %copy-start = (f32[24,2,512]{2,1,0:T(2,128)S(1)}, f32[24,2,512]{2,1,0:T(2,128)}, u32[]{:S(2)}) copy-start(f32[24,2,512]{2,1,0:T(2,128)} %param.18) | copy-start | bytes 294916
  0.6 5.9 %copy-start.3 = (s32[24,2,2,2]{0,3,2,1:T(2,128)S(1)}, s32[24,2,2,2]{0,3,2,1:T(2,128)}, u32[]{:S(2)}) copy-start(s32[24,2,2,2]{0,3,2,1:T(2,128)} %param.11) | copy-start | bytes 2308
  0.7 5.8 %copy-start.4 = (s32[3,24]{1,0:T(4,128)S(1)}, s32[3,24]{1,0:T(4,128)}, u32[]{:S(2)}) copy-start(s32[3,24]{1,0:T(4,128)} %nodes_ref.1) | copy-start | bytes 868
  0.7 5.8 %copy-start.5 = (f32[24]{0:T(128)S(1)}, f32[24]{0:T(128)}, u32[]{:S(2)}) copy-start(f32[24]{0:T(128)} %weights_ref.1) | copy-start | bytes 292
  3.5 6.3 %collective-permute-start = (f32[96,128]{1,0:T(8,128)S(1)}, f32[96,128]{1,0:T(8,128)S(1)}, u32[]{:S(2)}, u32[]{:S(2)}) collective-permute-start(f32[96,128]{1,0:T(8,128)S(1)} %get-tuple-element.47.pieces_ref), channel_id=1, source_target_pairs={{2,0},{0,2},{3,1},{1,3},{6,4},{4,6},{7,5},{5,7},{10,8},{8,10},{11,... | collective-permute-start | bytes 147464 | tf_op jit(solution)/shard_map/ppermute | solution.py:535
  9.7 8.1 %copy-start.1 = (f32[24,128]{1,0:T(8,128)S(1)}, f32[24,128]{1,0:T(8,128)}, u32[]{:S(2)}) copy-start(f32[24,128]{1,0:T(8,128)} %dual_ref.1) | copy-start | bytes 36868
  9.7 8.1 %copy-start.2 = (f32[24,128]{1,0:T(8,128)S(1)}, f32[24,128]{1,0:T(8,128)}, u32[]{:S(2)}) copy-start(f32[24,128]{1,0:T(8,128)} %rhs_ref.3) | copy-start | bytes 36868
  10.3 4.7 %collective-permute-start.1 = (f32[40,128]{1,0:T(8,128)S(1)}, f32[40,128]{1,0:T(8,128)S(1)}, u32[]{:S(2)}, u32[]{:S(2)}) collective-permute-start(f32[40,128]{1,0:T(8,128)S(1)} %get-tuple-element.50.x_ref), channel_id=1, source_target_pairs={{0,16},{4,20},{8,24},{12,28},{16,0},{20,4},{24,8},{28,12},{1,17},{... | collective-permute-start | bytes 61448 | tf_op jit(solution)/shard_map/ppermute | solution.py:542
  15.1 4.0 %collective-permute-start.2 = (f32[80,128]{1,0:T(8,128)S(1)}, f32[80,128]{1,0:T(8,128)S(1)}, u32[]{:S(2)}, u32[]{:S(2)}) collective-permute-start(f32[80,128]{1,0:T(8,128)S(1)} %merge.6.x_ref), channel_id=1, source_target_pairs={{0,8},{4,12},{8,0},{12,4},{16,24},{20,28},{24,16},{28,20},{1,9},{5... | collective-permute-start | bytes 122888 | tf_op jit(solution)/shard_map/ppermute | solution.py:542
  16.7 1.2 %collective-permute-start.3 = (f32[24,128]{1,0:T(8,128)S(1)}, f32[24,128]{1,0:T(8,128)S(1)}, u32[]{:S(2)}, u32[]{:S(2)}) collective-permute-start(f32[24,128]{1,0:T(8,128)S(1)} %image.2.rest_0_.image_ref), channel_id=1, source_target_pairs={{0,1},{1,0},{2,3},{3,2},{4,5},{5,4},{6,7},{7,6},{8,9},{9,8},{10,11... | collective-permute-start | bytes 36872 | tf_op jit(solution)/shard_map/ppermute | solution.py:539
  19.1 4.5 %collective-permute-start.4 = (f32[160,128]{1,0:T(8,128)S(1)}, f32[160,128]{1,0:T(8,128)S(1)}, u32[]{:S(2)}, u32[]{:S(2)}) collective-permute-start(f32[160,128]{1,0:T(8,128)S(1)} %merge.7.x_ref), channel_id=1, source_target_pairs={{0,4},{4,0},{8,12},{12,8},{16,20},{20,16},{24,28},{28,24},{1,5},{5... | collective-permute-start | bytes 245768 | tf_op jit(solution)/shard_map/ppermute | solution.py:542
  20.7 4.1 %collective-permute-start.6 = (f32[96,128]{1,0:T(8,128)S(1)}, f32[96,128]{1,0:T(8,128)S(1)}, u32[]{:S(2)}, u32[]{:S(2)}) collective-permute-start(f32[96,128]{1,0:T(8,128)S(1)} %get-tuple-element.53.rest_0_.pieces_ref), channel_id=1, source_target_pairs={{2,0},{0,2},{3,1},{1,3},{6,4},{4,6},{7,5},{5,7},{10,8},{8,10},{11,... | collective-permute-start | bytes 147464 | tf_op jit(solution)/shard_map/ppermute | solution.py:535
  24.3 1.2 %collective-permute-start.5 = (f32[8,128]{1,0:T(8,128)S(1)}, f32[8,128]{1,0:T(8,128)S(1)}, u32[]{:S(2)}, u32[]{:S(2)}) collective-permute-start(f32[8,128]{1,0:T(8,128)S(1)} %get-tuple-element.57.sums_ref), channel_id=1, source_target_pairs={{0,1},{1,0},{2,3},{3,2},{4,5},{5,4},{6,7},{7,6},{8,9},{9,8},{10,11... | collective-permute-start | bytes 12296 | tf_op jit(solution)/shard_map/ppermute | solution.py:539
  26.1 4.7 %collective-permute-start.8 = (f32[24,128]{1,0:T(8,128)S(1)}, f32[24,128]{1,0:T(8,128)S(1)}, u32[]{:S(2)}, u32[]{:S(2)}) collective-permute-start(f32[24,128]{1,0:T(8,128)S(1)} %get-tuple-element.62.x_ref), channel_id=1, source_target_pairs={{0,16},{4,20},{8,24},{12,28},{16,0},{20,4},{24,8},{28,12},{1,17},{... | collective-permute-start | bytes 36872 | tf_op jit(solution)/shard_map/ppermute | solution.py:542
  30.8 3.8 %collective-permute-start.9 = (f32[48,128]{1,0:T(8,128)S(1)}, f32[48,128]{1,0:T(8,128)S(1)}, u32[]{:S(2)}, u32[]{:S(2)}) collective-permute-start(f32[48,128]{1,0:T(8,128)S(1)} %merge.9.x_ref), channel_id=1, source_target_pairs={{0,8},{4,12},{8,0},{12,4},{16,24},{20,28},{24,16},{28,20},{1,9},{5... | collective-permute-start | bytes 73736 | tf_op jit(solution)/shard_map/ppermute | solution.py:542
  34.6 5.5 %collective-permute-start.10 = (f32[96,128]{1,0:T(8,128)S(1)}, f32[96,128]{1,0:T(8,128)S(1)}, u32[]{:S(2)}, u32[]{:S(2)}) collective-permute-start(f32[96,128]{1,0:T(8,128)S(1)} %merge.10.x_ref), channel_id=1, source_target_pairs={{0,4},{4,0},{8,12},{12,8},{16,20},{20,16},{24,28},{28,24},{1,5},{5... | collective-permute-start | bytes 147464 | tf_op jit(solution)/shard_map/ppermute | solution.py:542
  36.2 1.2 %collective-permute-start.7 = (f32[24,128]{1,0:T(8,128)S(1)}, f32[24,128]{1,0:T(8,128)S(1)}, u32[]{:S(2)}, u32[]{:S(2)}) collective-permute-start(f32[24,128]{1,0:T(8,128)S(1)} %image.3.image_ref.rest_0_), channel_id=1, source_target_pairs={{0,1},{1,0},{2,3},{3,2},{4,5},{5,4},{6,7},{7,6},{8,9},{9,8},{10,11... | collective-permute-start | bytes 36872 | tf_op jit(solution)/shard_map/ppermute | solution.py:539
  40.7 1.2 %collective-permute-start.11 = (f32[8,128]{1,0:T(8,128)S(1)}, f32[8,128]{1,0:T(8,128)S(1)}, u32[]{:S(2)}, u32[]{:S(2)}) collective-permute-start(f32[8,128]{1,0:T(8,128)S(1)} %get-tuple-element.67.sums_ref), channel_id=1, source_target_pairs={{0,1},{1,0},{2,3},{3,2},{4,5},{5,4},{6,7},{7,6},{8,9},{9,8},{10,11... | collective-permute-start | bytes 12296 | tf_op jit(solution)/shard_map/ppermute | solution.py:539

commit v3 on v2

--- a/solution.py
+++ b/solution.py
@@ -116,7 +116,7 @@
     nodes_ref,
     weights_ref,
     primal_ref,
-    cost_hbm,
+    cost_ref,
     mult_ref,
     table_hbm,
     pp_ref,
@@ -128,19 +128,15 @@
     an_ref,
     id_ref,
     wb_ref,
-    cost_ref,
     idx_sc,
     pp_sc,
     pc_sc,
     hp_sc,
     hc_sc,
     table_ref,
-    cost_sem,
     table_sem,
 ):
     K, Q = R * NZ, J * S
-    cost_copy = pltpu.make_async_copy(cost_hbm, cost_ref, cost_sem)
-    cost_copy.start()
     table_copy = pltpu.make_async_copy(table_hbm, table_ref, table_sem)
     table_copy.start()
     section = lax.axis_index("section")
@@ -188,7 +184,6 @@
             src, dst = pl.ds(h * J + j, S, stride=HB * J), pl.ds(h * Q + j * S, S)
             hp_ref[dst, :] = hp_sc[src, :]
             ml_ref[dst, :] = mult_ref[src, :]
-    cost_copy.wait()
     gather(cost_ref, pc_sc, hc_sc)
     for j in range(J):
         for k in range(K):
@@ -442,47 +437,49 @@
         ml_out[at, :] = ml_ref[at, :] + penalty * (h_ref[at, :] - anchor)
 
 
-def order_kernel(S, J, HB, ml_ref, out_ref):
+def finish_kernel(
+    S, J, HB, ml_ref, dual_ref, rhs_ref, image_ref, image2_ref, ml_out, dual_out
+):
     for h in range(HB):
         for j in range(J):
             src = pl.ds(h * J * S + j * S, S)
-            out_ref[pl.ds(h * J + j, S, stride=HB * J), :] = ml_ref[src, :]
-
-
-def last_dual_kernel(dual_ref, rhs_ref, image_ref, image2_ref, out_ref):
+            ml_out[pl.ds(h * J + j, S, stride=HB * J), :] = ml_ref[src, :]
     image = image_ref[...] + image2_ref[...]
-    out_ref[...] = jnp.maximum(dual_ref[...] + SIGMA_STEP * (image - rhs_ref[...]), 0.0)
+    dual_out[...] = jnp.maximum(dual_ref[...] + SIGMA_STEP * (image - rhs_ref[...]), 0.0)
 
 
 def penalty_kernel(pen_ref, sums_ref, sums2_ref, out_ref):
     out_ref[...] = scaled(pen_ref[0:1, 0:1], sums_ref, [sums2_ref])
 
 
-def bulk_kernel(S, J, R, NZ, HB, first, count, parts, cols_ref, primal_ref, cost_ref, p_ref, h_ref, *rest):
-    out_hbm, out_ref, sems = rest[-3:]
-    K, Q = R * NZ, J * S
-    step = count // parts
-    copies = [
-        pltpu.make_async_copy(
-            out_ref.at[pl.ds(i * step, step)], out_hbm.at[pl.ds(first + i * step, step)], sems.at[i]
-        )
-        for i in range(parts)
-    ]
-    for i in range(count):
-        s = first + i
+def bulk_kernel(S, primal_ref, cost_ref, out_ref):
+    for s in range(S):
         move = TAU_STEP * cost_ref[s].astype(F32)
         x = primal_ref[s].astype(F32)
         for _ in range(SWEEPS):
             x = jnp.maximum(x - move, 0.0)
-        out_ref[i] = x
+        out_ref[s] = x
+
+
+def place_kernel(S, J, R, NZ, HB, first, count, parts, cols_ref, bulk_ref, p_ref, h_ref, *rest):
+    near_ref, out_hbm, sems = rest[-3:]
+    K, Q = R * NZ, J * S
+    step = count // parts
+    copies = []
+    for i in range(count):
+        s = first + i
         for j in range(J):
             for k in range(K):
                 c = cols_ref[k // NZ, j, k % NZ, s]
-                out_ref[i, pl.ds(c * J + j, 1), :] = p_ref[pl.ds(k * Q + j * S + s, 1), :]
+                near_ref[s, pl.ds(c * J + j, 1), :] = p_ref[pl.ds(k * Q + j * S + s, 1), :]
             for h in range(HB):
-                out_ref[i, pl.ds(h * J + j, 1), :] = h_ref[pl.ds(h * Q + j * S + s, 1), :]
+                near_ref[s, pl.ds(h * J + j, 1), :] = h_ref[pl.ds(h * Q + j * S + s, 1), :]
         if (i + 1) % step == 0:
-            copies[i // step].start()
+            at = pl.ds(s + 1 - step, step)
+            copies.append(
+                pltpu.make_async_copy(near_ref.at[at], out_hbm.at[at], sems.at[i // step])
+            )
+            copies[-1].start()
     for copy in copies:
         copy.wait()
 
@@ -527,7 +524,7 @@
 
     columns_of = block_columns.transpose(1, 2, 3, 0)
     lp = in_hbm(lp_blocks.reshape(S, J * NZ, BLK, BLK))
-    primal, price = in_hbm(interleave(primal_start)), in_hbm(interleave(cost))
+    primal, price = in_hbm(interleave(primal_start)), in_vmem(interleave(cost))
     mult = interleave(multiplier_start).reshape(S * HB * J, BLK)
 
     def from_rows(x):
@@ -581,21 +578,20 @@
     )(lp, in_hbm(dual_start), primal)
     others = from_rows(pieces)
 
-    pp, pc, hp, hc, cb, ml, an, ids, wb, price = pl.pallas_call(
+    pp, pc, hp, hc, cb, ml, an, ids, wb = pl.pallas_call(
         functools.partial(setup_kernel, *static),
         out_shape=[near(K * Q, BLK)] * 2
         + [near(HB * Q, BLK)] * 2
         + [near(K * Q, BLK)]
         + [near(HB * Q, BLK)] * 2
-        + [near(Q, BLK)] * 2
-        + [near_like(price)],
-        in_specs=[SMEM] * 3 + [VMEM, HBM, VMEM, HBM],
-        out_specs=[VMEM] * 10,
+        + [near(Q, BLK)] * 2,
+        in_specs=[SMEM] * 3 + [VMEM] * 3 + [HBM],
+        out_specs=[VMEM] * 9,
         scratch_shapes=[pltpu.VMEM((S * K * J, BLK), jnp.int32)]
         + [pltpu.VMEM((S * K * J, BLK), F32)] * 2
         + [pltpu.VMEM((S * HB * J, BLK), F32)] * 2
         + [pltpu.VMEM(consensus_start.shape, F32)]
-        + [pltpu.SemaphoreType.DMA] * 2,
+        + [pltpu.SemaphoreType.DMA],
         compiler_params=params(16),
         name="setup",
     )(columns_of, scenario_nodes, scenario_weights, in_vmem(primal), price, mult, in_hbm(consensus_start))
@@ -647,7 +643,18 @@
         )(lp, dual_start, bounds_rhs, made["image"], from_section(made["image"]))
         return ((False, made["pieces"]),)
 
-    got1 = exchange(send1, image_work, dual_work)
+    def bulk_work():
+        made["bulk"] = pl.pallas_call(
+            functools.partial(bulk_kernel, S),
+            out_shape=near(S, C * J, BLK),
+            in_specs=[VMEM] * 2,
+            out_specs=VMEM,
+            compiler_params=params(8),
+            name="bulk",
+        )(primal, price)
+        return ((False, made["bulk"]),)
+
+    got1 = exchange(send1, image_work, dual_work, bulk_work)
     dual1, pieces2 = made["dual"], made["pieces"]
     others2 = from_rows(pieces2)
 
@@ -672,42 +679,33 @@
     )(p1, pc, h1, hc, cb, ml1, an1, ids, wb, sums1, sums1b, pieces2, *others2)
     half = S // 2
 
-    def bulk(first, count, *into):
-        cuts = max(p for p in (3, 2, 1) if count % p == 0)
+    def place(first, count, whole, *into):
+        cuts = max(p for p in (2, 1) if count % p == 0)
         return pl.pallas_call(
-            functools.partial(bulk_kernel, *static, first, count, cuts),
-            out_shape=shape(S, C * J, BLK),
-            in_specs=[SMEM] + [VMEM] * 4 + [HBM] * len(into),
-            out_specs=HBM,
-            scratch_shapes=[pltpu.VMEM((count, C * J, BLK), F32), pltpu.SemaphoreType.DMA((cuts,))],
-            input_output_aliases={5: 0} if into else {},
-            compiler_params=params(8),
-            name="bulk",
-        )(columns_of, primal, price, p2, h2, *into)
+            functools.partial(place_kernel, *static, first, count, cuts),
+            out_shape=[near(S, C * J, BLK), shape(S, C * J, BLK)],
+            in_specs=[SMEM] + [VMEM] * 3 + [HBM] * len(into),
+            out_specs=[VMEM, HBM],
+            scratch_shapes=[pltpu.SemaphoreType.DMA((cuts,))],
+            input_output_aliases={1: 0, 4: 1} if into else {1: 0},
+            compiler_params=params(4),
+            name="place",
+        )(columns_of, whole, p2, h2, *into)
 
     def last_image_work():
         made["image"] = image_of(step2)
         return ((False, made["image"]),)
 
-    def bulk_work():
-        made["out"] = bulk(0, half)
-        made["image2"] = from_section(made["image"])
+    def place_work():
+        made["bulk"], made["out"] = place(0, half, made["bulk"])
         return ((True, made["out"]),)
 
     def rest_work():
-        made["out"] = bulk(half, S - half, made["out"])
-        made["dual"] = pl.pallas_call(
-            last_dual_kernel,
-            out_shape=shape(S, BLK),
-            in_specs=[VMEM] * 4,
-            out_specs=VMEM,
-            compiler_params=params(4),
-            name="last_dual",
-        )(dual1, bounds_rhs, made["image"], made["image2"])
-        return ((True, made["out"]), (True, made["dual"]))
-
-    got2 = exchange(send2, last_image_work, bulk_work, rest_work)
-    out, dual2 = made["out"], made["dual"]
+        made["bulk"], made["out"] = place(half, S - half, made["bulk"], made["out"])
+        return ((True, made["out"]),)
+
+    got2 = exchange(send2, last_image_work, place_work, rest_work)
+    out, image2 = made["out"], made["image"]
     ml2, sums2 = pl.pallas_call(
         functools.partial(last_kernel, S, J, HB, devices),
         out_shape=[near(HB * Q, BLK), near(8, BLK)],
@@ -716,14 +714,14 @@
         compiler_params=params(8),
         name="last",
     )(got2, ids, ent1, mu2, h2, ml1, pen1)
-    ml2 = pl.pallas_call(
-        functools.partial(order_kernel, S, J, HB),
-        out_shape=shape(S * HB * J, BLK),
-        in_specs=[VMEM],
-        out_specs=VMEM,
+    ml2, dual2 = pl.pallas_call(
+        functools.partial(finish_kernel, S, J, HB),
+        out_shape=[shape(S * HB * J, BLK), shape(S, BLK)],
+        in_specs=[VMEM] * 5,
+        out_specs=[VMEM] * 2,
         compiler_params=params(4),
-        name="order",
-    )(ml2)
+        name="finish",
+    )(ml2, dual1, bounds_rhs, image2, from_section(image2))
     pen2 = pl.pallas_call(
         penalty_kernel,
         out_shape=shape(1, 1),

time: 42.7 us -> 40.7 us (0.953)
  waiting for transfers between devices: 7.01 us -> 4.6 us
  starting transfers between devices: 15.7 us -> 16.6 us
  Pallas kernels: 19 us -> 18.4 us
    ppermute x6, waiting for transfers between devices: 3.17 us -> 1.81 us  [partner(): return lax.ppermute(x, 'scen', [(i, i ^ apart) for i in range(scens)])]
    ppermute x4, waiting for transfers between devices: 3.4 us -> 2.28 us  [from_section(): lax.ppermute(x, 'section', [(i, (i + 1) % sections) for i in range(sectio...]
    pallas_call x1, Pallas kernels: 3.23 us -> 2.46 us  [local(): pl.pallas_call(functools.partial(setup_kernel, *static), out_shape=[near(...]
    ppermute x2, starting transfers between devices: 3.81 us -> 4.49 us  [from_rows(): lax.ppermute(x, 'rows', [((i + q) % R, i) for i in range(R)])]
  transfers between devices with their start and end apart: 12 -> 12, of which waited for: 10 -> 10; matrix products, arithmetic and copies ran while one was open for 0% -> 0% of each run, Pallas kernels for 32% -> 34%
where the time goes in v3:
time: 40.7 us; the launch traced here: 40.5 us
  Pallas kernels  18.4 us (45%)
  starting transfers between devices  16.6 us (41%)
  waiting for transfers between devices  4.6 us (11%)
  between operations  0.81 us (2%)
    ppermute x6, starting transfers between devices, partner(): return lax.ppermute(x, 'scen', [(i, i ^ apart) for i in range(scens)])  12 us
    ppermute x2, starting transfers between devices, from_rows(): lax.ppermute(x, 'rows', [((i + q) % R, i) for i in range(R)])  4.49 us
    pallas_call x2, Pallas kernels, place(): pl.pallas_call(functools.partial(place_kernel, *static, first, count, cut...  3.99 us
    pallas_call x2, Pallas kernels, image_of(): pl.pallas_call(functools.partial(image_kernel, S, J, NZ), out_shape=near(...  3.46 us
    pallas_call x1, Pallas kernels, local(): pl.pallas_call(functools.partial(pieces_kernel, S, J, NZ), out_shape=[nea...  2.9 us
    pallas_call x1, Pallas kernels, local(): pl.pallas_call(functools.partial(setup_kernel, *static), out_shape=[near(...  2.46 us
    ppermute x4, waiting for transfers between devices, from_section(): lax.ppermute(x, 'section', [(i, (i + 1) % sections) for i in range(sectio...  2.28 us
    ppermute x6, waiting for transfers between devices, partner(): return lax.ppermute(x, 'scen', [(i, i ^ apart) for i in range(scens)])  1.81 us
  transfers between devices with their start and end apart: 12, of which 10 were waited for; matrix products, arithmetic and copies ran while one was open for 0% of the time, Pallas kernels for 34%

profile of v3, /device:TPU:0, one launch (start us, length us, event | category | flops | bytes accessed | tf_op | source)
XLA Modules:
  0.0 40.5 jit_solution(4503491245878827539)
XLA Ops:
  0.7 2.9 %pieces.1 = (f32[96,128]{1,0:T(8,128)S(1)}, bf16[24,4,128,128]{3,2,1,0:T(8,128)(2,1)S(1)}, bf16[24,352,128]{2,1,0:T(8,128)(2,1)S(1)}) custom-call(bf16[24,4,128,128]{3,2,1,0:T(8,128)(2,1)} %bitcast.35, f32[24,128]{1,0:T(8,128)} %dual_ref.1, bf16[24,352,128]{2,1,0:T(8,128)(2,1)} %bitcast.36), custom_call_target="tpu_custom_call" | custom-call | tf_op jit(solution)/shard_map/pieces/pallas_call | solution.py:565
  3.6 3.0 %collective-permute-start = (f32[96,128]{1,0:T(8,128)S(1)}, f32[96,128]{1,0:T(8,128)S(1)}, u32[]{:S(2)}, u32[]{:S(2)}) collective-permute-start(f32[96,128]{1,0:T(8,128)S(1)} %get-tuple-element.50.pieces_ref), channel_id=1, source_target_pairs={{2,0},{0,2},{3,1},{1,3},{6,4},{4,6},{7,5},{5,7},{10,8},{8,10},{11,... | collective-permute-start | bytes 147464 | tf_op jit(solution)/shard_map/ppermute | solution.py:532
  6.6 2.5 %setup.1 = (f32[192,128]{1,0:T(8,128)S(1)}, f32[192,128]{1,0:T(8,128)S(1)}, f32[192,128]{1,0:T(8,128)S(1)}, f32[192,128]{1,0:T(8,128)S(1)}, f32[192,128]{1,0:T(8...) custom-call(s32[2,2,2,24]{3,2,1,0:T(2,128)S(1)} %bitcast.31, ...), custom_call_target="tpu_custom_call" | custom-call | tf_op jit(solution)/shard_map/setup/pallas_call | solution.py:581
  9.1 0.6 %first.1 = (f32[192,128]{1,0:T(8,128)S(1)}, f32[192,128]{1,0:T(8,128)S(1)}, f32[192,128]{1,0:T(8,128)S(1)}, f32[40,128]{1,0:T(8,128)S(1)}, f32[96,128]{1,0:T(8,128)S(1)}) custom-call(f32[192,128]{1,0:T(8,128)S(1)} %get-tuple-element.41.pp_ref, f32[192,128]{1,0:T(8,128)S(1)} %get-tuple-element.42.pc_ref, f32[192,128]{1,0:T(8,128)S(1)} %get-tuple-element.43.hp_ref, ...), custom_call_target="tpu_custom_call" | custom-call | tf_op jit(solution)/shard_map/first/pallas_call | solution.py:620
  9.7 2.7 %collective-permute-start.1 = (f32[40,128]{1,0:T(8,128)S(1)}, f32[40,128]{1,0:T(8,128)S(1)}, u32[]{:S(2)}, u32[]{:S(2)}) collective-permute-start(f32[40,128]{1,0:T(8,128)S(1)} %get-tuple-element.53.x_ref), channel_id=1, source_target_pairs={{0,16},{4,20},{8,24},{12,28},{16,0},{20,4},{24,8},{28,12},{1,17},{... | collective-permute-start | bytes 61448 | tf_op jit(solution)/shard_map/ppermute | solution.py:539
  12.4 1.7 %image.2.rest_0_.image_ref = f32[24,128]{1,0:T(8,128)S(1)} custom-call(bf16[24,4,128,128]{3,2,1,0:T(8,128)(2,1)S(1)} %get-tuple-element.54.lp_ref, f32[96,128]{1,0:T(8,128)S(1)} %get-tuple-element.55.step_ref), custom_call_target="tpu_custom_call" | custom-call | tf_op jit(solution)/shard_map/image/pallas_call | solution.py:610
  14.1 0.3 collective-permute-done.1.y_ref
  14.4 1.6 %collective-permute-start.2 = (f32[80,128]{1,0:T(8,128)S(1)}, f32[80,128]{1,0:T(8,128)S(1)}, u32[]{:S(2)}, u32[]{:S(2)}) collective-permute-start(f32[80,128]{1,0:T(8,128)S(1)} %merge.6.x_ref), channel_id=1, source_target_pairs={{0,8},{4,12},{8,0},{12,4},{16,24},{20,28},{24,16},{28,20},{1,9},{5... | collective-permute-start | bytes 122888 | tf_op jit(solution)/shard_map/ppermute | solution.py:539
  16.1 1.2 %collective-permute-done.3.image2_ref = f32[24,128]{1,0:T(8,128)S(1)} collective-permute-done((f32[24,128]{1,0:T(8,128)S(1)}, f32[24,128]{1,0:T(8,128)S(1)}, u32[]{:S(2)}, u32[]{:S(2)}) %collective-permute-start.3) | collective-permute-done | bytes 12320 | tf_op jit(solution)/shard_map/ppermute | solution.py:536
  17.3 0.9 %dual.1 = (f32[24,128]{1,0:T(8,128)S(1)}, f32[96,128]{1,0:T(8,128)S(1)}) custom-call(bf16[24,4,128,128]{3,2,1,0:T(8,128)(2,1)S(1)} %get-tuple-element.54.lp_ref, f32[24,128]{1,0:T(8,128)S(1)} %copy-done.2, f32[24,128]{1,0:T(8,128)S(1)} %copy-done.3, f32[24,128]{1,0:T(8,128)S(1)} %image.2.rest_0_.image_ref, f32[24,128]{1,0:T(8,128)S(1)} %collective-permute-done.3.image2_ref), custom_call_target="tpu_custom_call" | custom-call | tf_op jit(solution)/shard_map/dual/pallas_call | solution.py:636
  18.2 0.3 collective-permute-done.2.y_ref
  18.5 1.7 %collective-permute-start.4 = (f32[160,128]{1,0:T(8,128)S(1)}, f32[160,128]{1,0:T(8,128)S(1)}, u32[]{:S(2)}, u32[]{:S(2)}) collective-permute-start(f32[160,128]{1,0:T(8,128)S(1)} %merge.7.x_ref), channel_id=1, source_target_pairs={{0,4},{4,0},{8,12},{12,8},{16,20},{20,16},{24,28},{28,24},{1,5},{5... | collective-permute-start | bytes 245768 | tf_op jit(solution)/shard_map/ppermute | solution.py:539
  20.1 1.5 %collective-permute-start.6 = (f32[96,128]{1,0:T(8,128)S(1)}, f32[96,128]{1,0:T(8,128)S(1)}, u32[]{:S(2)}, u32[]{:S(2)}) collective-permute-start(f32[96,128]{1,0:T(8,128)S(1)} %get-tuple-element.56.rest_0_.pieces_ref), channel_id=1, source_target_pairs={{2,0},{0,2},{3,1},{1,3},{6,4},{4,6},{7,5},{5,7},{10,8},{8,10},{11,... | collective-permute-start | bytes 147464 | tf_op jit(solution)/shard_map/ppermute | solution.py:532
  21.6 1.0 %bulk.1.rest_0_.bulk_ref = f32[24,352,128]{2,1,0:T(8,128)S(1)} custom-call(bf16[24,352,128]{2,1,0:T(8,128)(2,1)S(1)} %get-tuple-element.40.primal_ref, bf16[24,352,128]{2,1,0:T(8,128)(2,1)S(1)} %bitcast.29), custom_call_target="tpu_custom_call" | custom-call | tf_op jit(solution)/shard_map/bulk/pallas_call | solution.py:647
  22.6 0.4 collective-permute-done.4.y_ref
  23.0 0.6 %nodes.1 = (f32[192,128]{1,0:T(8,128)S(1)}, f32[192,128]{1,0:T(8,128)S(1)}, f32[4,32,128]{2,1,0:T(8,128)S(1)}, f32[8,128]{1,0:T(8,128)S(1)}) custom-call(f32[320,128]{1,0:T(8,128)S(1)} %merge.8.got_ref, f32[48,128]{1,0:T(8,128)S(1)} %get-tuple-element.48.id_ref, f32[192,128]{1,0:T(8,128)S(1)} %get-tuple-element.57.mu_ref, ...), custom_call_target="tpu_custom_call" | custom-call | tf_op jit(solution)/shard_map/nodes/pallas_call | solution.py:661
  23.7 0.5 %collective-permute-done.6.rest_0_ = f32[96,128]{1,0:T(8,128)S(1)} collective-permute-done((f32[96,128]{1,0:T(8,128)S(1)}, f32[96,128]{1,0:T(8,128)S(1)}, u32[]{:S(2)}, u32[]{:S(2)}) %collective-permute-start.6) | collective-permute-done | bytes 49184 | tf_op jit(solution)/shard_map/ppermute | solution.py:532
  24.2 0.6 %collective-permute-done.5.sums2_ref = f32[8,128]{1,0:T(8,128)S(1)} collective-permute-done((f32[8,128]{1,0:T(8,128)S(1)}, f32[8,128]{1,0:T(8,128)S(1)}, u32[]{:S(2)}, u32[]{:S(2)}) %collective-permute-start.5) | collective-permute-done | bytes 4128 | tf_op jit(solution)/shard_map/ppermute | solution.py:536
  24.8 0.6 %second.1 = (f32[192,128]{1,0:T(8,128)S(1)}, f32[192,128]{1,0:T(8,128)S(1)}, f32[192,128]{1,0:T(8,128)S(1)}, f32[24,128]{1,0:T(8,128)S(1)}, f32[96,128]{1,0:T(8,128)S(1)}, /*index=5*/f32[8,128]{1,0:T(8,128)S(1)}) custom-call(f32[192,128]{1,0:T(8,128)S(1)} %get-tuple-element.51.pp_ref, f32[192,128]{1,0:T(8,128)S(1)} %get-tuple-element.42.pc_ref, ...), custom_call_target="tpu_custom_call" | custom-call | tf_op jit(solution)/shard_map/second/pallas_call | solution.py:671
  25.5 2.7 %collective-permute-start.7 = (f32[24,128]{1,0:T(8,128)S(1)}, f32[24,128]{1,0:T(8,128)S(1)}, u32[]{:S(2)}, u32[]{:S(2)}) collective-permute-start(f32[24,128]{1,0:T(8,128)S(1)} %get-tuple-element.66.x_ref), channel_id=1, source_target_pairs={{0,16},{4,20},{8,24},{12,28},{16,0},{20,4},{24,8},{28,12},{1,17},{... | collective-permute-start | bytes 36872 | tf_op jit(solution)/shard_map/ppermute | solution.py:539
  28.2 1.7 %image.3.rest_0_.image_ref = f32[24,128]{1,0:T(8,128)S(1)} custom-call(bf16[24,4,128,128]{3,2,1,0:T(8,128)(2,1)S(1)} %get-tuple-element.54.lp_ref, f32[96,128]{1,0:T(8,128)S(1)} %get-tuple-element.67.step_ref), custom_call_target="tpu_custom_call" | custom-call | tf_op jit(solution)/shard_map/image/pallas_call | solution.py:610
  29.9 0.2 collective-permute-done.7.y_ref
  30.1 1.6 %collective-permute-start.8 = (f32[48,128]{1,0:T(8,128)S(1)}, f32[48,128]{1,0:T(8,128)S(1)}, u32[]{:S(2)}, u32[]{:S(2)}) collective-permute-start(f32[48,128]{1,0:T(8,128)S(1)} %merge.9.x_ref), channel_id=1, source_target_pairs={{0,8},{4,12},{8,0},{12,4},{16,24},{20,28},{24,16},{28,20},{1,9},{5... | collective-permute-start | bytes 73736 | tf_op jit(solution)/shard_map/ppermute | solution.py:539
  31.8 2.0 %place.2 = (f32[24,352,128]{2,1,0:T(8,128)S(1)}, f32[24,352,128]{2,1,0:T(8,128)}) custom-call(s32[2,2,2,24]{3,2,1,0:T(2,128)S(1)} %bitcast.32, f32[24,352,128]{2,1,0:T(8,128)S(1)} %bulk.1.rest_0_.bulk_ref, f32[192,128]{1,0:T(8,128)S(1)} %get-tuple-element.61.p_ref, f32[192,128]{1,0:T(8,128)S(1)} %get-tuple-element.62.h_ref), custom_call_target="tpu_custom_call", output_to_operand_aliasing={{0}: (1, {})} | custom-call | tf_op jit(solution)/shard_map/place/pallas_call | solution.py:684
  33.8 0.2 collective-permute-done.8.y_ref
  34.0 1.6 %collective-permute-start.9 = (f32[96,128]{1,0:T(8,128)S(1)}, f32[96,128]{1,0:T(8,128)S(1)}, u32[]{:S(2)}, u32[]{:S(2)}) collective-permute-start(f32[96,128]{1,0:T(8,128)S(1)} %merge.10.x_ref), channel_id=1, source_target_pairs={{0,4},{4,0},{8,12},{12,8},{16,20},{20,16},{24,28},{28,24},{1,5},{5... | collective-permute-start | bytes 147464 | tf_op jit(solution)/shard_map/ppermute | solution.py:539
  35.6 2.0 %place.3 = (f32[24,352,128]{2,1,0:T(8,128)S(1)}, f32[24,352,128]{2,1,0:T(8,128)}) custom-call(s32[2,2,2,24]{3,2,1,0:T(2,128)S(1)} %bitcast.33, f32[24,352,128]{2,1,0:T(8,128)S(1)} %get-tuple-element.63.bulk_ref, f32[192,128]{1,0:T(8,128)S(1)} %get-tuple-element.61.p_ref, ...), custom_call_target="tpu_custom_call", output_to_operand_aliasing={{0}: (1, {}), {1}: (4, {})} | custom-call | tf_op jit(solution)/shard_map/place/pallas_call | solution.py:684
  37.6 0.5 %collective-permute-done.9.y_ref = f32[96,128]{1,0:T(8,128)S(1)} collective-permute-done((f32[96,128]{1,0:T(8,128)S(1)}, f32[96,128]{1,0:T(8,128)S(1)}, u32[]{:S(2)}, u32[]{:S(2)}) %collective-permute-start.9) | collective-permute-done | bytes 49184 | tf_op jit(solution)/shard_map/ppermute | solution.py:539
  38.1 0.6 %last.1 = (f32[192,128]{1,0:T(8,128)S(1)}, f32[8,128]{1,0:T(8,128)S(1)}) custom-call(f32[192,128]{1,0:T(8,128)S(1)} %merge.11.got_ref, f32[48,128]{1,0:T(8,128)S(1)} %get-tuple-element.48.id_ref, f32[4,32,128]{2,1,0:T(8,128)S(1)} %get-tuple-element.68.ent_ref, f32[192,128]{1,0:T(8,128)S(1)} %get-tuple-element.69.mu_ref, ...), custom_call_target="tpu_custom_call" | custom-call | tf_op jit(solution)/shard_map/last/pallas_call | solution.py:709
  38.8 0.7 %finish.1 = (f32[192,128]{1,0:T(8,128)}, f32[24,128]{1,0:T(8,128)}) custom-call(f32[192,128]{1,0:T(8,128)S(1)} %get-tuple-element.71.ml_ref, f32[24,128]{1,0:T(8,128)S(1)} %get-tuple-element.72.dual_ref, f32[24,128]{1,0:T(8,128)S(1)} %copy-done.3, f32[24,128]{1,0:T(8,128)S(1)} %image.3.rest_0_.image_ref, f32[24,128]{1,0:T(8,128)S(1)} %collective-permute-done.10.image2_ref), custom_call_target="tpu_custom_call" | custom-call | tf_op jit(solution)/shard_map/finish/pallas_call | solution.py:717
  39.5 0.5 %collective-permute-done.11.sums2_ref = f32[8,128]{1,0:T(8,128)S(1)} collective-permute-done((f32[8,128]{1,0:T(8,128)S(1)}, f32[8,128]{1,0:T(8,128)S(1)}, u32[]{:S(2)}, u32[]{:S(2)}) %collective-permute-start.11) | collective-permute-done | bytes 4128 | tf_op jit(solution)/shard_map/ppermute | solution.py:536
  39.9 0.6 %penalty.1 = f32[1,1]{1,0:T(1,128)} custom-call(f32[8,128]{1,0:T(8,128)S(1)} %get-tuple-element.70.pen_ref, f32[8,128]{1,0:T(8,128)S(1)} %get-tuple-element.75.sums_ref, f32[8,128]{1,0:T(8,128)S(1)} %collective-permute-done.11.sums2_ref), custom_call_target="tpu_custom_call" | custom-call | tf_op jit(solution)/shard_map/penalty/pallas_call | solution.py:725
  (26 shorter events, 0.3 us)
Async XLA Ops:
  0.6 6.0 %copy-start.4 = (s32[24,2,2,2]{0,3,2,1:T(2,128)S(1)}, s32[24,2,2,2]{0,3,2,1:T(2,128)}, u32[]{:S(2)}) copy-start(s32[24,2,2,2]{0,3,2,1:T(2,128)} %param.11) | copy-start | bytes 2308
  0.6 6.0 %copy-start = (bf16[24,2,22528]{2,1,0:T(2,128)(2,1)S(1)}, bf16[24,2,22528]{2,1,0:T(2,128)(2,1)}, u32[]{:S(2)}) copy-start(bf16[24,2,22528]{2,1,0:T(2,128)(2,1)} %param.14) | copy-start | bytes 6488068
  0.7 6.0 %copy-start.1 = (f32[24,2,512]{2,1,0:T(2,128)S(1)}, f32[24,2,512]{2,1,0:T(2,128)}, u32[]{:S(2)}) copy-start(f32[24,2,512]{2,1,0:T(2,128)} %param.18) | copy-start | bytes 294916
  0.7 5.9 %copy-start.5 = (s32[3,24]{1,0:T(4,128)S(1)}, s32[3,24]{1,0:T(4,128)}, u32[]{:S(2)}) copy-start(s32[3,24]{1,0:T(4,128)} %nodes_ref.1) | copy-start | bytes 868
  0.7 5.9 %copy-start.6 = (f32[24]{0:T(128)S(1)}, f32[24]{0:T(128)}, u32[]{:S(2)}) copy-start(f32[24]{0:T(128)} %weights_ref.1) | copy-start | bytes 292
  3.6 5.5 %collective-permute-start = (f32[96,128]{1,0:T(8,128)S(1)}, f32[96,128]{1,0:T(8,128)S(1)}, u32[]{:S(2)}, u32[]{:S(2)}) collective-permute-start(f32[96,128]{1,0:T(8,128)S(1)} %get-tuple-element.50.pieces_ref), channel_id=1, source_target_pairs={{2,0},{0,2},{3,1},{1,3},{6,4},{4,6},{7,5},{5,7},{10,8},{8,10},{11,... | collective-permute-start | bytes 147464 | tf_op jit(solution)/shard_map/ppermute | solution.py:532
  9.1 8.2 %copy-start.2 = (f32[24,128]{1,0:T(8,128)S(1)}, f32[24,128]{1,0:T(8,128)}, u32[]{:S(2)}) copy-start(f32[24,128]{1,0:T(8,128)} %dual_ref.1) | copy-start | bytes 36868
  9.1 8.2 %copy-start.3 = (f32[24,128]{1,0:T(8,128)S(1)}, f32[24,128]{1,0:T(8,128)}, u32[]{:S(2)}) copy-start(f32[24,128]{1,0:T(8,128)} %rhs_ref.3) | copy-start | bytes 36868
  9.7 4.7 %collective-permute-start.1 = (f32[40,128]{1,0:T(8,128)S(1)}, f32[40,128]{1,0:T(8,128)S(1)}, u32[]{:S(2)}, u32[]{:S(2)}) collective-permute-start(f32[40,128]{1,0:T(8,128)S(1)} %get-tuple-element.53.x_ref), channel_id=1, source_target_pairs={{0,16},{4,20},{8,24},{12,28},{16,0},{20,4},{24,8},{28,12},{1,17},{... | collective-permute-start | bytes 61448 | tf_op jit(solution)/shard_map/ppermute | solution.py:539
  14.4 4.0 %collective-permute-start.2 = (f32[80,128]{1,0:T(8,128)S(1)}, f32[80,128]{1,0:T(8,128)S(1)}, u32[]{:S(2)}, u32[]{:S(2)}) collective-permute-start(f32[80,128]{1,0:T(8,128)S(1)} %merge.6.x_ref), channel_id=1, source_target_pairs={{0,8},{4,12},{8,0},{12,4},{16,24},{20,28},{24,16},{28,20},{1,9},{5... | collective-permute-start | bytes 122888 | tf_op jit(solution)/shard_map/ppermute | solution.py:539
  16.1 1.2 %collective-permute-start.3 = (f32[24,128]{1,0:T(8,128)S(1)}, f32[24,128]{1,0:T(8,128)S(1)}, u32[]{:S(2)}, u32[]{:S(2)}) collective-permute-start(f32[24,128]{1,0:T(8,128)S(1)} %image.2.rest_0_.image_ref), channel_id=1, source_target_pairs={{0,1},{1,0},{2,3},{3,2},{4,5},{5,4},{6,7},{7,6},{8,9},{9,8},{10,11... | collective-permute-start | bytes 36872 | tf_op jit(solution)/shard_map/ppermute | solution.py:536
  18.5 4.5 %collective-permute-start.4 = (f32[160,128]{1,0:T(8,128)S(1)}, f32[160,128]{1,0:T(8,128)S(1)}, u32[]{:S(2)}, u32[]{:S(2)}) collective-permute-start(f32[160,128]{1,0:T(8,128)S(1)} %merge.7.x_ref), channel_id=1, source_target_pairs={{0,4},{4,0},{8,12},{12,8},{16,20},{20,16},{24,28},{28,24},{1,5},{5... | collective-permute-start | bytes 245768 | tf_op jit(solution)/shard_map/ppermute | solution.py:539
  20.1 4.1 %collective-permute-start.6 = (f32[96,128]{1,0:T(8,128)S(1)}, f32[96,128]{1,0:T(8,128)S(1)}, u32[]{:S(2)}, u32[]{:S(2)}) collective-permute-start(f32[96,128]{1,0:T(8,128)S(1)} %get-tuple-element.56.rest_0_.pieces_ref), channel_id=1, source_target_pairs={{2,0},{0,2},{3,1},{1,3},{6,4},{4,6},{7,5},{5,7},{10,8},{8,10},{11,... | collective-permute-start | bytes 147464 | tf_op jit(solution)/shard_map/ppermute | solution.py:532
  23.6 1.2 %collective-permute-start.5 = (f32[8,128]{1,0:T(8,128)S(1)}, f32[8,128]{1,0:T(8,128)S(1)}, u32[]{:S(2)}, u32[]{:S(2)}) collective-permute-start(f32[8,128]{1,0:T(8,128)S(1)} %get-tuple-element.60.sums_ref), channel_id=1, source_target_pairs={{0,1},{1,0},{2,3},{3,2},{4,5},{5,4},{6,7},{7,6},{8,9},{9,8},{10,11... | collective-permute-start | bytes 12296 | tf_op jit(solution)/shard_map/ppermute | solution.py:536
  25.5 4.7 %collective-permute-start.7 = (f32[24,128]{1,0:T(8,128)S(1)}, f32[24,128]{1,0:T(8,128)S(1)}, u32[]{:S(2)}, u32[]{:S(2)}) collective-permute-start(f32[24,128]{1,0:T(8,128)S(1)} %get-tuple-element.66.x_ref), channel_id=1, source_target_pairs={{0,16},{4,20},{8,24},{12,28},{16,0},{20,4},{24,8},{28,12},{1,17},{... | collective-permute-start | bytes 36872 | tf_op jit(solution)/shard_map/ppermute | solution.py:539
  30.1 3.8 %collective-permute-start.8 = (f32[48,128]{1,0:T(8,128)S(1)}, f32[48,128]{1,0:T(8,128)S(1)}, u32[]{:S(2)}, u32[]{:S(2)}) collective-permute-start(f32[48,128]{1,0:T(8,128)S(1)} %merge.9.x_ref), channel_id=1, source_target_pairs={{0,8},{4,12},{8,0},{12,4},{16,24},{20,28},{24,16},{28,20},{1,9},{5... | collective-permute-start | bytes 73736 | tf_op jit(solution)/shard_map/ppermute | solution.py:539
  34.0 4.1 %collective-permute-start.9 = (f32[96,128]{1,0:T(8,128)S(1)}, f32[96,128]{1,0:T(8,128)S(1)}, u32[]{:S(2)}, u32[]{:S(2)}) collective-permute-start(f32[96,128]{1,0:T(8,128)S(1)} %merge.10.x_ref), channel_id=1, source_target_pairs={{0,4},{4,0},{8,12},{12,8},{16,20},{20,16},{24,28},{28,24},{1,5},{5... | collective-permute-start | bytes 147464 | tf_op jit(solution)/shard_map/ppermute | solution.py:539
  35.6 3.2 %collective-permute-start.10 = (f32[24,128]{1,0:T(8,128)S(1)}, f32[24,128]{1,0:T(8,128)S(1)}, u32[]{:S(2)}, u32[]{:S(2)}) collective-permute-start(f32[24,128]{1,0:T(8,128)S(1)} %image.3.rest_0_.image_ref), channel_id=1, source_target_pairs={{0,1},{1,0},{2,3},{3,2},{4,5},{5,4},{6,7},{7,6},{8,9},{9,8},{10,11... | collective-permute-start | bytes 36872 | tf_op jit(solution)/shard_map/ppermute | solution.py:536
  38.7 1.2 %collective-permute-start.11 = (f32[8,128]{1,0:T(8,128)S(1)}, f32[8,128]{1,0:T(8,128)S(1)}, u32[]{:S(2)}, u32[]{:S(2)}) collective-permute-start(f32[8,128]{1,0:T(8,128)S(1)} %get-tuple-element.75.sums_ref), channel_id=1, source_target_pairs={{0,1},{1,0},{2,3},{3,2},{4,5},{5,4},{6,7},{7,6},{8,9},{9,8},{10,11... | collective-permute-start | bytes 12296 | tf_op jit(solution)/shard_map/ppermute | solution.py:536

commit v4 on v3

--- a/solution.py
+++ b/solution.py
@@ -106,15 +106,19 @@
     write_pieces(lp_ref, dual, out_ref, S, J, NZ)
 
 
+def down(row, count):
+    return jnp.transpose(jnp.broadcast_to(row, (BLK, row.shape[1])))[:count]
+
+
 def setup_kernel(
     S,
     J,
     R,
     NZ,
     HB,
-    cols_ref,
     nodes_ref,
     weights_ref,
+    cols_ref,
     primal_ref,
     cost_ref,
     mult_ref,
@@ -128,12 +132,13 @@
     an_ref,
     id_ref,
     wb_ref,
+    same_ref,
+    table_ref,
     idx_sc,
     pp_sc,
     pc_sc,
     hp_sc,
     hc_sc,
-    table_ref,
     table_sem,
 ):
     K, Q = R * NZ, J * S
@@ -141,62 +146,68 @@
     table_copy.start()
     section = lax.axis_index("section")
     rows = primal_ref.shape[1]
+
+    cols = cols_ref[...]
+    section_of = lax.rem(lax.broadcasted_iota(jnp.int32, (K * J, BLK), 0) // NZ, J)
+    tiles = -(-rows // BLK)
+    lane = lax.broadcasted_iota(jnp.int32, (K * J, BLK), 1)
+    picks = []
     for s in range(S):
-        for j in range(J):
-            for k in range(K):
-                c = cols_ref[k // NZ, j, k % NZ, s]
-                idx_sc[pl.ds((s * K + k) * J + j, 1), :] = jnp.full(
-                    (1, BLK), c * J + j, jnp.int32
-                )
-    nodes_of = []
+        want = jnp.broadcast_to(cols[:, s : s + 1], (K * J, BLK))
+        idx_sc[pl.ds(s * K * J, K * J), :] = want.astype(F32)
+        want = want * J + section_of
+        picks.append(
+            jnp.concatenate(
+                [(want == lane + t * BLK).astype(F32).astype(BF16) for t in range(tiles)], axis=1
+            )[:, :rows]
+        )
+
+    def gather(source_ref, placed_ref, hedged_ref):
+        for s in range(S):
+            placed_ref[pl.ds(s * K * J, K * J), :] = jnp.dot(
+                picks[s], source_ref[s], preferred_element_type=F32
+            )
+            hedged_ref[pl.ds(s * HB * J, HB * J), :] = source_ref[s, : HB * J, :].astype(F32)
+
+    def placed_rows(k, j):
+        return pl.ds(((k // NZ) * J + j) * NZ + k % NZ, S, stride=K * J), pl.ds(k * Q + j * S, S)
+
+    def hedged_rows(h, j):
+        return pl.ds(h * J + j, S, stride=HB * J), pl.ds(h * Q + j * S, S)
+
+    gather(primal_ref, pp_sc, hp_sc)
+    gather(cost_ref, pc_sc, hc_sc)
+    weights = down(weights_ref[...], S)
+    ids, picked = [], []
     for j in range(J):
         g = section * J + j
-        level = jnp.maximum(g - 1, 0)
-        off = jnp.where(g == 0, 0, jnp.where(g == 1, 1, jnp.where(g == 2, 1 + N1, 1 + N1 + N2)))
-        keep = jnp.where(g == 0, 0, 1)
-        for s in range(S):
-            node = nodes_ref[level, s] * keep + off
-            q = j * S + s
-            id_ref[pl.ds(q, 1), :] = jnp.full((1, BLK), node, jnp.int32).astype(F32)
-            wb_ref[pl.ds(q, 1), :] = jnp.full((1, BLK), weights_ref[s], F32)
-            nodes_of.append(node)
-    tiles = -(-rows // BLK)
-    lane = lax.broadcasted_iota(jnp.int32, (K * J, BLK), 1)
-
-    def gather(source_ref, placed_ref, hedged_ref):
-        for s in range(S):
-            want = idx_sc[pl.ds(s * K * J, K * J), :]
-            pick = jnp.concatenate(
-                [(want == lane + t * BLK).astype(F32).astype(BF16) for t in range(tiles)], axis=1
-            )[:, :rows]
-            placed_ref[pl.ds(s * K * J, K * J), :] = jnp.dot(
-                pick, source_ref[s], preferred_element_type=F32
-            )
-            hedged_ref[pl.ds(s * HB * J, HB * J), :] = source_ref[s, : HB * J, :].astype(F32)
-
-    gather(primal_ref, pp_sc, hp_sc)
+        own = jnp.zeros((1, nodes_ref.shape[1]), jnp.int32)
+        for level, off in enumerate((1, 1 + N1, 1 + N1 + N2)):
+            own = jnp.where(g == level + 1, nodes_ref[level : level + 1, :] + off, own)
+        ids.append(down(own.astype(F32), S))
+        picked.append(own)
+        wb_ref[pl.ds(j * S, S), :] = weights
+    ids = jnp.concatenate(ids, axis=0)
+    id_ref[...] = ids
+    across = jnp.transpose(ids)[0:1, :Q]
+    same_ref[:, :Q] = (jnp.broadcast_to(ids[:, :1], (Q, Q)) == across).astype(F32)
     for j in range(J):
         for k in range(K):
-            src, dst = pl.ds(k * J + j, S, stride=K * J), pl.ds(k * Q + j * S, S)
+            src, dst = placed_rows(k, j)
             pp_ref[dst, :] = pp_sc[src, :]
-            cb_ref[dst, :] = (idx_sc[src, :] - j).astype(F32)
+            pc_ref[dst, :] = pc_sc[src, :]
+            cb_ref[dst, :] = idx_sc[src, :]
         for h in range(HB):
-            src, dst = pl.ds(h * J + j, S, stride=HB * J), pl.ds(h * Q + j * S, S)
+            src, dst = hedged_rows(h, j)
             hp_ref[dst, :] = hp_sc[src, :]
+            hc_ref[dst, :] = hc_sc[src, :]
             ml_ref[dst, :] = mult_ref[src, :]
-    gather(cost_ref, pc_sc, hc_sc)
+    table_copy.wait()
     for j in range(J):
-        for k in range(K):
-            src, dst = pl.ds(k * J + j, S, stride=K * J), pl.ds(k * Q + j * S, S)
-            pc_ref[dst, :] = pc_sc[src, :]
-        for h in range(HB):
-            src, dst = pl.ds(h * J + j, S, stride=HB * J), pl.ds(h * Q + j * S, S)
-            hc_ref[dst, :] = hc_sc[src, :]
-    table_copy.wait()
-    for q, node in enumerate(nodes_of):
-        line = table_ref[pl.ds(node, 1), :]
-        for h in range(HB):
-            an_ref[pl.ds(h * Q + q, 1), :] = line[:, h * BLK : (h + 1) * BLK]
+        for s in range(S):
+            line = table_ref[pl.ds(picked[j][0, s], 1), :]
+            for h in range(HB):
+                an_ref[pl.ds(h * Q + j * S + s, 1), :] = line[:, h * BLK : (h + 1) * BLK]
 
 
 def total(x):
@@ -221,14 +232,14 @@
             term = parts[m] if m == k else jnp.where(cols[m] == cols[k], parts[m], 0.0)
             add = term if add is None else add + term
         for h in range(HB):
-            add = add + jnp.where(cols[k] == float(h * J), hedge[h], 0.0)
+            add = add + jnp.where(cols[k] == float(h), hedge[h], 0.0)
         placed.append(
             jnp.maximum(slot(p_ref, k) - TAU_STEP * (slot(pc_ref, k) + add), 0.0)
         )
     for h in range(HB):
         add = None
         for m in range(K):
-            term = jnp.where(cols[m] == float(h * J), parts[m], 0.0)
+            term = jnp.where(cols[m] == float(h), parts[m], 0.0)
             add = term if add is None else add + term
         add = add + hedge[h]
         hedged.append(jnp.maximum(slot(h_ref, h) - TAU_STEP * (slot(hc_ref, h) + add), 0.0))
@@ -236,7 +247,7 @@
 
 
 def finish_step(
-    S, J, R, NZ, HB, own, p_ref, placed, hedged, anchors, with_anchors, ids, wb, p_out, h_out, mu_ref, send_ref, step_ref
+    S, J, R, NZ, HB, own, p_ref, placed, hedged, anchors, ids, wb, same, p_out, h_out, mu_ref, send_ref, step_ref
 ):
     K, Q = R * NZ, J * S
     for k in range(K):
@@ -245,10 +256,8 @@
     step_ref[...] = 2.0 * p_out[mine, :] - p_ref[mine, :]
     for h in range(HB):
         h_out[h * Q : (h + 1) * Q, :] = hedged[h]
-    across = jnp.transpose(ids)[0:1, :Q]
-    same = (jnp.broadcast_to(ids[:, :1], (Q, Q)) == across).astype(F32)
     sums = jnp.dot(
-        same,
+        same[:, :Q],
         jnp.concatenate([wb * x for x in hedged] + [wb], axis=1),
         precision=HIGHEST,
         preferred_element_type=F32,
@@ -283,13 +292,7 @@
             note = jnp.where(lane == 2 * J + e, weight, note)
     note = jnp.where(lane == 4 * J, total(gap), note)
     note = jnp.where(lane == 4 * J + 1, total(drift), note)
-    if with_anchors:
-        for j in range(J):
-            for f in range(2):
-                at = j * S + (S - 1) * f
-                for h in range(HB):
-                    send_ref[pl.ds(2 * J * HB + 1 + (f * J + j) * HB + h, 1), :] = anchors[h][at : at + 1]
-    at = 2 * J * HB * (2 if with_anchors else 1)
+    at = 2 * J * HB
     send_ref[pl.ds(2 * J * HB, 1), :] = note
     send_ref[pl.ds(at + 1, send_ref.shape[0] - at - 1), :] = jnp.zeros(
         (send_ref.shape[0] - at - 1, BLK), F32
@@ -297,7 +300,7 @@
 
 
 def first_kernel(
-    S, J, R, NZ, HB, pp_ref, pc_ref, hp_ref, hc_ref, cb_ref, ml_ref, an_ref, id_ref, wb_ref, pieces_ref, *rest
+    S, J, R, NZ, HB, pp_ref, pc_ref, hp_ref, hc_ref, cb_ref, ml_ref, an_ref, id_ref, wb_ref, same_ref, pieces_ref, *rest
 ):
     other_refs = rest[: R - 1]
     p_out, h_out, mu_ref, send_ref, step_ref, all_sc = rest[R - 1 :]
@@ -312,20 +315,19 @@
         S, J, R, NZ, HB, own, pieces_ref, other_refs, pp_ref, pc_ref, hp_ref, hc_ref, cb_ref, hedge, all_sc
     )
     finish_step(
-        S, J, R, NZ, HB, own, pp_ref, placed, hedged, anchors, True, id_ref[...], wb_ref[...], p_out, h_out, mu_ref, send_ref, step_ref
+        S, J, R, NZ, HB, own, pp_ref, placed, hedged, anchors, id_ref[...], wb_ref[...], same_ref[...], p_out, h_out, mu_ref, send_ref, step_ref
     )
 
 
 def read_nodes(J, HB, got_ref, ids, devices):
-    step = got_ref.shape[0] // devices
     E = 2 * J
     sums = [
         jnp.concatenate(
-            [got_ref[pl.ds(e * HB + h, devices, stride=step), :] for e in range(E)], axis=0
+            [got_ref[pl.ds(e * HB + h, devices, stride=E * HB), :] for e in range(E)], axis=0
         )
         for h in range(HB)
     ]
-    notes = got_ref[pl.ds(E * HB, devices, stride=step), :]
+    notes = got_ref[pl.ds(E * HB * devices, devices), :]
     wide = lambda at: jnp.broadcast_to(notes[:, at : at + 1], (devices, BLK))
     names = jnp.concatenate([wide(e) for e in range(E)], axis=0)
     weight = jnp.concatenate([wide(E + e) for e in range(E)], axis=0)
@@ -348,22 +350,12 @@
     own_safe = jnp.where(weight > 0, weight, 1.0)
     gap = total(notes[:, 2 * E : 2 * E + 1])
     drift = total(notes[:, 2 * E + 1 : 2 * E + 2])
-    before = [
-        jnp.concatenate(
-            [
-                got_ref[pl.ds(E * HB + 1 + e * HB + h, devices, stride=step), :]
-                for e in range(E)
-            ],
-            axis=0,
-        )
-        for h in range(HB)
-    ] if step > 2 * E * HB else None
     rows = ids.shape[0]
     spread = jnp.zeros((count, BLK), F32)
     for h in range(HB):
         spread = spread + weight * (sums[h] / own_safe - means[h][rows:]) ** 2
     gap = gap + total(spread)
-    return positive[:rows], [m[:rows] for m in means], [m[rows:] for m in means], before, weight, gap, drift
+    return positive[:rows], [m[:rows] for m in means], [m[rows:] for m in means], weight, gap, drift
 
 
 def moved(weight, means, before):
@@ -386,23 +378,28 @@
 
 
 def nodes_kernel(
-    S, J, HB, devices, got_ref, id_ref, mu_ref, h_ref, ml_ref, an_out, ml_out, ent_ref, sums_ref
-):
-    Q = J * S
-    shared, means, entry_means, before, weight, gap, drift = read_nodes(
+    S, J, HB, devices, got_ref, id_ref, mu_ref, h_ref, ml_ref, table_ref, an_out, ml_out, ent_ref, sums_ref, old_sc
+):
+    Q, E = J * S, 2 * J
+    names = jnp.maximum(got_ref[pl.ds(E * HB * devices, devices), :], 0.0).astype(jnp.int32)
+    shared, means, entry_means, weight, gap, drift = read_nodes(
         J, HB, got_ref, id_ref[...], devices
     )
-    put_sums(gap, drift + moved(weight, entry_means, before), sums_ref)
     for h in range(HB):
         at = pl.ds(h * Q, Q)
         ent_ref[h] = entry_means[h]
         anchor = jnp.where(shared, means[h], mu_ref[at, :])
         an_out[at, :] = anchor
         ml_out[at, :] = ml_ref[at, :] + RHO_START * (h_ref[at, :] - anchor)
+    for e in range(E):
+        for d in range(devices):
+            old_sc[pl.ds(e * devices + d, 1), :] = table_ref[pl.ds(names[d, e], 1), :]
+    before = [old_sc[:, h * BLK : (h + 1) * BLK] for h in range(HB)]
+    put_sums(gap, drift + moved(weight, entry_means, before), sums_ref)
 
 
 def second_kernel(
-    S, J, R, NZ, HB, pp_ref, pc_ref, hp_ref, hc_ref, cb_ref, ml_ref, an_ref, id_ref, wb_ref, sums_ref, sums2_ref, pieces_ref, *rest
+    S, J, R, NZ, HB, pp_ref, pc_ref, hp_ref, hc_ref, cb_ref, ml_ref, an_ref, id_ref, wb_ref, same_ref, sums_ref, sums2_ref, pieces_ref, *rest
 ):
     other_refs = rest[: R - 1]
     p_out, h_out, mu_out, send_ref, step_ref, pen_ref, all_sc = rest[R - 1 :]
@@ -417,7 +414,7 @@
         S, J, R, NZ, HB, own, pieces_ref, other_refs, pp_ref, pc_ref, hp_ref, hc_ref, cb_ref, hedge, all_sc
     )
     finish_step(
-        S, J, R, NZ, HB, own, pp_ref, placed, hedged, anchors, False, id_ref[...], wb_ref[...], p_out, h_out, mu_out, send_ref, step_ref
+        S, J, R, NZ, HB, own, pp_ref, placed, hedged, anchors, id_ref[...], wb_ref[...], same_ref[...], p_out, h_out, mu_out, send_ref, step_ref
     )
 
 
@@ -425,7 +422,7 @@
     S, J, HB, devices, got_ref, id_ref, ent_ref, mu_ref, h_ref, ml_ref, pen_ref, ml_out, sums_ref
 ):
     Q = J * S
-    shared, means, entry_means, before, weight, gap, drift = read_nodes(
+    shared, means, entry_means, weight, gap, drift = read_nodes(
         J, HB, got_ref, id_ref[...], devices
     )
     drift = drift + moved(weight, entry_means, [ent_ref[h] for h in range(HB)])
@@ -484,12 +481,17 @@
         copy.wait()
 
 
-def merge_kernel(apart, x_ref, y_ref, *rest):
+def merge_kernel(apart, count, sums, x_ref, y_ref, *rest):
     out_ref = rest[-1]
-    rows = x_ref.shape[0]
+    rows = count * sums
     high = lax.rem(lax.axis_index("scen") // apart, 2)
-    out_ref[pl.ds(pl.multiple_of(high * rows, 8), rows), :] = x_ref[...]
-    out_ref[pl.ds(pl.multiple_of((1 - high) * rows, 8), rows), :] = y_ref[...]
+    for place, ref in ((high, x_ref), (1 - high, y_ref)):
+        out_ref[pl.ds(pl.multiple_of(place * rows, 8), rows), :] = ref[:rows, :]
+        for i in range(count):
+            out_ref[pl.ds(2 * rows + place * count + i, 1), :] = ref[rows + i : rows + i + 1, :]
+    used = 2 * rows + 2 * count
+    if out_ref.shape[0] > used:
+        out_ref[used:, :] = jnp.zeros((out_ref.shape[0] - used, BLK), F32)
 
 
 def local(
@@ -513,7 +515,6 @@
     K, Q = R * NZ, J * S
     devices = scens
     message = -(-(2 * J * HB + 1) // 8) * 8
-    message1 = -(-(4 * J * HB + 1) // 8) * 8
     static = (S, J, R, NZ, HB)
 
     def interleave(x):
@@ -538,23 +539,23 @@
     def partner(x, apart):
         return lax.ppermute(x, "scen", [(i, i ^ apart) for i in range(scens)])
 
-    def merge(x, y, apart, *after):
+    def merge(x, y, apart, count, least, *after):
+        rows = max(least, 2 * count * (2 * J * HB) + -(-2 * count // 8) * 8)
         return pl.pallas_call(
-            functools.partial(merge_kernel, apart),
-            out_shape=near(2 * x.shape[0], BLK),
+            functools.partial(merge_kernel, apart, count, 2 * J * HB),
+            out_shape=near(rows, BLK),
             in_specs=[VMEM] * 2 + [HBM if far else VMEM for far, _ in after],
             out_specs=VMEM,
             compiler_params=params(4),
             name="merge",
         )(x, y, *[in_hbm(z) if far else z for far, z in after])
 
-    def exchange(x, *work):
-        if scens & (scens - 1):
-            return lax.all_gather(x, "scen", axis=0, tiled=True)
+    def exchange(x, least, *work):
+        assert scens & (scens - 1) == 0
         apart, turn = scens // 2, 0
         while apart:
             y = partner(x, apart)
-            x = merge(x, y, apart, *(work[turn]() if turn < len(work) else ()))
+            x = merge(x, y, apart, 1 << turn, least if apart == 2 else 0, *(work[turn]() if turn < len(work) else ()))
             apart, turn = apart // 2, turn + 1
         return x
 
@@ -578,23 +579,30 @@
     )(lp, in_hbm(dual_start), primal)
     others = from_rows(pieces)
 
-    pp, pc, hp, hc, cb, ml, an, ids, wb = pl.pallas_call(
+    pp, pc, hp, hc, cb, ml, an, ids, wb, same, table = pl.pallas_call(
         functools.partial(setup_kernel, *static),
         out_shape=[near(K * Q, BLK)] * 2
         + [near(HB * Q, BLK)] * 2
         + [near(K * Q, BLK)]
         + [near(HB * Q, BLK)] * 2
-        + [near(Q, BLK)] * 2,
-        in_specs=[SMEM] * 3 + [VMEM] * 3 + [HBM],
-        out_specs=[VMEM] * 9,
-        scratch_shapes=[pltpu.VMEM((S * K * J, BLK), jnp.int32)]
-        + [pltpu.VMEM((S * K * J, BLK), F32)] * 2
+        + [near(Q, BLK)] * 3
+        + [near_like(consensus_start)],
+        in_specs=[VMEM] * 6 + [HBM],
+        out_specs=[VMEM] * 11,
+        scratch_shapes=[pltpu.VMEM((S * K * J, BLK), F32)] * 3
         + [pltpu.VMEM((S * HB * J, BLK), F32)] * 2
-        + [pltpu.VMEM(consensus_start.shape, F32)]
         + [pltpu.SemaphoreType.DMA],
         compiler_params=params(16),
         name="setup",
-    )(columns_of, scenario_nodes, scenario_weights, in_vmem(primal), price, mult, in_hbm(consensus_start))
+    )(
+        scenario_nodes,
+        scenario_weights.reshape(1, S),
+        columns_of.reshape(K * J, S),
+        in_vmem(primal),
+        price,
+        mult,
+        in_hbm(consensus_start),
+    )
     primal = in_vmem(primal)
 
     def step_out(rows):
@@ -619,13 +627,13 @@
     scratch = [pltpu.VMEM((K * Q, BLK), F32)]
     p1, h1, mu1, send1, step1 = pl.pallas_call(
         functools.partial(first_kernel, *static),
-        out_shape=step_out(message1),
-        in_specs=[VMEM] * (10 + R - 1),
+        out_shape=step_out(message),
+        in_specs=[VMEM] * (11 + R - 1),
         out_specs=[VMEM] * 5,
         scratch_shapes=scratch,
         compiler_params=params(8),
         name="first",
-    )(pp, pc, hp, hc, cb, ml, an, ids, wb, pieces, *others)
+    )(pp, pc, hp, hc, cb, ml, an, ids, wb, same, pieces, *others)
     made = {}
 
     def image_work():
@@ -633,6 +641,14 @@
         return ((False, made["image"]),)
 
     def dual_work():
+        made["bulk"] = pl.pallas_call(
+            functools.partial(bulk_kernel, S),
+            out_shape=near(S, C * J, BLK),
+            in_specs=[VMEM] * 2,
+            out_specs=VMEM,
+            compiler_params=params(8),
+            name="bulk",
+        )(primal, price)
         made["dual"], made["pieces"] = pl.pallas_call(
             functools.partial(dual_kernel, S, J, NZ),
             out_shape=[near(S, BLK), near(NZ * Q, BLK)],
@@ -641,42 +657,34 @@
             compiler_params=params(8),
             name="dual",
         )(lp, dual_start, bounds_rhs, made["image"], from_section(made["image"]))
-        return ((False, made["pieces"]),)
-
-    def bulk_work():
-        made["bulk"] = pl.pallas_call(
-            functools.partial(bulk_kernel, S),
-            out_shape=near(S, C * J, BLK),
-            in_specs=[VMEM] * 2,
-            out_specs=VMEM,
-            compiler_params=params(8),
-            name="bulk",
-        )(primal, price)
-        return ((False, made["bulk"]),)
-
-    got1 = exchange(send1, image_work, dual_work, bulk_work)
+        return ((False, made["pieces"]), (False, made["bulk"]))
+
+    got1 = exchange(send1, NZ * Q, image_work, dual_work)
     dual1, pieces2 = made["dual"], made["pieces"]
     others2 = from_rows(pieces2)
 
     an1, ml1, ent1, sums1 = pl.pallas_call(
         functools.partial(nodes_kernel, S, J, HB, devices),
         out_shape=[near(HB * Q, BLK)] * 2 + [near(HB, 2 * J * devices, BLK), near(8, BLK)],
-        in_specs=[VMEM] * 5,
+        in_specs=[VMEM] * 6,
         out_specs=[VMEM] * 4,
+        scratch_shapes=[
+            pltpu.VMEM((2 * J * devices, hedged), F32),
+        ],
         compiler_params=params(8),
         name="nodes",
-    )(got1, ids, mu1, h1, ml)
+    )(got1, ids, mu1, h1, ml, table)
     sums1b = from_section(sums1)
 
     p2, h2, mu2, send2, step2, pen1 = pl.pallas_call(
         functools.partial(second_kernel, *static),
         out_shape=step_out(message) + [near(8, BLK)],
-        in_specs=[VMEM] * (12 + R - 1),
+        in_specs=[VMEM] * (13 + R - 1),
         out_specs=[VMEM] * 6,
         scratch_shapes=scratch,
         compiler_params=params(8),
         name="second",
-    )(p1, pc, h1, hc, cb, ml1, an1, ids, wb, sums1, sums1b, pieces2, *others2)
+    )(p1, pc, h1, hc, cb, ml1, an1, ids, wb, same, sums1, sums1b, pieces2, *others2)
     half = S // 2
 
     def place(first, count, whole, *into):
@@ -704,7 +712,7 @@
         made["bulk"], made["out"] = place(half, S - half, made["bulk"], made["out"])
         return ((True, made["out"]),)
 
-    got2 = exchange(send2, last_image_work, place_work, rest_work)
+    got2 = exchange(send2, 0, last_image_work, place_work, rest_work)
     out, image2 = made["out"], made["image"]
     ml2, sums2 = pl.pallas_call(
         functools.partial(last_kernel, S, J, HB, devices),

time: 40.7 us -> 40.1 us (0.985)
  waiting for transfers between devices: 4.6 us -> 3.34 us
  starting transfers between devices: 16.6 us -> 17.6 us
    ppermute x4, waiting for transfers between devices: 2.28 us -> 0.95 us  [from_section(): lax.ppermute(x, 'section', [(i, (i + 1) % sections) for i in range(sectio...]
    ppermute x6, starting transfers between devices: 12 us -> 12.8 us  [partner(): return lax.ppermute(x, 'scen', [(i, i ^ apart) for i in range(scens)])]
    pallas_call x1, Pallas kernels: 2.46 us -> 2.04 us  [local(): pl.pallas_call(functools.partial(setup_kernel, *static), out_shape=[near(...]
  transfers between devices with their start and end apart: 12 -> 12, of which waited for: 10 -> 8; matrix products, arithmetic and copies ran while one was open for 0% -> 0% of each run, Pallas kernels for 34% -> 34%
where the time goes in v4:
time: 40.1 us; the launch traced here: 39.9 us
  Pallas kernels  18.2 us (45%)
  starting transfers between devices  17.6 us (44%)
  waiting for transfers between devices  3.34 us (8%)
  between operations  0.82 us (2%)
    ppermute x6, starting transfers between devices, partner(): return lax.ppermute(x, 'scen', [(i, i ^ apart) for i in range(scens)])  12.8 us
    ppermute x2, starting transfers between devices, from_rows(): lax.ppermute(x, 'rows', [((i + q) % R, i) for i in range(R)])  4.5 us
    pallas_call x2, Pallas kernels, place(): pl.pallas_call(functools.partial(place_kernel, *static, first, count, cut...  3.99 us
    pallas_call x2, Pallas kernels, image_of(): pl.pallas_call(functools.partial(image_kernel, S, J, NZ), out_shape=near(...  3.46 us
    pallas_call x1, Pallas kernels, local(): pl.pallas_call(functools.partial(pieces_kernel, S, J, NZ), out_shape=[nea...  2.9 us
    pallas_call x1, Pallas kernels, local(): pl.pallas_call(functools.partial(setup_kernel, *static), out_shape=[near(...  2.04 us
    ppermute x6, waiting for transfers between devices, partner(): return lax.ppermute(x, 'scen', [(i, i ^ apart) for i in range(scens)])  1.66 us
    pallas_call x1, Pallas kernels, dual_work(): pl.pallas_call(functools.partial(bulk_kernel, S), out_shape=near(S, C * J...  0.98 us
  transfers between devices with their start and end apart: 12, of which 8 were waited for; matrix products, arithmetic and copies ran while one was open for 0% of the time, Pallas kernels for 34%

profile of v4, /device:TPU:0, one launch (start us, length us, event | category | flops | bytes accessed | tf_op | source)
XLA Modules:
  0.0 39.9 jit_solution(17794590866719510210)
XLA Ops:
  0.7 2.9 %pieces.1 = (f32[96,128]{1,0:T(8,128)S(1)}, bf16[24,4,128,128]{3,2,1,0:T(8,128)(2,1)S(1)}, bf16[24,352,128]{2,1,0:T(8,128)(2,1)S(1)}) custom-call(bf16[24,4,128,128]{3,2,1,0:T(8,128)(2,1)} %bitcast.39, f32[24,128]{1,0:T(8,128)} %dual_ref.1, bf16[24,352,128]{2,1,0:T(8,128)(2,1)} %bitcast.40), custom_call_target="tpu_custom_call" | custom-call | tf_op jit(solution)/shard_map/pieces/pallas_call | solution.py:566
  3.6 3.0 %collective-permute-start = (f32[96,128]{1,0:T(8,128)S(1)}, f32[96,128]{1,0:T(8,128)S(1)}, u32[]{:S(2)}, u32[]{:S(2)}) collective-permute-start(f32[96,128]{1,0:T(8,128)S(1)} %get-tuple-element.53.pieces_ref), channel_id=1, source_target_pairs={{2,0},{0,2},{3,1},{1,3},{6,4},{4,6},{7,5},{5,7},{10,8},{8,10},{11,... | collective-permute-start | bytes 147464 | tf_op jit(solution)/shard_map/ppermute | solution.py:533
  6.6 2.0 %setup.1 = (f32[192,128]{1,0:T(8,128)S(1)}, f32[192,128]{1,0:T(8,128)S(1)}, f32[192,128]{1,0:T(8,128)S(1)}, f32[192,128]{1,0:T(8,128)S(1)}, f32[192,128]{1,0:T(8...) custom-call(s32[3,24]{1,0:T(4,128)S(1)} %copy-done.5, ...), custom_call_target="tpu_custom_call" | custom-call | tf_op jit(solution)/shard_map/setup/pallas_call | solution.py:582
  8.7 0.6 %first.1 = (f32[192,128]{1,0:T(8,128)S(1)}, f32[192,128]{1,0:T(8,128)S(1)}, f32[192,128]{1,0:T(8,128)S(1)}, f32[24,128]{1,0:T(8,128)S(1)}, f32[96,128]{1,0:T(8,128)S(1)}) custom-call(f32[192,128]{1,0:T(8,128)S(1)} %get-tuple-element.43.pp_ref, f32[192,128]{1,0:T(8,128)S(1)} %get-tuple-element.44.pc_ref, f32[192,128]{1,0:T(8,128)S(1)} %get-tuple-element.45.hp_ref, ...), custom_call_target="tpu_custom_call" | custom-call | tf_op jit(solution)/shard_map/first/pallas_call | solution.py:628
  9.3 3.2 %collective-permute-start.1 = (f32[24,128]{1,0:T(8,128)S(1)}, f32[24,128]{1,0:T(8,128)S(1)}, u32[]{:S(2)}, u32[]{:S(2)}) collective-permute-start(f32[24,128]{1,0:T(8,128)S(1)} %get-tuple-element.56.x_ref), channel_id=1, source_target_pairs={{0,16},{4,20},{8,24},{12,28},{16,0},{20,4},{24,8},{28,12},{1,17},{... | collective-permute-start | bytes 36872 | tf_op jit(solution)/shard_map/ppermute | solution.py:540
  12.4 1.7 %image.2.rest_0_.image_ref = f32[24,128]{1,0:T(8,128)S(1)} custom-call(bf16[24,4,128,128]{3,2,1,0:T(8,128)(2,1)S(1)} %get-tuple-element.57.lp_ref, f32[96,128]{1,0:T(8,128)S(1)} %get-tuple-element.58.step_ref), custom_call_target="tpu_custom_call" | custom-call | tf_op jit(solution)/shard_map/image/pallas_call | solution.py:618
  14.2 1.9 %collective-permute-start.2 = (f32[40,128]{1,0:T(8,128)S(1)}, f32[40,128]{1,0:T(8,128)S(1)}, u32[]{:S(2)}, u32[]{:S(2)}) collective-permute-start(f32[40,128]{1,0:T(8,128)S(1)} %merge.6.x_ref), channel_id=1, source_target_pairs={{0,8},{4,12},{8,0},{12,4},{16,24},{20,28},{24,16},{28,20},{1,9},{5... | collective-permute-start | bytes 61448 | tf_op jit(solution)/shard_map/ppermute | solution.py:540
  16.1 1.0 %bulk.1.rest_1_.bulk_ref = f32[24,352,128]{2,1,0:T(8,128)S(1)} custom-call(bf16[24,352,128]{2,1,0:T(8,128)(2,1)S(1)} %get-tuple-element.42.primal_ref, bf16[24,352,128]{2,1,0:T(8,128)(2,1)S(1)} %bitcast.32), custom_call_target="tpu_custom_call" | custom-call | tf_op jit(solution)/shard_map/bulk/pallas_call | solution.py:644
  17.1 0.2 collective-permute-done.3.image2_ref
  17.3 0.9 %dual.1 = (f32[24,128]{1,0:T(8,128)S(1)}, f32[96,128]{1,0:T(8,128)S(1)}) custom-call(bf16[24,4,128,128]{3,2,1,0:T(8,128)(2,1)S(1)} %get-tuple-element.57.lp_ref, f32[24,128]{1,0:T(8,128)S(1)} %copy-done.2, f32[24,128]{1,0:T(8,128)S(1)} %copy-done.3, f32[24,128]{1,0:T(8,128)S(1)} %image.2.rest_0_.image_ref, f32[24,128]{1,0:T(8,128)S(1)} %collective-permute-done.3.image2_ref), custom_call_target="tpu_custom_call" | custom-call | tf_op jit(solution)/shard_map/dual/pallas_call | solution.py:652
  18.2 1.7 %collective-permute-start.4 = (f32[96,128]{1,0:T(8,128)S(1)}, f32[96,128]{1,0:T(8,128)S(1)}, u32[]{:S(2)}, u32[]{:S(2)}) collective-permute-start(f32[96,128]{1,0:T(8,128)S(1)} %merge.7.x_ref), channel_id=1, source_target_pairs={{0,4},{4,0},{8,12},{12,8},{16,20},{20,16},{24,28},{28,24},{1,5},{5... | collective-permute-start | bytes 147464 | tf_op jit(solution)/shard_map/ppermute | solution.py:540
  19.9 1.5 %collective-permute-start.6 = (f32[96,128]{1,0:T(8,128)S(1)}, f32[96,128]{1,0:T(8,128)S(1)}, u32[]{:S(2)}, u32[]{:S(2)}) collective-permute-start(f32[96,128]{1,0:T(8,128)S(1)} %get-tuple-element.59.rest_0_.pieces_ref), channel_id=1, source_target_pairs={{2,0},{0,2},{3,1},{1,3},{6,4},{4,6},{7,5},{5,7},{10,8},{8,10},{11,... | collective-permute-start | bytes 147464 | tf_op jit(solution)/shard_map/ppermute | solution.py:533
  21.4 1.0 %collective-permute-done.4.y_ref = f32[96,128]{1,0:T(8,128)S(1)} collective-permute-done((f32[96,128]{1,0:T(8,128)S(1)}, f32[96,128]{1,0:T(8,128)S(1)}, u32[]{:S(2)}, u32[]{:S(2)}) %collective-permute-start.4) | collective-permute-done | bytes 49184 | tf_op jit(solution)/shard_map/ppermute | solution.py:540
  22.4 0.8 %nodes.1 = (f32[192,128]{1,0:T(8,128)S(1)}, f32[192,128]{1,0:T(8,128)S(1)}, f32[4,32,128]{2,1,0:T(8,128)S(1)}, f32[8,128]{1,0:T(8,128)S(1)}) custom-call(f32[136,128]{1,0:T(8,128)S(1)} %merge.8.got_ref, f32[48,128]{1,0:T(8,128)S(1)} %get-tuple-element.50.id_ref, f32[192,128]{1,0:T(8,128)S(1)} %get-tuple-element.60.mu_ref, ...), custom_call_target="tpu_custom_call" | custom-call | tf_op jit(solution)/shard_map/nodes/pallas_call | solution.py:666
  23.2 0.1 collective-permute-start.5
  23.2 0.7 %collective-permute-done.6.rest_0_ = f32[96,128]{1,0:T(8,128)S(1)} collective-permute-done((f32[96,128]{1,0:T(8,128)S(1)}, f32[96,128]{1,0:T(8,128)S(1)}, u32[]{:S(2)}, u32[]{:S(2)}) %collective-permute-start.6) | collective-permute-done | bytes 49184 | tf_op jit(solution)/shard_map/ppermute | solution.py:533
  24.0 0.4 %collective-permute-done.5.sums2_ref = f32[8,128]{1,0:T(8,128)S(1)} collective-permute-done((f32[8,128]{1,0:T(8,128)S(1)}, f32[8,128]{1,0:T(8,128)S(1)}, u32[]{:S(2)}, u32[]{:S(2)}) %collective-permute-start.5) | collective-permute-done | bytes 4128 | tf_op jit(solution)/shard_map/ppermute | solution.py:537
  24.4 0.6 %second.1 = (f32[192,128]{1,0:T(8,128)S(1)}, f32[192,128]{1,0:T(8,128)S(1)}, f32[192,128]{1,0:T(8,128)S(1)}, f32[24,128]{1,0:T(8,128)S(1)}, f32[96,128]{1,0:T(8,128)S(1)}, /*index=5*/f32[8,128]{1,0:T(8,128)S(1)}) custom-call(f32[192,128]{1,0:T(8,128)S(1)} %get-tuple-element.54.pp_ref, f32[192,128]{1,0:T(8,128)S(1)} %get-tuple-element.44.pc_ref, ...), custom_call_target="tpu_custom_call" | custom-call | tf_op jit(solution)/shard_map/second/pallas_call | solution.py:679
  25.0 2.7 %collective-permute-start.7 = (f32[24,128]{1,0:T(8,128)S(1)}, f32[24,128]{1,0:T(8,128)S(1)}, u32[]{:S(2)}, u32[]{:S(2)}) collective-permute-start(f32[24,128]{1,0:T(8,128)S(1)} %get-tuple-element.70.x_ref), channel_id=1, source_target_pairs={{0,16},{4,20},{8,24},{12,28},{16,0},{20,4},{24,8},{28,12},{1,17},{... | collective-permute-start | bytes 36872 | tf_op jit(solution)/shard_map/ppermute | solution.py:540
  27.7 1.7 %image.3.rest_0_.image_ref = f32[24,128]{1,0:T(8,128)S(1)} custom-call(bf16[24,4,128,128]{3,2,1,0:T(8,128)(2,1)S(1)} %get-tuple-element.57.lp_ref, f32[96,128]{1,0:T(8,128)S(1)} %get-tuple-element.71.step_ref), custom_call_target="tpu_custom_call" | custom-call | tf_op jit(solution)/shard_map/image/pallas_call | solution.py:618
  29.5 0.2 collective-permute-done.7.y_ref
  29.7 1.7 %collective-permute-start.8 = (f32[40,128]{1,0:T(8,128)S(1)}, f32[40,128]{1,0:T(8,128)S(1)}, u32[]{:S(2)}, u32[]{:S(2)}) collective-permute-start(f32[40,128]{1,0:T(8,128)S(1)} %merge.9.x_ref), channel_id=1, source_target_pairs={{0,8},{4,12},{8,0},{12,4},{16,24},{20,28},{24,16},{28,20},{1,9},{5... | collective-permute-start | bytes 61448 | tf_op jit(solution)/shard_map/ppermute | solution.py:540
  31.3 2.0 %place.2 = (f32[24,352,128]{2,1,0:T(8,128)S(1)}, f32[24,352,128]{2,1,0:T(8,128)}) custom-call(s32[2,2,2,24]{3,2,1,0:T(2,128)S(1)} %bitcast.35, f32[24,352,128]{2,1,0:T(8,128)S(1)} %bulk.1.rest_1_.bulk_ref, f32[192,128]{1,0:T(8,128)S(1)} %get-tuple-element.65.p_ref, f32[192,128]{1,0:T(8,128)S(1)} %get-tuple-element.66.h_ref), custom_call_target="tpu_custom_call", output_to_operand_aliasing={{0}: (1, {})} | custom-call | tf_op jit(solution)/shard_map/place/pallas_call | solution.py:692
  33.3 0.1 collective-permute-done.8.y_ref
  33.5 1.7 %collective-permute-start.9 = (f32[72,128]{1,0:T(8,128)S(1)}, f32[72,128]{1,0:T(8,128)S(1)}, u32[]{:S(2)}, u32[]{:S(2)}) collective-permute-start(f32[72,128]{1,0:T(8,128)S(1)} %merge.10.x_ref), channel_id=1, source_target_pairs={{0,4},{4,0},{8,12},{12,8},{16,20},{20,16},{24,28},{28,24},{1,5},{5... | collective-permute-start | bytes 110600 | tf_op jit(solution)/shard_map/ppermute | solution.py:540
  35.1 2.0 %place.3 = (f32[24,352,128]{2,1,0:T(8,128)S(1)}, f32[24,352,128]{2,1,0:T(8,128)}) custom-call(s32[2,2,2,24]{3,2,1,0:T(2,128)S(1)} %bitcast.36, f32[24,352,128]{2,1,0:T(8,128)S(1)} %get-tuple-element.67.bulk_ref, f32[192,128]{1,0:T(8,128)S(1)} %get-tuple-element.65.p_ref, ...), custom_call_target="tpu_custom_call", output_to_operand_aliasing={{0}: (1, {}), {1}: (4, {})} | custom-call | tf_op jit(solution)/shard_map/place/pallas_call | solution.py:692
  37.1 0.4 collective-permute-done.9.y_ref
  37.5 0.6 %last.1 = (f32[192,128]{1,0:T(8,128)S(1)}, f32[8,128]{1,0:T(8,128)S(1)}) custom-call(f32[136,128]{1,0:T(8,128)S(1)} %merge.11.got_ref, f32[48,128]{1,0:T(8,128)S(1)} %get-tuple-element.50.id_ref, f32[4,32,128]{2,1,0:T(8,128)S(1)} %get-tuple-element.72.ent_ref, f32[192,128]{1,0:T(8,128)S(1)} %get-tuple-element.73.mu_ref, ...), custom_call_target="tpu_custom_call" | custom-call | tf_op jit(solution)/shard_map/last/pallas_call | solution.py:717
  38.1 0.2 collective-permute-start.11
  38.4 0.7 %finish.1 = (f32[192,128]{1,0:T(8,128)}, f32[24,128]{1,0:T(8,128)}) custom-call(f32[192,128]{1,0:T(8,128)S(1)} %get-tuple-element.75.ml_ref, f32[24,128]{1,0:T(8,128)S(1)} %get-tuple-element.76.dual_ref, f32[24,128]{1,0:T(8,128)S(1)} %copy-done.3, f32[24,128]{1,0:T(8,128)S(1)} %image.3.rest_0_.image_ref, f32[24,128]{1,0:T(8,128)S(1)} %collective-permute-done.10.image2_ref), custom_call_target="tpu_custom_call" | custom-call | tf_op jit(solution)/shard_map/finish/pallas_call | solution.py:725
  39.0 0.3 collective-permute-done.11.sums2_ref
  39.3 0.6 %penalty.1 = f32[1,1]{1,0:T(1,128)} custom-call(f32[8,128]{1,0:T(8,128)S(1)} %get-tuple-element.74.pen_ref, f32[8,128]{1,0:T(8,128)S(1)} %get-tuple-element.79.sums_ref, f32[8,128]{1,0:T(8,128)S(1)} %collective-permute-done.11.sums2_ref), custom_call_target="tpu_custom_call" | custom-call | tf_op jit(solution)/shard_map/penalty/pallas_call | solution.py:733
  (26 shorter events, 0.1 us)
Async XLA Ops:
  0.6 6.0 %copy-start = (bf16[24,2,22528]{2,1,0:T(2,128)(2,1)S(1)}, bf16[24,2,22528]{2,1,0:T(2,128)(2,1)}, u32[]{:S(2)}) copy-start(bf16[24,2,22528]{2,1,0:T(2,128)(2,1)} %param.14) | copy-start | bytes 6488068
  0.6 6.0 %copy-start.1 = (f32[24,2,512]{2,1,0:T(2,128)S(1)}, f32[24,2,512]{2,1,0:T(2,128)}, u32[]{:S(2)}) copy-start(f32[24,2,512]{2,1,0:T(2,128)} %param.18) | copy-start | bytes 294916
  0.7 6.0 %copy-start.6 = (f32[24]{0:T(128)S(1)}, f32[24]{0:T(128)}, u32[]{:S(2)}) copy-start(f32[24]{0:T(128)} %param.13) | copy-start | bytes 292
  0.7 5.9 %copy-start.4 = (s32[24,2,2,2]{0,3,2,1:T(2,128)S(1)}, s32[24,2,2,2]{0,3,2,1:T(2,128)}, u32[]{:S(2)}) copy-start(s32[24,2,2,2]{0,3,2,1:T(2,128)} %param.11) | copy-start | bytes 2308
  0.7 5.9 %copy-start.5 = (s32[3,24]{1,0:T(4,128)S(1)}, s32[3,24]{1,0:T(4,128)}, u32[]{:S(2)}) copy-start(s32[3,24]{1,0:T(4,128)} %nodes_ref.1) | copy-start | bytes 868
  3.6 5.1 %collective-permute-start = (f32[96,128]{1,0:T(8,128)S(1)}, f32[96,128]{1,0:T(8,128)S(1)}, u32[]{:S(2)}, u32[]{:S(2)}) collective-permute-start(f32[96,128]{1,0:T(8,128)S(1)} %get-tuple-element.53.pieces_ref), channel_id=1, source_target_pairs={{2,0},{0,2},{3,1},{1,3},{6,4},{4,6},{7,5},{5,7},{10,8},{8,10},{11,... | collective-permute-start | bytes 147464 | tf_op jit(solution)/shard_map/ppermute | solution.py:533
  9.3 4.9 %collective-permute-start.1 = (f32[24,128]{1,0:T(8,128)S(1)}, f32[24,128]{1,0:T(8,128)S(1)}, u32[]{:S(2)}, u32[]{:S(2)}) collective-permute-start(f32[24,128]{1,0:T(8,128)S(1)} %get-tuple-element.56.x_ref), channel_id=1, source_target_pairs={{0,16},{4,20},{8,24},{12,28},{16,0},{20,4},{24,8},{28,12},{1,17},{... | collective-permute-start | bytes 36872 | tf_op jit(solution)/shard_map/ppermute | solution.py:540
  14.2 3.1 %copy-start.2 = (f32[24,128]{1,0:T(8,128)S(1)}, f32[24,128]{1,0:T(8,128)}, u32[]{:S(2)}) copy-start(f32[24,128]{1,0:T(8,128)} %dual_ref.1) | copy-start | bytes 36868
  14.2 3.1 %copy-start.3 = (f32[24,128]{1,0:T(8,128)S(1)}, f32[24,128]{1,0:T(8,128)}, u32[]{:S(2)}) copy-start(f32[24,128]{1,0:T(8,128)} %rhs_ref.3) | copy-start | bytes 36868
  14.2 4.0 %collective-permute-start.2 = (f32[40,128]{1,0:T(8,128)S(1)}, f32[40,128]{1,0:T(8,128)S(1)}, u32[]{:S(2)}, u32[]{:S(2)}) collective-permute-start(f32[40,128]{1,0:T(8,128)S(1)} %merge.6.x_ref), channel_id=1, source_target_pairs={{0,8},{4,12},{8,0},{12,4},{16,24},{20,28},{24,16},{28,20},{1,9},{5... | collective-permute-start | bytes 61448 | tf_op jit(solution)/shard_map/ppermute | solution.py:540
  16.1 1.2 %collective-permute-start.3 = (f32[24,128]{1,0:T(8,128)S(1)}, f32[24,128]{1,0:T(8,128)S(1)}, u32[]{:S(2)}, u32[]{:S(2)}) collective-permute-start(f32[24,128]{1,0:T(8,128)S(1)} %image.2.rest_0_.image_ref), channel_id=1, source_target_pairs={{0,1},{1,0},{2,3},{3,2},{4,5},{5,4},{6,7},{7,6},{8,9},{9,8},{10,11... | collective-permute-start | bytes 36872 | tf_op jit(solution)/shard_map/ppermute | solution.py:537
  18.2 4.2 %collective-permute-start.4 = (f32[96,128]{1,0:T(8,128)S(1)}, f32[96,128]{1,0:T(8,128)S(1)}, u32[]{:S(2)}, u32[]{:S(2)}) collective-permute-start(f32[96,128]{1,0:T(8,128)S(1)} %merge.7.x_ref), channel_id=1, source_target_pairs={{0,4},{4,0},{8,12},{12,8},{16,20},{20,16},{24,28},{28,24},{1,5},{5... | collective-permute-start | bytes 147464 | tf_op jit(solution)/shard_map/ppermute | solution.py:540
  19.9 4.1 %collective-permute-start.6 = (f32[96,128]{1,0:T(8,128)S(1)}, f32[96,128]{1,0:T(8,128)S(1)}, u32[]{:S(2)}, u32[]{:S(2)}) collective-permute-start(f32[96,128]{1,0:T(8,128)S(1)} %get-tuple-element.59.rest_0_.pieces_ref), channel_id=1, source_target_pairs={{2,0},{0,2},{3,1},{1,3},{6,4},{4,6},{7,5},{5,7},{10,8},{8,10},{11,... | collective-permute-start | bytes 147464 | tf_op jit(solution)/shard_map/ppermute | solution.py:533
  23.2 1.2 %collective-permute-start.5 = (f32[8,128]{1,0:T(8,128)S(1)}, f32[8,128]{1,0:T(8,128)S(1)}, u32[]{:S(2)}, u32[]{:S(2)}) collective-permute-start(f32[8,128]{1,0:T(8,128)S(1)} %get-tuple-element.64.sums_ref), channel_id=1, source_target_pairs={{0,1},{1,0},{2,3},{3,2},{4,5},{5,4},{6,7},{7,6},{8,9},{9,8},{10,11... | collective-permute-start | bytes 12296 | tf_op jit(solution)/shard_map/ppermute | solution.py:537
  25.0 4.7 %collective-permute-start.7 = (f32[24,128]{1,0:T(8,128)S(1)}, f32[24,128]{1,0:T(8,128)S(1)}, u32[]{:S(2)}, u32[]{:S(2)}) collective-permute-start(f32[24,128]{1,0:T(8,128)S(1)} %get-tuple-element.70.x_ref), channel_id=1, source_target_pairs={{0,16},{4,20},{8,24},{12,28},{16,0},{20,4},{24,8},{28,12},{1,17},{... | collective-permute-start | bytes 36872 | tf_op jit(solution)/shard_map/ppermute | solution.py:540
  29.7 3.8 %collective-permute-start.8 = (f32[40,128]{1,0:T(8,128)S(1)}, f32[40,128]{1,0:T(8,128)S(1)}, u32[]{:S(2)}, u32[]{:S(2)}) collective-permute-start(f32[40,128]{1,0:T(8,128)S(1)} %merge.9.x_ref), channel_id=1, source_target_pairs={{0,8},{4,12},{8,0},{12,4},{16,24},{20,28},{24,16},{28,20},{1,9},{5... | collective-permute-start | bytes 61448 | tf_op jit(solution)/shard_map/ppermute | solution.py:540
  33.5 4.0 %collective-permute-start.9 = (f32[72,128]{1,0:T(8,128)S(1)}, f32[72,128]{1,0:T(8,128)S(1)}, u32[]{:S(2)}, u32[]{:S(2)}) collective-permute-start(f32[72,128]{1,0:T(8,128)S(1)} %merge.10.x_ref), channel_id=1, source_target_pairs={{0,4},{4,0},{8,12},{12,8},{16,20},{20,16},{24,28},{28,24},{1,5},{5... | collective-permute-start | bytes 110600 | tf_op jit(solution)/shard_map/ppermute | solution.py:540
  35.1 3.2 %collective-permute-start.10 = (f32[24,128]{1,0:T(8,128)S(1)}, f32[24,128]{1,0:T(8,128)S(1)}, u32[]{:S(2)}, u32[]{:S(2)}) collective-permute-start(f32[24,128]{1,0:T(8,128)S(1)} %image.3.rest_0_.image_ref), channel_id=1, source_target_pairs={{0,1},{1,0},{2,3},{3,2},{4,5},{5,4},{6,7},{7,6},{8,9},{9,8},{10,11... | collective-permute-start | bytes 36872 | tf_op jit(solution)/shard_map/ppermute | solution.py:537
  38.1 1.2 %collective-permute-start.11 = (f32[8,128]{1,0:T(8,128)S(1)}, f32[8,128]{1,0:T(8,128)S(1)}, u32[]{:S(2)}, u32[]{:S(2)}) collective-permute-start(f32[8,128]{1,0:T(8,128)S(1)} %get-tuple-element.79.sums_ref), channel_id=1, source_target_pairs={{0,1},{1,0},{2,3},{3,2},{4,5},{5,4},{6,7},{7,6},{8,9},{9,8},{10,11... | collective-permute-start | bytes 12296 | tf_op jit(solution)/shard_map/ppermute | solution.py:537

commit v5 on v4

--- a/solution.py
+++ b/solution.py
@@ -17,7 +17,7 @@
 EPSILON = 1e-06
 F32 = jnp.float32
 BF16 = jnp.bfloat16
-HIGHEST = lax.Precision.HIGHEST
+NOTES = 3
 
 VMEM = pl.BlockSpec(memory_space=pltpu.VMEM)
 SMEM = pl.BlockSpec(memory_space=pltpu.SMEM)
@@ -210,8 +210,18 @@
                 an_ref[pl.ds(h * Q + j * S + s, 1), :] = line[:, h * BLK : (h + 1) * BLK]
 
 
-def total(x):
-    return jnp.sum(x, axis=(0, 1), keepdims=True)
+def added(x):
+    return jnp.sum(x, axis=0, keepdims=True)
+
+
+def chosen_sums(same, x):
+    same, sums = same.astype(BF16), None
+    for _ in range(3):
+        part = x.astype(BF16)
+        y = jnp.dot(same, part, preferred_element_type=F32)
+        sums = y if sums is None else sums + y
+        x = x - part.astype(F32)
+    return sums
 
 
 def primal_step(
@@ -256,12 +266,7 @@
     step_ref[...] = 2.0 * p_out[mine, :] - p_ref[mine, :]
     for h in range(HB):
         h_out[h * Q : (h + 1) * Q, :] = hedged[h]
-    sums = jnp.dot(
-        same[:, :Q],
-        jnp.concatenate([wb * x for x in hedged] + [wb], axis=1),
-        precision=HIGHEST,
-        preferred_element_type=F32,
-    )
+    sums = chosen_sums(same[:, :Q], jnp.concatenate([wb * x for x in hedged] + [wb], axis=1))
     mass = sums[:, HB * BLK :]
     inner = []
     for j in range(J):
@@ -290,13 +295,11 @@
                 name, weight = jnp.where(fresh, name, -1.0), jnp.where(fresh, weight, 0.0)
             note = jnp.where(lane == e, name, note)
             note = jnp.where(lane == 2 * J + e, weight, note)
-    note = jnp.where(lane == 4 * J, total(gap), note)
-    note = jnp.where(lane == 4 * J + 1, total(drift), note)
     at = 2 * J * HB
-    send_ref[pl.ds(2 * J * HB, 1), :] = note
-    send_ref[pl.ds(at + 1, send_ref.shape[0] - at - 1), :] = jnp.zeros(
-        (send_ref.shape[0] - at - 1, BLK), F32
-    )
+    for i, row in enumerate((note, added(gap), added(drift))):
+        send_ref[pl.ds(at + i, 1), :] = row
+    rest = send_ref.shape[0] - at - NOTES
+    send_ref[pl.ds(at + NOTES, rest), :] = jnp.zeros((rest, BLK), F32)
 
 
 def first_kernel(
@@ -327,7 +330,9 @@
         )
         for h in range(HB)
     ]
-    notes = got_ref[pl.ds(E * HB * devices, devices), :]
+    notes, gaps, drifts = (
+        got_ref[pl.ds(E * HB * devices + i, devices, stride=NOTES), :] for i in range(NOTES)
+    )
     wide = lambda at: jnp.broadcast_to(notes[:, at : at + 1], (devices, BLK))
     names = jnp.concatenate([wide(e) for e in range(E)], axis=0)
     weight = jnp.concatenate([wide(E + e) for e in range(E)], axis=0)
@@ -335,12 +340,7 @@
     across = jnp.transpose(names)[0:1, :]
     count = E * devices
     same = (jnp.broadcast_to(every[:, :1], (every.shape[0], count)) == across).astype(F32)
-    totals = jnp.dot(
-        same,
-        jnp.concatenate(sums + [weight], axis=1),
-        precision=HIGHEST,
-        preferred_element_type=F32,
-    )
+    totals = chosen_sums(same, jnp.concatenate(sums + [weight], axis=1))
     mass = totals[:, HB * BLK :]
     positive = mass > 0
     safe = jnp.where(positive, mass, 1.0)
@@ -348,13 +348,11 @@
         jnp.where(positive, totals[:, h * BLK : (h + 1) * BLK] / safe, 0.0) for h in range(HB)
     ]
     own_safe = jnp.where(weight > 0, weight, 1.0)
-    gap = total(notes[:, 2 * E : 2 * E + 1])
-    drift = total(notes[:, 2 * E + 1 : 2 * E + 2])
     rows = ids.shape[0]
     spread = jnp.zeros((count, BLK), F32)
     for h in range(HB):
         spread = spread + weight * (sums[h] / own_safe - means[h][rows:]) ** 2
-    gap = gap + total(spread)
+    gap, drift = added(gaps) + added(spread), added(drifts)
     return positive[:rows], [m[:rows] for m in means], [m[rows:] for m in means], weight, gap, drift
 
 
@@ -362,26 +360,29 @@
     change = jnp.zeros_like(weight)
     for mean, old in zip(means, before):
         change = change + weight * (mean - old) ** 2
-    return total(change)
+    return added(change)
 
 
 def put_sums(gap, drift, out_ref):
-    lane = lax.broadcasted_iota(jnp.int32, out_ref.shape, 1)
-    out_ref[...] = jnp.where(lane == 0, gap, drift)
+    out_ref[...] = jnp.concatenate(
+        [gap, drift, jnp.zeros((out_ref.shape[0] - 2, BLK), F32)], axis=0
+    )
 
 
 def scaled(penalty, own_ref, other_refs):
     sums = own_ref[...]
     for ref in other_refs:
         sums = sums + ref[...]
-    return penalty * jnp.sqrt(sums[0:1, 0:1] / (sums[0:1, 1:2] + EPSILON))
+    sums = jnp.sum(sums, axis=1, keepdims=True)
+    return penalty * jnp.sqrt(sums[0:1] / (sums[1:2] + EPSILON))
 
 
 def nodes_kernel(
     S, J, HB, devices, got_ref, id_ref, mu_ref, h_ref, ml_ref, table_ref, an_out, ml_out, ent_ref, sums_ref, old_sc
 ):
     Q, E = J * S, 2 * J
-    names = jnp.maximum(got_ref[pl.ds(E * HB * devices, devices), :], 0.0).astype(jnp.int32)
+    names = got_ref[pl.ds(E * HB * devices, devices, stride=NOTES), :]
+    names = jnp.maximum(names, 0.0).astype(jnp.int32)
     shared, means, entry_means, weight, gap, drift = read_nodes(
         J, HB, got_ref, id_ref[...], devices
     )
@@ -487,9 +488,10 @@
     high = lax.rem(lax.axis_index("scen") // apart, 2)
     for place, ref in ((high, x_ref), (1 - high, y_ref)):
         out_ref[pl.ds(pl.multiple_of(place * rows, 8), rows), :] = ref[:rows, :]
-        for i in range(count):
-            out_ref[pl.ds(2 * rows + place * count + i, 1), :] = ref[rows + i : rows + i + 1, :]
-    used = 2 * rows + 2 * count
+        for i in range(NOTES * count):
+            at = 2 * rows + place * (NOTES * count) + i
+            out_ref[pl.ds(at, 1), :] = ref[rows + i : rows + i + 1, :]
+    used = 2 * rows + 2 * NOTES * count
     if out_ref.shape[0] > used:
         out_ref[used:, :] = jnp.zeros((out_ref.shape[0] - used, BLK), F32)
 
@@ -514,7 +516,7 @@
     HB, C = hedged // BLK, columns // BLK
     K, Q = R * NZ, J * S
     devices = scens
-    message = -(-(2 * J * HB + 1) // 8) * 8
+    message = -(-(2 * J * HB + NOTES) // 8) * 8
     static = (S, J, R, NZ, HB)
 
     def interleave(x):
@@ -540,7 +542,7 @@
         return lax.ppermute(x, "scen", [(i, i ^ apart) for i in range(scens)])
 
     def merge(x, y, apart, count, least, *after):
-        rows = max(least, 2 * count * (2 * J * HB) + -(-2 * count // 8) * 8)
+        rows = max(least, 2 * count * (2 * J * HB) + -(-2 * NOTES * count // 8) * 8)
         return pl.pallas_call(
             functools.partial(merge_kernel, apart, count, 2 * J * HB),
             out_shape=near(rows, BLK),

time: 40.1 us -> 39.3 us (0.980)
  Pallas kernels: 18.2 us -> 17.3 us
  transfers between devices with their start and end apart: 12 -> 12, of which waited for: 8 -> 8; matrix products, arithmetic and copies ran while one was open for 0% -> 0% of each run, Pallas kernels for 34% -> 33%
where the time goes in v5:
time: 39.3 us; the launch traced here: 39.1 us
  starting transfers between devices  17.5 us (45%)
  Pallas kernels  17.3 us (44%)
  waiting for transfers between devices  3.47 us (9%)
  between operations  0.81 us (2%)
    ppermute x6, starting transfers between devices, partner(): return lax.ppermute(x, 'scen', [(i, i ^ apart) for i in range(scens)])  12.7 us
    ppermute x2, starting transfers between devices, from_rows(): lax.ppermute(x, 'rows', [((i + q) % R, i) for i in range(R)])  4.5 us
    pallas_call x2, Pallas kernels, place(): pl.pallas_call(functools.partial(place_kernel, *static, first, count, cut...  3.99 us
    pallas_call x2, Pallas kernels, image_of(): pl.pallas_call(functools.partial(image_kernel, S, J, NZ), out_shape=near(...  3.46 us
    pallas_call x1, Pallas kernels, local(): pl.pallas_call(functools.partial(pieces_kernel, S, J, NZ), out_shape=[nea...  2.9 us
    pallas_call x1, Pallas kernels, local(): pl.pallas_call(functools.partial(setup_kernel, *static), out_shape=[near(...  2.04 us
    ppermute x6, waiting for transfers between devices, partner(): return lax.ppermute(x, 'scen', [(i, i ^ apart) for i in range(scens)])  1.75 us
    ppermute x2, waiting for transfers between devices, from_rows(): lax.ppermute(x, 'rows', [((i + q) % R, i) for i in range(R)])  1.08 us
  transfers between devices with their start and end apart: 12, of which 8 were waited for; matrix products, arithmetic and copies ran while one was open for 0% of the time, Pallas kernels for 33%

profile of v5, /device:TPU:0, one launch (start us, length us, event | category | flops | bytes accessed | tf_op | source)
XLA Modules:
  0.0 39.1 jit_solution(10533339738559329886)
XLA Ops:
  0.7 2.9 %pieces.1 = (f32[96,128]{1,0:T(8,128)S(1)}, bf16[24,4,128,128]{3,2,1,0:T(8,128)(2,1)S(1)}, bf16[24,352,128]{2,1,0:T(8,128)(2,1)S(1)}) custom-call(bf16[24,4,128,128]{3,2,1,0:T(8,128)(2,1)} %bitcast.39, f32[24,128]{1,0:T(8,128)} %dual_ref.1, bf16[24,352,128]{2,1,0:T(8,128)(2,1)} %bitcast.40), custom_call_target="tpu_custom_call" | custom-call | tf_op jit(solution)/shard_map/pieces/pallas_call | solution.py:568
  3.6 3.0 %collective-permute-start = (f32[96,128]{1,0:T(8,128)S(1)}, f32[96,128]{1,0:T(8,128)S(1)}, u32[]{:S(2)}, u32[]{:S(2)}) collective-permute-start(f32[96,128]{1,0:T(8,128)S(1)} %get-tuple-element.53.pieces_ref), channel_id=1, source_target_pairs={{2,0},{0,2},{3,1},{1,3},{6,4},{4,6},{7,5},{5,7},{10,8},{8,10},{11,... | collective-permute-start | bytes 147464 | tf_op jit(solution)/shard_map/ppermute | solution.py:535
  6.6 2.0 %setup.1 = (f32[192,128]{1,0:T(8,128)S(1)}, f32[192,128]{1,0:T(8,128)S(1)}, f32[192,128]{1,0:T(8,128)S(1)}, f32[192,128]{1,0:T(8,128)S(1)}, f32[192,128]{1,0:T(8...) custom-call(s32[3,24]{1,0:T(4,128)S(1)} %copy-done.5, ...), custom_call_target="tpu_custom_call" | custom-call | tf_op jit(solution)/shard_map/setup/pallas_call | solution.py:584
  8.7 0.4 first.1
  9.1 3.2 %collective-permute-start.1 = (f32[24,128]{1,0:T(8,128)S(1)}, f32[24,128]{1,0:T(8,128)S(1)}, u32[]{:S(2)}, u32[]{:S(2)}) collective-permute-start(f32[24,128]{1,0:T(8,128)S(1)} %get-tuple-element.56.x_ref), channel_id=1, source_target_pairs={{0,16},{4,20},{8,24},{12,28},{16,0},{20,4},{24,8},{28,12},{1,17},{... | collective-permute-start | bytes 36872 | tf_op jit(solution)/shard_map/ppermute | solution.py:542
  12.2 1.7 %image.2.rest_0_.image_ref = f32[24,128]{1,0:T(8,128)S(1)} custom-call(bf16[24,4,128,128]{3,2,1,0:T(8,128)(2,1)S(1)} %get-tuple-element.57.lp_ref, f32[96,128]{1,0:T(8,128)S(1)} %get-tuple-element.58.step_ref), custom_call_target="tpu_custom_call" | custom-call | tf_op jit(solution)/shard_map/image/pallas_call | solution.py:620
  14.0 1.9 %collective-permute-start.2 = (f32[40,128]{1,0:T(8,128)S(1)}, f32[40,128]{1,0:T(8,128)S(1)}, u32[]{:S(2)}, u32[]{:S(2)}) collective-permute-start(f32[40,128]{1,0:T(8,128)S(1)} %merge.6.x_ref), channel_id=1, source_target_pairs={{0,8},{4,12},{8,0},{12,4},{16,24},{20,28},{24,16},{28,20},{1,9},{5... | collective-permute-start | bytes 61448 | tf_op jit(solution)/shard_map/ppermute | solution.py:542
  15.9 1.0 %bulk.1.rest_1_.bulk_ref = f32[24,352,128]{2,1,0:T(8,128)S(1)} custom-call(bf16[24,352,128]{2,1,0:T(8,128)(2,1)S(1)} %get-tuple-element.42.primal_ref, bf16[24,352,128]{2,1,0:T(8,128)(2,1)S(1)} %bitcast.32), custom_call_target="tpu_custom_call" | custom-call | tf_op jit(solution)/shard_map/bulk/pallas_call | solution.py:646
  16.9 0.2 collective-permute-done.3.image2_ref
  17.1 0.9 %dual.1 = (f32[24,128]{1,0:T(8,128)S(1)}, f32[96,128]{1,0:T(8,128)S(1)}) custom-call(bf16[24,4,128,128]{3,2,1,0:T(8,128)(2,1)S(1)} %get-tuple-element.57.lp_ref, f32[24,128]{1,0:T(8,128)S(1)} %copy-done.2, f32[24,128]{1,0:T(8,128)S(1)} %copy-done.3, f32[24,128]{1,0:T(8,128)S(1)} %image.2.rest_0_.image_ref, f32[24,128]{1,0:T(8,128)S(1)} %collective-permute-done.3.image2_ref), custom_call_target="tpu_custom_call" | custom-call | tf_op jit(solution)/shard_map/dual/pallas_call | solution.py:654
  18.0 1.7 %collective-permute-start.4 = (f32[96,128]{1,0:T(8,128)S(1)}, f32[96,128]{1,0:T(8,128)S(1)}, u32[]{:S(2)}, u32[]{:S(2)}) collective-permute-start(f32[96,128]{1,0:T(8,128)S(1)} %merge.7.x_ref), channel_id=1, source_target_pairs={{0,4},{4,0},{8,12},{12,8},{16,20},{20,16},{24,28},{28,24},{1,5},{5... | collective-permute-start | bytes 147464 | tf_op jit(solution)/shard_map/ppermute | solution.py:542
  19.7 1.5 %collective-permute-start.6 = (f32[96,128]{1,0:T(8,128)S(1)}, f32[96,128]{1,0:T(8,128)S(1)}, u32[]{:S(2)}, u32[]{:S(2)}) collective-permute-start(f32[96,128]{1,0:T(8,128)S(1)} %get-tuple-element.59.rest_0_.pieces_ref), channel_id=1, source_target_pairs={{2,0},{0,2},{3,1},{1,3},{6,4},{4,6},{7,5},{5,7},{10,8},{8,10},{11,... | collective-permute-start | bytes 147464 | tf_op jit(solution)/shard_map/ppermute | solution.py:535
  21.2 1.0 %collective-permute-done.4.y_ref = f32[96,128]{1,0:T(8,128)S(1)} collective-permute-done((f32[96,128]{1,0:T(8,128)S(1)}, f32[96,128]{1,0:T(8,128)S(1)}, u32[]{:S(2)}, u32[]{:S(2)}) %collective-permute-start.4) | collective-permute-done | bytes 49184 | tf_op jit(solution)/shard_map/ppermute | solution.py:542
  22.2 0.4 %nodes.1 = (f32[192,128]{1,0:T(8,128)S(1)}, f32[192,128]{1,0:T(8,128)S(1)}, f32[4,32,128]{2,1,0:T(8,128)S(1)}, f32[8,128]{1,0:T(8,128)S(1)}) custom-call(f32[152,128]{1,0:T(8,128)S(1)} %merge.8.got_ref, f32[48,128]{1,0:T(8,128)S(1)} %get-tuple-element.50.id_ref, f32[192,128]{1,0:T(8,128)S(1)} %get-tuple-element.60.mu_ref, ...), custom_call_target="tpu_custom_call" | custom-call | tf_op jit(solution)/shard_map/nodes/pallas_call | solution.py:668
  22.6 0.1 collective-permute-start.5
  22.7 1.1 %collective-permute-done.6.rest_0_ = f32[96,128]{1,0:T(8,128)S(1)} collective-permute-done((f32[96,128]{1,0:T(8,128)S(1)}, f32[96,128]{1,0:T(8,128)S(1)}, u32[]{:S(2)}, u32[]{:S(2)}) %collective-permute-start.6) | collective-permute-done | bytes 49184 | tf_op jit(solution)/shard_map/ppermute | solution.py:535
  23.8 0.1 collective-permute-done.5.sums2_ref
  23.9 0.4 %second.1 = (f32[192,128]{1,0:T(8,128)S(1)}, f32[192,128]{1,0:T(8,128)S(1)}, f32[192,128]{1,0:T(8,128)S(1)}, f32[24,128]{1,0:T(8,128)S(1)}, f32[96,128]{1,0:T(8,128)S(1)}, /*index=5*/f32[8,128]{1,0:T(8,128)S(1)}) custom-call(f32[192,128]{1,0:T(8,128)S(1)} %get-tuple-element.54.pp_ref, f32[192,128]{1,0:T(8,128)S(1)} %get-tuple-element.44.pc_ref, ...), custom_call_target="tpu_custom_call" | custom-call | tf_op jit(solution)/shard_map/second/pallas_call | solution.py:681
  24.3 2.7 %collective-permute-start.7 = (f32[24,128]{1,0:T(8,128)S(1)}, f32[24,128]{1,0:T(8,128)S(1)}, u32[]{:S(2)}, u32[]{:S(2)}) collective-permute-start(f32[24,128]{1,0:T(8,128)S(1)} %get-tuple-element.70.x_ref), channel_id=1, source_target_pairs={{0,16},{4,20},{8,24},{12,28},{16,0},{20,4},{24,8},{28,12},{1,17},{... | collective-permute-start | bytes 36872 | tf_op jit(solution)/shard_map/ppermute | solution.py:542
  27.0 1.7 %image.3.rest_0_.image_ref = f32[24,128]{1,0:T(8,128)S(1)} custom-call(bf16[24,4,128,128]{3,2,1,0:T(8,128)(2,1)S(1)} %get-tuple-element.57.lp_ref, f32[96,128]{1,0:T(8,128)S(1)} %get-tuple-element.71.step_ref), custom_call_target="tpu_custom_call" | custom-call | tf_op jit(solution)/shard_map/image/pallas_call | solution.py:620
  28.8 0.2 collective-permute-done.7.y_ref
  29.0 1.6 %collective-permute-start.8 = (f32[40,128]{1,0:T(8,128)S(1)}, f32[40,128]{1,0:T(8,128)S(1)}, u32[]{:S(2)}, u32[]{:S(2)}) collective-permute-start(f32[40,128]{1,0:T(8,128)S(1)} %merge.9.x_ref), channel_id=1, source_target_pairs={{0,8},{4,12},{8,0},{12,4},{16,24},{20,28},{24,16},{28,20},{1,9},{5... | collective-permute-start | bytes 61448 | tf_op jit(solution)/shard_map/ppermute | solution.py:542
  30.6 2.0 %place.2 = (f32[24,352,128]{2,1,0:T(8,128)S(1)}, f32[24,352,128]{2,1,0:T(8,128)}) custom-call(s32[2,2,2,24]{3,2,1,0:T(2,128)S(1)} %bitcast.35, f32[24,352,128]{2,1,0:T(8,128)S(1)} %bulk.1.rest_1_.bulk_ref, f32[192,128]{1,0:T(8,128)S(1)} %get-tuple-element.65.p_ref, f32[192,128]{1,0:T(8,128)S(1)} %get-tuple-element.66.h_ref), custom_call_target="tpu_custom_call", output_to_operand_aliasing={{0}: (1, {})} | custom-call | tf_op jit(solution)/shard_map/place/pallas_call | solution.py:694
  32.6 0.1 collective-permute-done.8.y_ref
  32.8 1.7 %collective-permute-start.9 = (f32[80,128]{1,0:T(8,128)S(1)}, f32[80,128]{1,0:T(8,128)S(1)}, u32[]{:S(2)}, u32[]{:S(2)}) collective-permute-start(f32[80,128]{1,0:T(8,128)S(1)} %merge.10.x_ref), channel_id=1, source_target_pairs={{0,4},{4,0},{8,12},{12,8},{16,20},{20,16},{24,28},{28,24},{1,5},{5... | collective-permute-start | bytes 122888 | tf_op jit(solution)/shard_map/ppermute | solution.py:542
  34.4 2.0 %place.3 = (f32[24,352,128]{2,1,0:T(8,128)S(1)}, f32[24,352,128]{2,1,0:T(8,128)}) custom-call(s32[2,2,2,24]{3,2,1,0:T(2,128)S(1)} %bitcast.36, f32[24,352,128]{2,1,0:T(8,128)S(1)} %get-tuple-element.67.bulk_ref, f32[192,128]{1,0:T(8,128)S(1)} %get-tuple-element.65.p_ref, ...), custom_call_target="tpu_custom_call", output_to_operand_aliasing={{0}: (1, {}), {1}: (4, {})} | custom-call | tf_op jit(solution)/shard_map/place/pallas_call | solution.py:694
  36.4 0.4 %collective-permute-done.9.y_ref = f32[80,128]{1,0:T(8,128)S(1)} collective-permute-done((f32[80,128]{1,0:T(8,128)S(1)}, f32[80,128]{1,0:T(8,128)S(1)}, u32[]{:S(2)}, u32[]{:S(2)}) %collective-permute-start.9) | collective-permute-done | bytes 40992 | tf_op jit(solution)/shard_map/ppermute | solution.py:542
  36.9 0.4 %last.1 = (f32[192,128]{1,0:T(8,128)S(1)}, f32[8,128]{1,0:T(8,128)S(1)}) custom-call(f32[152,128]{1,0:T(8,128)S(1)} %merge.11.got_ref, f32[48,128]{1,0:T(8,128)S(1)} %get-tuple-element.50.id_ref, f32[4,32,128]{2,1,0:T(8,128)S(1)} %get-tuple-element.72.ent_ref, f32[192,128]{1,0:T(8,128)S(1)} %get-tuple-element.73.mu_ref, ...), custom_call_target="tpu_custom_call" | custom-call | tf_op jit(solution)/shard_map/last/pallas_call | solution.py:719
  37.3 0.2 collective-permute-start.11
  37.5 0.7 %finish.1 = (f32[192,128]{1,0:T(8,128)}, f32[24,128]{1,0:T(8,128)}) custom-call(f32[192,128]{1,0:T(8,128)S(1)} %get-tuple-element.75.ml_ref, f32[24,128]{1,0:T(8,128)S(1)} %get-tuple-element.76.dual_ref, f32[24,128]{1,0:T(8,128)S(1)} %copy-done.3, f32[24,128]{1,0:T(8,128)S(1)} %image.3.rest_0_.image_ref, f32[24,128]{1,0:T(8,128)S(1)} %collective-permute-done.10.image2_ref), custom_call_target="tpu_custom_call" | custom-call | tf_op jit(solution)/shard_map/finish/pallas_call | solution.py:727
  38.1 0.4 collective-permute-done.11.sums2_ref
  38.5 0.6 %penalty.1 = f32[1,1]{1,0:T(1,128)} custom-call(f32[8,128]{1,0:T(8,128)S(1)} %get-tuple-element.74.pen_ref, f32[8,128]{1,0:T(8,128)S(1)} %get-tuple-element.79.sums_ref, f32[8,128]{1,0:T(8,128)S(1)} %collective-permute-done.11.sums2_ref), custom_call_target="tpu_custom_call" | custom-call | tf_op jit(solution)/shard_map/penalty/pallas_call | solution.py:735
  (26 shorter events, 0.1 us)
Async XLA Ops:
  0.6 6.0 %copy-start = (bf16[24,2,22528]{2,1,0:T(2,128)(2,1)S(1)}, bf16[24,2,22528]{2,1,0:T(2,128)(2,1)}, u32[]{:S(2)}) copy-start(bf16[24,2,22528]{2,1,0:T(2,128)(2,1)} %param.14) | copy-start | bytes 6488068
  0.6 6.0 %copy-start.1 = (f32[24,2,512]{2,1,0:T(2,128)S(1)}, f32[24,2,512]{2,1,0:T(2,128)}, u32[]{:S(2)}) copy-start(f32[24,2,512]{2,1,0:T(2,128)} %param.18) | copy-start | bytes 294916
  0.7 6.0 %copy-start.6 = (f32[24]{0:T(128)S(1)}, f32[24]{0:T(128)}, u32[]{:S(2)}) copy-start(f32[24]{0:T(128)} %param.13) | copy-start | bytes 292
  0.7 5.9 %copy-start.4 = (s32[24,2,2,2]{0,3,2,1:T(2,128)S(1)}, s32[24,2,2,2]{0,3,2,1:T(2,128)}, u32[]{:S(2)}) copy-start(s32[24,2,2,2]{0,3,2,1:T(2,128)} %param.11) | copy-start | bytes 2308
  0.7 5.9 %copy-start.5 = (s32[3,24]{1,0:T(4,128)S(1)}, s32[3,24]{1,0:T(4,128)}, u32[]{:S(2)}) copy-start(s32[3,24]{1,0:T(4,128)} %nodes_ref.1) | copy-start | bytes 868
  3.6 5.1 %collective-permute-start = (f32[96,128]{1,0:T(8,128)S(1)}, f32[96,128]{1,0:T(8,128)S(1)}, u32[]{:S(2)}, u32[]{:S(2)}) collective-permute-start(f32[96,128]{1,0:T(8,128)S(1)} %get-tuple-element.53.pieces_ref), channel_id=1, source_target_pairs={{2,0},{0,2},{3,1},{1,3},{6,4},{4,6},{7,5},{5,7},{10,8},{8,10},{11,... | collective-permute-start | bytes 147464 | tf_op jit(solution)/shard_map/ppermute | solution.py:535
  9.1 4.9 %collective-permute-start.1 = (f32[24,128]{1,0:T(8,128)S(1)}, f32[24,128]{1,0:T(8,128)S(1)}, u32[]{:S(2)}, u32[]{:S(2)}) collective-permute-start(f32[24,128]{1,0:T(8,128)S(1)} %get-tuple-element.56.x_ref), channel_id=1, source_target_pairs={{0,16},{4,20},{8,24},{12,28},{16,0},{20,4},{24,8},{28,12},{1,17},{... | collective-permute-start | bytes 36872 | tf_op jit(solution)/shard_map/ppermute | solution.py:542
  14.0 3.1 %copy-start.2 = (f32[24,128]{1,0:T(8,128)S(1)}, f32[24,128]{1,0:T(8,128)}, u32[]{:S(2)}) copy-start(f32[24,128]{1,0:T(8,128)} %dual_ref.1) | copy-start | bytes 36868
  14.0 3.1 %copy-start.3 = (f32[24,128]{1,0:T(8,128)S(1)}, f32[24,128]{1,0:T(8,128)}, u32[]{:S(2)}) copy-start(f32[24,128]{1,0:T(8,128)} %rhs_ref.3) | copy-start | bytes 36868
  14.0 4.0 %collective-permute-start.2 = (f32[40,128]{1,0:T(8,128)S(1)}, f32[40,128]{1,0:T(8,128)S(1)}, u32[]{:S(2)}, u32[]{:S(2)}) collective-permute-start(f32[40,128]{1,0:T(8,128)S(1)} %merge.6.x_ref), channel_id=1, source_target_pairs={{0,8},{4,12},{8,0},{12,4},{16,24},{20,28},{24,16},{28,20},{1,9},{5... | collective-permute-start | bytes 61448 | tf_op jit(solution)/shard_map/ppermute | solution.py:542
  15.9 1.2 %collective-permute-start.3 = (f32[24,128]{1,0:T(8,128)S(1)}, f32[24,128]{1,0:T(8,128)S(1)}, u32[]{:S(2)}, u32[]{:S(2)}) collective-permute-start(f32[24,128]{1,0:T(8,128)S(1)} %image.2.rest_0_.image_ref), channel_id=1, source_target_pairs={{0,1},{1,0},{2,3},{3,2},{4,5},{5,4},{6,7},{7,6},{8,9},{9,8},{10,11... | collective-permute-start | bytes 36872 | tf_op jit(solution)/shard_map/ppermute | solution.py:539
  18.0 4.2 %collective-permute-start.4 = (f32[96,128]{1,0:T(8,128)S(1)}, f32[96,128]{1,0:T(8,128)S(1)}, u32[]{:S(2)}, u32[]{:S(2)}) collective-permute-start(f32[96,128]{1,0:T(8,128)S(1)} %merge.7.x_ref), channel_id=1, source_target_pairs={{0,4},{4,0},{8,12},{12,8},{16,20},{20,16},{24,28},{28,24},{1,5},{5... | collective-permute-start | bytes 147464 | tf_op jit(solution)/shard_map/ppermute | solution.py:542
  19.7 4.1 %collective-permute-start.6 = (f32[96,128]{1,0:T(8,128)S(1)}, f32[96,128]{1,0:T(8,128)S(1)}, u32[]{:S(2)}, u32[]{:S(2)}) collective-permute-start(f32[96,128]{1,0:T(8,128)S(1)} %get-tuple-element.59.rest_0_.pieces_ref), channel_id=1, source_target_pairs={{2,0},{0,2},{3,1},{1,3},{6,4},{4,6},{7,5},{5,7},{10,8},{8,10},{11,... | collective-permute-start | bytes 147464 | tf_op jit(solution)/shard_map/ppermute | solution.py:535
  22.6 1.2 %collective-permute-start.5 = (f32[8,128]{1,0:T(8,128)S(1)}, f32[8,128]{1,0:T(8,128)S(1)}, u32[]{:S(2)}, u32[]{:S(2)}) collective-permute-start(f32[8,128]{1,0:T(8,128)S(1)} %get-tuple-element.64.sums_ref), channel_id=1, source_target_pairs={{0,1},{1,0},{2,3},{3,2},{4,5},{5,4},{6,7},{7,6},{8,9},{9,8},{10,11... | collective-permute-start | bytes 12296 | tf_op jit(solution)/shard_map/ppermute | solution.py:539
  24.3 4.7 %collective-permute-start.7 = (f32[24,128]{1,0:T(8,128)S(1)}, f32[24,128]{1,0:T(8,128)S(1)}, u32[]{:S(2)}, u32[]{:S(2)}) collective-permute-start(f32[24,128]{1,0:T(8,128)S(1)} %get-tuple-element.70.x_ref), channel_id=1, source_target_pairs={{0,16},{4,20},{8,24},{12,28},{16,0},{20,4},{24,8},{28,12},{1,17},{... | collective-permute-start | bytes 36872 | tf_op jit(solution)/shard_map/ppermute | solution.py:542
  29.0 3.8 %collective-permute-start.8 = (f32[40,128]{1,0:T(8,128)S(1)}, f32[40,128]{1,0:T(8,128)S(1)}, u32[]{:S(2)}, u32[]{:S(2)}) collective-permute-start(f32[40,128]{1,0:T(8,128)S(1)} %merge.9.x_ref), channel_id=1, source_target_pairs={{0,8},{4,12},{8,0},{12,4},{16,24},{20,28},{24,16},{28,20},{1,9},{5... | collective-permute-start | bytes 61448 | tf_op jit(solution)/shard_map/ppermute | solution.py:542
  32.8 4.1 %collective-permute-start.9 = (f32[80,128]{1,0:T(8,128)S(1)}, f32[80,128]{1,0:T(8,128)S(1)}, u32[]{:S(2)}, u32[]{:S(2)}) collective-permute-start(f32[80,128]{1,0:T(8,128)S(1)} %merge.10.x_ref), channel_id=1, source_target_pairs={{0,4},{4,0},{8,12},{12,8},{16,20},{20,16},{24,28},{28,24},{1,5},{5... | collective-permute-start | bytes 122888 | tf_op jit(solution)/shard_map/ppermute | solution.py:542
  34.4 3.0 %collective-permute-start.10 = (f32[24,128]{1,0:T(8,128)S(1)}, f32[24,128]{1,0:T(8,128)S(1)}, u32[]{:S(2)}, u32[]{:S(2)}) collective-permute-start(f32[24,128]{1,0:T(8,128)S(1)} %image.3.rest_0_.image_ref), channel_id=1, source_target_pairs={{0,1},{1,0},{2,3},{3,2},{4,5},{5,4},{6,7},{7,6},{8,9},{9,8},{10,11... | collective-permute-start | bytes 36872 | tf_op jit(solution)/shard_map/ppermute | solution.py:539
  37.3 1.2 %collective-permute-start.11 = (f32[8,128]{1,0:T(8,128)S(1)}, f32[8,128]{1,0:T(8,128)S(1)}, u32[]{:S(2)}, u32[]{:S(2)}) collective-permute-start(f32[8,128]{1,0:T(8,128)S(1)} %get-tuple-element.79.sums_ref), channel_id=1, source_target_pairs={{0,1},{1,0},{2,3},{3,2},{4,5},{5,4},{6,7},{7,6},{8,9},{9,8},{10,11... | collective-permute-start | bytes 12296 | tf_op jit(solution)/shard_map/ppermute | solution.py:539

commit v6 on v5

--- a/solution.py
+++ b/solution.py
@@ -564,7 +564,7 @@
     def near_like(x):
         return pltpu.VMEM(x.shape, x.dtype)
 
-    parts = max(p for p in (4, 3, 2, 1) if S % p == 0)
+    parts = max(p for p in (3, 2, 1) if S % p == 0)
     pieces, lp, primal = pl.pallas_call(
         functools.partial(pieces_kernel, S, J, NZ),
         out_shape=[near(NZ * Q, BLK), near_like(lp), near_like(primal)],
@@ -661,7 +661,7 @@
         )(lp, dual_start, bounds_rhs, made["image"], from_section(made["image"]))
         return ((False, made["pieces"]), (False, made["bulk"]))
 
-    got1 = exchange(send1, NZ * Q, image_work, dual_work)
+    got1 = exchange(send1, 88, image_work, dual_work)
     dual1, pieces2 = made["dual"], made["pieces"]
     others2 = from_rows(pieces2)
 

time: 39.3 us -> 39.1 us (level)
  transfers between devices with their start and end apart: 12 -> 12, of which waited for: 8 -> 7; matrix products, arithmetic and copies ran while one was open for 0% -> 0% of each run, Pallas kernels for 33% -> 33%
where the time goes in v6:
time: 39.1 us; the launch traced here: 38.9 us
  starting transfers between devices  17.5 us (45%)
  Pallas kernels  17.2 us (44%)
  waiting for transfers between devices  3.42 us (9%)
  between operations  0.81 us (2%)
    ppermute x6, starting transfers between devices, partner(): return lax.ppermute(x, 'scen', [(i, i ^ apart) for i in range(scens)])  12.7 us
    ppermute x2, starting transfers between devices, from_rows(): lax.ppermute(x, 'rows', [((i + q) % R, i) for i in range(R)])  4.5 us
    pallas_call x2, Pallas kernels, place(): pl.pallas_call(functools.partial(place_kernel, *static, first, count, cut...  3.99 us
    pallas_call x2, Pallas kernels, image_of(): pl.pallas_call(functools.partial(image_kernel, S, J, NZ), out_shape=near(...  3.46 us
    pallas_call x1, Pallas kernels, local(): pl.pallas_call(functools.partial(pieces_kernel, S, J, NZ), out_shape=[nea...  2.77 us
    pallas_call x1, Pallas kernels, local(): pl.pallas_call(functools.partial(setup_kernel, *static), out_shape=[near(...  2.04 us
    ppermute x6, waiting for transfers between devices, partner(): return lax.ppermute(x, 'scen', [(i, i ^ apart) for i in range(scens)])  1.7 us
    ppermute x2, waiting for transfers between devices, from_rows(): lax.ppermute(x, 'rows', [((i + q) % R, i) for i in range(R)])  1.12 us
  transfers between devices with their start and end apart: 12, of which 7 were waited for; matrix products, arithmetic and copies ran while one was open for 0% of the time, Pallas kernels for 33%

profile of v6, /device:TPU:0, one launch (start us, length us, event | category | flops | bytes accessed | tf_op | source)
XLA Modules:
  0.0 38.9 jit_solution(10270061223026929966)
XLA Ops:
  0.7 2.8 %pieces.1 = (f32[96,128]{1,0:T(8,128)S(1)}, bf16[24,4,128,128]{3,2,1,0:T(8,128)(2,1)S(1)}, bf16[24,352,128]{2,1,0:T(8,128)(2,1)S(1)}) custom-call(bf16[24,4,128,128]{3,2,1,0:T(8,128)(2,1)} %bitcast.39, f32[24,128]{1,0:T(8,128)} %dual_ref.1, bf16[24,352,128]{2,1,0:T(8,128)(2,1)} %bitcast.40), custom_call_target="tpu_custom_call" | custom-call | tf_op jit(solution)/shard_map/pieces/pallas_call | solution.py:568
  3.5 3.0 %collective-permute-start = (f32[96,128]{1,0:T(8,128)S(1)}, f32[96,128]{1,0:T(8,128)S(1)}, u32[]{:S(2)}, u32[]{:S(2)}) collective-permute-start(f32[96,128]{1,0:T(8,128)S(1)} %get-tuple-element.53.pieces_ref), channel_id=1, source_target_pairs={{2,0},{0,2},{3,1},{1,3},{6,4},{4,6},{7,5},{5,7},{10,8},{8,10},{11,... | collective-permute-start | bytes 147464 | tf_op jit(solution)/shard_map/ppermute | solution.py:535
  6.5 2.0 %setup.1 = (f32[192,128]{1,0:T(8,128)S(1)}, f32[192,128]{1,0:T(8,128)S(1)}, f32[192,128]{1,0:T(8,128)S(1)}, f32[192,128]{1,0:T(8,128)S(1)}, f32[192,128]{1,0:T(8...) custom-call(s32[3,24]{1,0:T(4,128)S(1)} %copy-done.5, ...), custom_call_target="tpu_custom_call" | custom-call | tf_op jit(solution)/shard_map/setup/pallas_call | solution.py:584
  8.5 0.4 first.1
  8.9 3.2 %collective-permute-start.1 = (f32[24,128]{1,0:T(8,128)S(1)}, f32[24,128]{1,0:T(8,128)S(1)}, u32[]{:S(2)}, u32[]{:S(2)}) collective-permute-start(f32[24,128]{1,0:T(8,128)S(1)} %get-tuple-element.56.x_ref), channel_id=1, source_target_pairs={{0,16},{4,20},{8,24},{12,28},{16,0},{20,4},{24,8},{28,12},{1,17},{... | collective-permute-start | bytes 36872 | tf_op jit(solution)/shard_map/ppermute | solution.py:542
  12.1 1.7 %image.2.rest_0_.image_ref = f32[24,128]{1,0:T(8,128)S(1)} custom-call(bf16[24,4,128,128]{3,2,1,0:T(8,128)(2,1)S(1)} %get-tuple-element.57.lp_ref, f32[96,128]{1,0:T(8,128)S(1)} %get-tuple-element.58.step_ref), custom_call_target="tpu_custom_call" | custom-call | tf_op jit(solution)/shard_map/image/pallas_call | solution.py:620
  13.9 1.9 %collective-permute-start.2 = (f32[40,128]{1,0:T(8,128)S(1)}, f32[40,128]{1,0:T(8,128)S(1)}, u32[]{:S(2)}, u32[]{:S(2)}) collective-permute-start(f32[40,128]{1,0:T(8,128)S(1)} %merge.6.x_ref), channel_id=1, source_target_pairs={{0,8},{4,12},{8,0},{12,4},{16,24},{20,28},{24,16},{28,20},{1,9},{5... | collective-permute-start | bytes 61448 | tf_op jit(solution)/shard_map/ppermute | solution.py:542
  15.8 1.0 %bulk.1.rest_1_.bulk_ref = f32[24,352,128]{2,1,0:T(8,128)S(1)} custom-call(bf16[24,352,128]{2,1,0:T(8,128)(2,1)S(1)} %get-tuple-element.42.primal_ref, bf16[24,352,128]{2,1,0:T(8,128)(2,1)S(1)} %bitcast.32), custom_call_target="tpu_custom_call" | custom-call | tf_op jit(solution)/shard_map/bulk/pallas_call | solution.py:646
  16.7 0.2 collective-permute-done.3.image2_ref
  16.9 0.9 %dual.1 = (f32[24,128]{1,0:T(8,128)S(1)}, f32[96,128]{1,0:T(8,128)S(1)}) custom-call(bf16[24,4,128,128]{3,2,1,0:T(8,128)(2,1)S(1)} %get-tuple-element.57.lp_ref, f32[24,128]{1,0:T(8,128)S(1)} %copy-done.2, f32[24,128]{1,0:T(8,128)S(1)} %copy-done.3, f32[24,128]{1,0:T(8,128)S(1)} %image.2.rest_0_.image_ref, f32[24,128]{1,0:T(8,128)S(1)} %collective-permute-done.3.image2_ref), custom_call_target="tpu_custom_call" | custom-call | tf_op jit(solution)/shard_map/dual/pallas_call | solution.py:654
  17.9 1.7 %collective-permute-start.4 = (f32[88,128]{1,0:T(8,128)S(1)}, f32[88,128]{1,0:T(8,128)S(1)}, u32[]{:S(2)}, u32[]{:S(2)}) collective-permute-start(f32[88,128]{1,0:T(8,128)S(1)} %merge.7.x_ref), channel_id=1, source_target_pairs={{0,4},{4,0},{8,12},{12,8},{16,20},{20,16},{24,28},{28,24},{1,5},{5... | collective-permute-start | bytes 135176 | tf_op jit(solution)/shard_map/ppermute | solution.py:542
  19.6 1.5 %collective-permute-start.6 = (f32[96,128]{1,0:T(8,128)S(1)}, f32[96,128]{1,0:T(8,128)S(1)}, u32[]{:S(2)}, u32[]{:S(2)}) collective-permute-start(f32[96,128]{1,0:T(8,128)S(1)} %get-tuple-element.59.rest_0_.pieces_ref), channel_id=1, source_target_pairs={{2,0},{0,2},{3,1},{1,3},{6,4},{4,6},{7,5},{5,7},{10,8},{8,10},{11,... | collective-permute-start | bytes 147464 | tf_op jit(solution)/shard_map/ppermute | solution.py:535
  21.1 1.0 %collective-permute-done.4.y_ref = f32[88,128]{1,0:T(8,128)S(1)} collective-permute-done((f32[88,128]{1,0:T(8,128)S(1)}, f32[88,128]{1,0:T(8,128)S(1)}, u32[]{:S(2)}, u32[]{:S(2)}) %collective-permute-start.4) | collective-permute-done | bytes 45088 | tf_op jit(solution)/shard_map/ppermute | solution.py:542
  22.0 0.4 %nodes.1 = (f32[192,128]{1,0:T(8,128)S(1)}, f32[192,128]{1,0:T(8,128)S(1)}, f32[4,32,128]{2,1,0:T(8,128)S(1)}, f32[8,128]{1,0:T(8,128)S(1)}) custom-call(f32[152,128]{1,0:T(8,128)S(1)} %merge.8.got_ref, f32[48,128]{1,0:T(8,128)S(1)} %get-tuple-element.50.id_ref, f32[192,128]{1,0:T(8,128)S(1)} %get-tuple-element.60.mu_ref, ...), custom_call_target="tpu_custom_call" | custom-call | tf_op jit(solution)/shard_map/nodes/pallas_call | solution.py:668
  22.5 0.1 collective-permute-start.5
  22.5 1.1 %collective-permute-done.6.rest_0_ = f32[96,128]{1,0:T(8,128)S(1)} collective-permute-done((f32[96,128]{1,0:T(8,128)S(1)}, f32[96,128]{1,0:T(8,128)S(1)}, u32[]{:S(2)}, u32[]{:S(2)}) %collective-permute-start.6) | collective-permute-done | bytes 49184 | tf_op jit(solution)/shard_map/ppermute | solution.py:535
  23.7 0.0 collective-permute-done.5.sums2_ref
  23.7 0.4 %second.1 = (f32[192,128]{1,0:T(8,128)S(1)}, f32[192,128]{1,0:T(8,128)S(1)}, f32[192,128]{1,0:T(8,128)S(1)}, f32[24,128]{1,0:T(8,128)S(1)}, f32[96,128]{1,0:T(8,128)S(1)}, /*index=5*/f32[8,128]{1,0:T(8,128)S(1)}) custom-call(f32[192,128]{1,0:T(8,128)S(1)} %get-tuple-element.54.pp_ref, f32[192,128]{1,0:T(8,128)S(1)} %get-tuple-element.44.pc_ref, ...), custom_call_target="tpu_custom_call" | custom-call | tf_op jit(solution)/shard_map/second/pallas_call | solution.py:681
  24.1 2.7 %collective-permute-start.7 = (f32[24,128]{1,0:T(8,128)S(1)}, f32[24,128]{1,0:T(8,128)S(1)}, u32[]{:S(2)}, u32[]{:S(2)}) collective-permute-start(f32[24,128]{1,0:T(8,128)S(1)} %get-tuple-element.70.x_ref), channel_id=1, source_target_pairs={{0,16},{4,20},{8,24},{12,28},{16,0},{20,4},{24,8},{28,12},{1,17},{... | collective-permute-start | bytes 36872 | tf_op jit(solution)/shard_map/ppermute | solution.py:542
  26.9 1.7 %image.3.rest_0_.image_ref = f32[24,128]{1,0:T(8,128)S(1)} custom-call(bf16[24,4,128,128]{3,2,1,0:T(8,128)(2,1)S(1)} %get-tuple-element.57.lp_ref, f32[96,128]{1,0:T(8,128)S(1)} %get-tuple-element.71.step_ref), custom_call_target="tpu_custom_call" | custom-call | tf_op jit(solution)/shard_map/image/pallas_call | solution.py:620
  28.6 0.2 collective-permute-done.7.y_ref
  28.8 1.6 %collective-permute-start.8 = (f32[40,128]{1,0:T(8,128)S(1)}, f32[40,128]{1,0:T(8,128)S(1)}, u32[]{:S(2)}, u32[]{:S(2)}) collective-permute-start(f32[40,128]{1,0:T(8,128)S(1)} %merge.9.x_ref), channel_id=1, source_target_pairs={{0,8},{4,12},{8,0},{12,4},{16,24},{20,28},{24,16},{28,20},{1,9},{5... | collective-permute-start | bytes 61448 | tf_op jit(solution)/shard_map/ppermute | solution.py:542
  30.4 2.0 %place.2 = (f32[24,352,128]{2,1,0:T(8,128)S(1)}, f32[24,352,128]{2,1,0:T(8,128)}) custom-call(s32[2,2,2,24]{3,2,1,0:T(2,128)S(1)} %bitcast.35, f32[24,352,128]{2,1,0:T(8,128)S(1)} %bulk.1.rest_1_.bulk_ref, f32[192,128]{1,0:T(8,128)S(1)} %get-tuple-element.65.p_ref, f32[192,128]{1,0:T(8,128)S(1)} %get-tuple-element.66.h_ref), custom_call_target="tpu_custom_call", output_to_operand_aliasing={{0}: (1, {})} | custom-call | tf_op jit(solution)/shard_map/place/pallas_call | solution.py:694
  32.5 0.1 collective-permute-done.8.y_ref
  32.6 1.7 %collective-permute-start.9 = (f32[80,128]{1,0:T(8,128)S(1)}, f32[80,128]{1,0:T(8,128)S(1)}, u32[]{:S(2)}, u32[]{:S(2)}) collective-permute-start(f32[80,128]{1,0:T(8,128)S(1)} %merge.10.x_ref), channel_id=1, source_target_pairs={{0,4},{4,0},{8,12},{12,8},{16,20},{20,16},{24,28},{28,24},{1,5},{5... | collective-permute-start | bytes 122888 | tf_op jit(solution)/shard_map/ppermute | solution.py:542
  34.3 2.0 %place.3 = (f32[24,352,128]{2,1,0:T(8,128)S(1)}, f32[24,352,128]{2,1,0:T(8,128)}) custom-call(s32[2,2,2,24]{3,2,1,0:T(2,128)S(1)} %bitcast.36, f32[24,352,128]{2,1,0:T(8,128)S(1)} %get-tuple-element.67.bulk_ref, f32[192,128]{1,0:T(8,128)S(1)} %get-tuple-element.65.p_ref, ...), custom_call_target="tpu_custom_call", output_to_operand_aliasing={{0}: (1, {}), {1}: (4, {})} | custom-call | tf_op jit(solution)/shard_map/place/pallas_call | solution.py:694
  36.3 0.4 %collective-permute-done.9.y_ref = f32[80,128]{1,0:T(8,128)S(1)} collective-permute-done((f32[80,128]{1,0:T(8,128)S(1)}, f32[80,128]{1,0:T(8,128)S(1)}, u32[]{:S(2)}, u32[]{:S(2)}) %collective-permute-start.9) | collective-permute-done | bytes 40992 | tf_op jit(solution)/shard_map/ppermute | solution.py:542
  36.7 0.4 %last.1 = (f32[192,128]{1,0:T(8,128)S(1)}, f32[8,128]{1,0:T(8,128)S(1)}) custom-call(f32[152,128]{1,0:T(8,128)S(1)} %merge.11.got_ref, f32[48,128]{1,0:T(8,128)S(1)} %get-tuple-element.50.id_ref, f32[4,32,128]{2,1,0:T(8,128)S(1)} %get-tuple-element.72.ent_ref, f32[192,128]{1,0:T(8,128)S(1)} %get-tuple-element.73.mu_ref, ...), custom_call_target="tpu_custom_call" | custom-call | tf_op jit(solution)/shard_map/last/pallas_call | solution.py:719
  37.1 0.2 collective-permute-start.11
  37.3 0.7 %finish.1 = (f32[192,128]{1,0:T(8,128)}, f32[24,128]{1,0:T(8,128)}) custom-call(f32[192,128]{1,0:T(8,128)S(1)} %get-tuple-element.75.ml_ref, f32[24,128]{1,0:T(8,128)S(1)} %get-tuple-element.76.dual_ref, f32[24,128]{1,0:T(8,128)S(1)} %copy-done.3, f32[24,128]{1,0:T(8,128)S(1)} %image.3.rest_0_.image_ref, f32[24,128]{1,0:T(8,128)S(1)} %collective-permute-done.10.image2_ref), custom_call_target="tpu_custom_call" | custom-call | tf_op jit(solution)/shard_map/finish/pallas_call | solution.py:727
  38.0 0.4 collective-permute-done.11.sums2_ref
  38.3 0.6 %penalty.1 = f32[1,1]{1,0:T(1,128)} custom-call(f32[8,128]{1,0:T(8,128)S(1)} %get-tuple-element.74.pen_ref, f32[8,128]{1,0:T(8,128)S(1)} %get-tuple-element.79.sums_ref, f32[8,128]{1,0:T(8,128)S(1)} %collective-permute-done.11.sums2_ref), custom_call_target="tpu_custom_call" | custom-call | tf_op jit(solution)/shard_map/penalty/pallas_call | solution.py:735
  (26 shorter events, 0.1 us)
Async XLA Ops:
  0.6 5.8 %copy-start = (bf16[24,2,22528]{2,1,0:T(2,128)(2,1)S(1)}, bf16[24,2,22528]{2,1,0:T(2,128)(2,1)}, u32[]{:S(2)}) copy-start(bf16[24,2,22528]{2,1,0:T(2,128)(2,1)} %param.14) | copy-start | bytes 6488068
  0.6 5.8 %copy-start.1 = (f32[24,2,512]{2,1,0:T(2,128)S(1)}, f32[24,2,512]{2,1,0:T(2,128)}, u32[]{:S(2)}) copy-start(f32[24,2,512]{2,1,0:T(2,128)} %param.18) | copy-start | bytes 294916
  0.7 5.8 %copy-start.6 = (f32[24]{0:T(128)S(1)}, f32[24]{0:T(128)}, u32[]{:S(2)}) copy-start(f32[24]{0:T(128)} %param.13) | copy-start | bytes 292
  0.7 5.8 %copy-start.4 = (s32[24,2,2,2]{0,3,2,1:T(2,128)S(1)}, s32[24,2,2,2]{0,3,2,1:T(2,128)}, u32[]{:S(2)}) copy-start(s32[24,2,2,2]{0,3,2,1:T(2,128)} %param.11) | copy-start | bytes 2308
  0.7 5.8 %copy-start.5 = (s32[3,24]{1,0:T(4,128)S(1)}, s32[3,24]{1,0:T(4,128)}, u32[]{:S(2)}) copy-start(s32[3,24]{1,0:T(4,128)} %nodes_ref.1) | copy-start | bytes 868
  3.5 5.1 %collective-permute-start = (f32[96,128]{1,0:T(8,128)S(1)}, f32[96,128]{1,0:T(8,128)S(1)}, u32[]{:S(2)}, u32[]{:S(2)}) collective-permute-start(f32[96,128]{1,0:T(8,128)S(1)} %get-tuple-element.53.pieces_ref), channel_id=1, source_target_pairs={{2,0},{0,2},{3,1},{1,3},{6,4},{4,6},{7,5},{5,7},{10,8},{8,10},{11,... | collective-permute-start | bytes 147464 | tf_op jit(solution)/shard_map/ppermute | solution.py:535
  8.9 4.9 %collective-permute-start.1 = (f32[24,128]{1,0:T(8,128)S(1)}, f32[24,128]{1,0:T(8,128)S(1)}, u32[]{:S(2)}, u32[]{:S(2)}) collective-permute-start(f32[24,128]{1,0:T(8,128)S(1)} %get-tuple-element.56.x_ref), channel_id=1, source_target_pairs={{0,16},{4,20},{8,24},{12,28},{16,0},{20,4},{24,8},{28,12},{1,17},{... | collective-permute-start | bytes 36872 | tf_op jit(solution)/shard_map/ppermute | solution.py:542
  13.9 3.1 %copy-start.2 = (f32[24,128]{1,0:T(8,128)S(1)}, f32[24,128]{1,0:T(8,128)}, u32[]{:S(2)}) copy-start(f32[24,128]{1,0:T(8,128)} %dual_ref.1) | copy-start | bytes 36868
  13.9 3.1 %copy-start.3 = (f32[24,128]{1,0:T(8,128)S(1)}, f32[24,128]{1,0:T(8,128)}, u32[]{:S(2)}) copy-start(f32[24,128]{1,0:T(8,128)} %rhs_ref.3) | copy-start | bytes 36868
  13.9 4.0 %collective-permute-start.2 = (f32[40,128]{1,0:T(8,128)S(1)}, f32[40,128]{1,0:T(8,128)S(1)}, u32[]{:S(2)}, u32[]{:S(2)}) collective-permute-start(f32[40,128]{1,0:T(8,128)S(1)} %merge.6.x_ref), channel_id=1, source_target_pairs={{0,8},{4,12},{8,0},{12,4},{16,24},{20,28},{24,16},{28,20},{1,9},{5... | collective-permute-start | bytes 61448 | tf_op jit(solution)/shard_map/ppermute | solution.py:542
  15.8 1.2 %collective-permute-start.3 = (f32[24,128]{1,0:T(8,128)S(1)}, f32[24,128]{1,0:T(8,128)S(1)}, u32[]{:S(2)}, u32[]{:S(2)}) collective-permute-start(f32[24,128]{1,0:T(8,128)S(1)} %image.2.rest_0_.image_ref), channel_id=1, source_target_pairs={{0,1},{1,0},{2,3},{3,2},{4,5},{5,4},{6,7},{7,6},{8,9},{9,8},{10,11... | collective-permute-start | bytes 36872 | tf_op jit(solution)/shard_map/ppermute | solution.py:539
  17.9 4.1 %collective-permute-start.4 = (f32[88,128]{1,0:T(8,128)S(1)}, f32[88,128]{1,0:T(8,128)S(1)}, u32[]{:S(2)}, u32[]{:S(2)}) collective-permute-start(f32[88,128]{1,0:T(8,128)S(1)} %merge.7.x_ref), channel_id=1, source_target_pairs={{0,4},{4,0},{8,12},{12,8},{16,20},{20,16},{24,28},{28,24},{1,5},{5... | collective-permute-start | bytes 135176 | tf_op jit(solution)/shard_map/ppermute | solution.py:542
  19.6 4.1 %collective-permute-start.6 = (f32[96,128]{1,0:T(8,128)S(1)}, f32[96,128]{1,0:T(8,128)S(1)}, u32[]{:S(2)}, u32[]{:S(2)}) collective-permute-start(f32[96,128]{1,0:T(8,128)S(1)} %get-tuple-element.59.rest_0_.pieces_ref), channel_id=1, source_target_pairs={{2,0},{0,2},{3,1},{1,3},{6,4},{4,6},{7,5},{5,7},{10,8},{8,10},{11,... | collective-permute-start | bytes 147464 | tf_op jit(solution)/shard_map/ppermute | solution.py:535
  22.5 1.2 %collective-permute-start.5 = (f32[8,128]{1,0:T(8,128)S(1)}, f32[8,128]{1,0:T(8,128)S(1)}, u32[]{:S(2)}, u32[]{:S(2)}) collective-permute-start(f32[8,128]{1,0:T(8,128)S(1)} %get-tuple-element.64.sums_ref), channel_id=1, source_target_pairs={{0,1},{1,0},{2,3},{3,2},{4,5},{5,4},{6,7},{7,6},{8,9},{9,8},{10,11... | collective-permute-start | bytes 12296 | tf_op jit(solution)/shard_map/ppermute | solution.py:539
  24.1 4.7 %collective-permute-start.7 = (f32[24,128]{1,0:T(8,128)S(1)}, f32[24,128]{1,0:T(8,128)S(1)}, u32[]{:S(2)}, u32[]{:S(2)}) collective-permute-start(f32[24,128]{1,0:T(8,128)S(1)} %get-tuple-element.70.x_ref), channel_id=1, source_target_pairs={{0,16},{4,20},{8,24},{12,28},{16,0},{20,4},{24,8},{28,12},{1,17},{... | collective-permute-start | bytes 36872 | tf_op jit(solution)/shard_map/ppermute | solution.py:542
  28.8 3.8 %collective-permute-start.8 = (f32[40,128]{1,0:T(8,128)S(1)}, f32[40,128]{1,0:T(8,128)S(1)}, u32[]{:S(2)}, u32[]{:S(2)}) collective-permute-start(f32[40,128]{1,0:T(8,128)S(1)} %merge.9.x_ref), channel_id=1, source_target_pairs={{0,8},{4,12},{8,0},{12,4},{16,24},{20,28},{24,16},{28,20},{1,9},{5... | collective-permute-start | bytes 61448 | tf_op jit(solution)/shard_map/ppermute | solution.py:542
  32.6 4.1 %collective-permute-start.9 = (f32[80,128]{1,0:T(8,128)S(1)}, f32[80,128]{1,0:T(8,128)S(1)}, u32[]{:S(2)}, u32[]{:S(2)}) collective-permute-start(f32[80,128]{1,0:T(8,128)S(1)} %merge.10.x_ref), channel_id=1, source_target_pairs={{0,4},{4,0},{8,12},{12,8},{16,20},{20,16},{24,28},{28,24},{1,5},{5... | collective-permute-start | bytes 122888 | tf_op jit(solution)/shard_map/ppermute | solution.py:542
  34.3 3.0 %collective-permute-start.10 = (f32[24,128]{1,0:T(8,128)S(1)}, f32[24,128]{1,0:T(8,128)S(1)}, u32[]{:S(2)}, u32[]{:S(2)}) collective-permute-start(f32[24,128]{1,0:T(8,128)S(1)} %image.3.rest_0_.image_ref), channel_id=1, source_target_pairs={{0,1},{1,0},{2,3},{3,2},{4,5},{5,4},{6,7},{7,6},{8,9},{9,8},{10,11... | collective-permute-start | bytes 36872 | tf_op jit(solution)/shard_map/ppermute | solution.py:539
  37.1 1.2 %collective-permute-start.11 = (f32[8,128]{1,0:T(8,128)S(1)}, f32[8,128]{1,0:T(8,128)S(1)}, u32[]{:S(2)}, u32[]{:S(2)}) collective-permute-start(f32[8,128]{1,0:T(8,128)S(1)} %get-tuple-element.79.sums_ref), channel_id=1, source_target_pairs={{0,1},{1,0},{2,3},{3,2},{4,5},{5,4},{6,7},{7,6},{8,9},{9,8},{10,11... | collective-permute-start | bytes 12296 | tf_op jit(solution)/shard_map/ppermute | solution.py:539

commit v7 on v6

--- a/solution.py
+++ b/solution.py
@@ -687,7 +687,7 @@
         compiler_params=params(8),
         name="second",
     )(p1, pc, h1, hc, cb, ml1, an1, ids, wb, same, sums1, sums1b, pieces2, *others2)
-    half = S // 2
+    half = S * 5 // 12
 
     def place(first, count, whole, *into):
         cuts = max(p for p in (2, 1) if count % p == 0)

time: 39.1 us -> 39.1 us (level)
  no operation moved by 1% of the time
where the time goes in v7:
time: 39.1 us; the launch traced here: 38.9 us
  starting transfers between devices  17.6 us (45%)
  Pallas kernels  17.2 us (44%)
  waiting for transfers between devices  3.3 us (8%)
  between operations  0.81 us (2%)
    ppermute x6, starting transfers between devices, partner(): return lax.ppermute(x, 'scen', [(i, i ^ apart) for i in range(scens)])  12.7 us
    ppermute x2, starting transfers between devices, from_rows(): lax.ppermute(x, 'rows', [((i + q) % R, i) for i in range(R)])  4.5 us
    pallas_call x2, Pallas kernels, place(): pl.pallas_call(functools.partial(place_kernel, *static, first, count, cut...  3.99 us
    pallas_call x2, Pallas kernels, image_of(): pl.pallas_call(functools.partial(image_kernel, S, J, NZ), out_shape=near(...  3.46 us
    pallas_call x1, Pallas kernels, local(): pl.pallas_call(functools.partial(pieces_kernel, S, J, NZ), out_shape=[nea...  2.77 us
    pallas_call x1, Pallas kernels, local(): pl.pallas_call(functools.partial(setup_kernel, *static), out_shape=[near(...  2.04 us
    ppermute x6, waiting for transfers between devices, partner(): return lax.ppermute(x, 'scen', [(i, i ^ apart) for i in range(scens)])  1.7 us
    ppermute x2, waiting for transfers between devices, from_rows(): lax.ppermute(x, 'rows', [((i + q) % R, i) for i in range(R)])  1.12 us
  transfers between devices with their start and end apart: 12, of which 7 were waited for; matrix products, arithmetic and copies ran while one was open for 0% of the time, Pallas kernels for 33%

profile of v7, /device:TPU:0, one launch (start us, length us, event | category | flops | bytes accessed | tf_op | source)
XLA Modules:
  0.0 38.9 jit_solution(15385154460005210197)
XLA Ops:
  0.7 2.8 %pieces.1 = (f32[96,128]{1,0:T(8,128)S(1)}, bf16[24,4,128,128]{3,2,1,0:T(8,128)(2,1)S(1)}, bf16[24,352,128]{2,1,0:T(8,128)(2,1)S(1)}) custom-call(bf16[24,4,128,128]{3,2,1,0:T(8,128)(2,1)} %bitcast.39, f32[24,128]{1,0:T(8,128)} %dual_ref.1, bf16[24,352,128]{2,1,0:T(8,128)(2,1)} %bitcast.40), custom_call_target="tpu_custom_call" | custom-call | tf_op jit(solution)/shard_map/pieces/pallas_call | solution.py:568
  3.5 3.0 %collective-permute-start = (f32[96,128]{1,0:T(8,128)S(1)}, f32[96,128]{1,0:T(8,128)S(1)}, u32[]{:S(2)}, u32[]{:S(2)}) collective-permute-start(f32[96,128]{1,0:T(8,128)S(1)} %get-tuple-element.53.pieces_ref), channel_id=1, source_target_pairs={{2,0},{0,2},{3,1},{1,3},{6,4},{4,6},{7,5},{5,7},{10,8},{8,10},{11,... | collective-permute-start | bytes 147464 | tf_op jit(solution)/shard_map/ppermute | solution.py:535
  6.5 2.0 %setup.1 = (f32[192,128]{1,0:T(8,128)S(1)}, f32[192,128]{1,0:T(8,128)S(1)}, f32[192,128]{1,0:T(8,128)S(1)}, f32[192,128]{1,0:T(8,128)S(1)}, f32[192,128]{1,0:T(8...) custom-call(s32[3,24]{1,0:T(4,128)S(1)} %copy-done.5, ...), custom_call_target="tpu_custom_call" | custom-call | tf_op jit(solution)/shard_map/setup/pallas_call | solution.py:584
  8.5 0.4 first.1
  8.9 3.2 %collective-permute-start.1 = (f32[24,128]{1,0:T(8,128)S(1)}, f32[24,128]{1,0:T(8,128)S(1)}, u32[]{:S(2)}, u32[]{:S(2)}) collective-permute-start(f32[24,128]{1,0:T(8,128)S(1)} %get-tuple-element.56.x_ref), channel_id=1, source_target_pairs={{0,16},{4,20},{8,24},{12,28},{16,0},{20,4},{24,8},{28,12},{1,17},{... | collective-permute-start | bytes 36872 | tf_op jit(solution)/shard_map/ppermute | solution.py:542
  12.1 1.7 %image.2.rest_0_.image_ref = f32[24,128]{1,0:T(8,128)S(1)} custom-call(bf16[24,4,128,128]{3,2,1,0:T(8,128)(2,1)S(1)} %get-tuple-element.57.lp_ref, f32[96,128]{1,0:T(8,128)S(1)} %get-tuple-element.58.step_ref), custom_call_target="tpu_custom_call" | custom-call | tf_op jit(solution)/shard_map/image/pallas_call | solution.py:620
  13.9 1.9 %collective-permute-start.2 = (f32[40,128]{1,0:T(8,128)S(1)}, f32[40,128]{1,0:T(8,128)S(1)}, u32[]{:S(2)}, u32[]{:S(2)}) collective-permute-start(f32[40,128]{1,0:T(8,128)S(1)} %merge.6.x_ref), channel_id=1, source_target_pairs={{0,8},{4,12},{8,0},{12,4},{16,24},{20,28},{24,16},{28,20},{1,9},{5... | collective-permute-start | bytes 61448 | tf_op jit(solution)/shard_map/ppermute | solution.py:542
  15.8 1.0 %bulk.1.rest_1_.bulk_ref = f32[24,352,128]{2,1,0:T(8,128)S(1)} custom-call(bf16[24,352,128]{2,1,0:T(8,128)(2,1)S(1)} %get-tuple-element.42.primal_ref, bf16[24,352,128]{2,1,0:T(8,128)(2,1)S(1)} %bitcast.32), custom_call_target="tpu_custom_call" | custom-call | tf_op jit(solution)/shard_map/bulk/pallas_call | solution.py:646
  16.7 0.2 collective-permute-done.3.image2_ref
  16.9 0.9 %dual.1 = (f32[24,128]{1,0:T(8,128)S(1)}, f32[96,128]{1,0:T(8,128)S(1)}) custom-call(bf16[24,4,128,128]{3,2,1,0:T(8,128)(2,1)S(1)} %get-tuple-element.57.lp_ref, f32[24,128]{1,0:T(8,128)S(1)} %copy-done.2, f32[24,128]{1,0:T(8,128)S(1)} %copy-done.3, f32[24,128]{1,0:T(8,128)S(1)} %image.2.rest_0_.image_ref, f32[24,128]{1,0:T(8,128)S(1)} %collective-permute-done.3.image2_ref), custom_call_target="tpu_custom_call" | custom-call | tf_op jit(solution)/shard_map/dual/pallas_call | solution.py:654
  17.9 1.7 %collective-permute-start.4 = (f32[88,128]{1,0:T(8,128)S(1)}, f32[88,128]{1,0:T(8,128)S(1)}, u32[]{:S(2)}, u32[]{:S(2)}) collective-permute-start(f32[88,128]{1,0:T(8,128)S(1)} %merge.7.x_ref), channel_id=1, source_target_pairs={{0,4},{4,0},{8,12},{12,8},{16,20},{20,16},{24,28},{28,24},{1,5},{5... | collective-permute-start | bytes 135176 | tf_op jit(solution)/shard_map/ppermute | solution.py:542
  19.6 1.5 %collective-permute-start.6 = (f32[96,128]{1,0:T(8,128)S(1)}, f32[96,128]{1,0:T(8,128)S(1)}, u32[]{:S(2)}, u32[]{:S(2)}) collective-permute-start(f32[96,128]{1,0:T(8,128)S(1)} %get-tuple-element.59.rest_0_.pieces_ref), channel_id=1, source_target_pairs={{2,0},{0,2},{3,1},{1,3},{6,4},{4,6},{7,5},{5,7},{10,8},{8,10},{11,... | collective-permute-start | bytes 147464 | tf_op jit(solution)/shard_map/ppermute | solution.py:535
  21.1 1.0 %collective-permute-done.4.y_ref = f32[88,128]{1,0:T(8,128)S(1)} collective-permute-done((f32[88,128]{1,0:T(8,128)S(1)}, f32[88,128]{1,0:T(8,128)S(1)}, u32[]{:S(2)}, u32[]{:S(2)}) %collective-permute-start.4) | collective-permute-done | bytes 45088 | tf_op jit(solution)/shard_map/ppermute | solution.py:542
  22.0 0.4 %nodes.1 = (f32[192,128]{1,0:T(8,128)S(1)}, f32[192,128]{1,0:T(8,128)S(1)}, f32[4,32,128]{2,1,0:T(8,128)S(1)}, f32[8,128]{1,0:T(8,128)S(1)}) custom-call(f32[152,128]{1,0:T(8,128)S(1)} %merge.8.got_ref, f32[48,128]{1,0:T(8,128)S(1)} %get-tuple-element.50.id_ref, f32[192,128]{1,0:T(8,128)S(1)} %get-tuple-element.60.mu_ref, ...), custom_call_target="tpu_custom_call" | custom-call | tf_op jit(solution)/shard_map/nodes/pallas_call | solution.py:668
  22.5 0.1 collective-permute-start.5
  22.5 1.1 %collective-permute-done.6.rest_0_ = f32[96,128]{1,0:T(8,128)S(1)} collective-permute-done((f32[96,128]{1,0:T(8,128)S(1)}, f32[96,128]{1,0:T(8,128)S(1)}, u32[]{:S(2)}, u32[]{:S(2)}) %collective-permute-start.6) | collective-permute-done | bytes 49184 | tf_op jit(solution)/shard_map/ppermute | solution.py:535
  23.7 0.0 collective-permute-done.5.sums2_ref
  23.7 0.4 %second.1 = (f32[192,128]{1,0:T(8,128)S(1)}, f32[192,128]{1,0:T(8,128)S(1)}, f32[192,128]{1,0:T(8,128)S(1)}, f32[24,128]{1,0:T(8,128)S(1)}, f32[96,128]{1,0:T(8,128)S(1)}, /*index=5*/f32[8,128]{1,0:T(8,128)S(1)}) custom-call(f32[192,128]{1,0:T(8,128)S(1)} %get-tuple-element.54.pp_ref, f32[192,128]{1,0:T(8,128)S(1)} %get-tuple-element.44.pc_ref, ...), custom_call_target="tpu_custom_call" | custom-call | tf_op jit(solution)/shard_map/second/pallas_call | solution.py:681
  24.1 2.7 %collective-permute-start.7 = (f32[24,128]{1,0:T(8,128)S(1)}, f32[24,128]{1,0:T(8,128)S(1)}, u32[]{:S(2)}, u32[]{:S(2)}) collective-permute-start(f32[24,128]{1,0:T(8,128)S(1)} %get-tuple-element.70.x_ref), channel_id=1, source_target_pairs={{0,16},{4,20},{8,24},{12,28},{16,0},{20,4},{24,8},{28,12},{1,17},{... | collective-permute-start | bytes 36872 | tf_op jit(solution)/shard_map/ppermute | solution.py:542
  26.9 1.7 %image.3.rest_0_.image_ref = f32[24,128]{1,0:T(8,128)S(1)} custom-call(bf16[24,4,128,128]{3,2,1,0:T(8,128)(2,1)S(1)} %get-tuple-element.57.lp_ref, f32[96,128]{1,0:T(8,128)S(1)} %get-tuple-element.71.step_ref), custom_call_target="tpu_custom_call" | custom-call | tf_op jit(solution)/shard_map/image/pallas_call | solution.py:620
  28.6 0.2 collective-permute-done.7.y_ref
  28.8 1.6 %collective-permute-start.8 = (f32[40,128]{1,0:T(8,128)S(1)}, f32[40,128]{1,0:T(8,128)S(1)}, u32[]{:S(2)}, u32[]{:S(2)}) collective-permute-start(f32[40,128]{1,0:T(8,128)S(1)} %merge.9.x_ref), channel_id=1, source_target_pairs={{0,8},{4,12},{8,0},{12,4},{16,24},{20,28},{24,16},{28,20},{1,9},{5... | collective-permute-start | bytes 61448 | tf_op jit(solution)/shard_map/ppermute | solution.py:542
  30.4 1.9 %place.2 = (f32[24,352,128]{2,1,0:T(8,128)S(1)}, f32[24,352,128]{2,1,0:T(8,128)}) custom-call(s32[2,2,2,24]{3,2,1,0:T(2,128)S(1)} %bitcast.35, f32[24,352,128]{2,1,0:T(8,128)S(1)} %bulk.1.rest_1_.bulk_ref, f32[192,128]{1,0:T(8,128)S(1)} %get-tuple-element.65.p_ref, f32[192,128]{1,0:T(8,128)S(1)} %get-tuple-element.66.h_ref), custom_call_target="tpu_custom_call", output_to_operand_aliasing={{0}: (1, {})} | custom-call | tf_op jit(solution)/shard_map/place/pallas_call | solution.py:694
  32.3 0.3 collective-permute-done.8.y_ref
  32.6 1.7 %collective-permute-start.9 = (f32[80,128]{1,0:T(8,128)S(1)}, f32[80,128]{1,0:T(8,128)S(1)}, u32[]{:S(2)}, u32[]{:S(2)}) collective-permute-start(f32[80,128]{1,0:T(8,128)S(1)} %merge.10.x_ref), channel_id=1, source_target_pairs={{0,4},{4,0},{8,12},{12,8},{16,20},{20,16},{24,28},{28,24},{1,5},{5... | collective-permute-start | bytes 122888 | tf_op jit(solution)/shard_map/ppermute | solution.py:542
  34.3 2.1 %place.3 = (f32[24,352,128]{2,1,0:T(8,128)S(1)}, f32[24,352,128]{2,1,0:T(8,128)}) custom-call(s32[2,2,2,24]{3,2,1,0:T(2,128)S(1)} %bitcast.36, f32[24,352,128]{2,1,0:T(8,128)S(1)} %get-tuple-element.67.bulk_ref, f32[192,128]{1,0:T(8,128)S(1)} %get-tuple-element.65.p_ref, ...), custom_call_target="tpu_custom_call", output_to_operand_aliasing={{0}: (1, {}), {1}: (4, {})} | custom-call | tf_op jit(solution)/shard_map/place/pallas_call | solution.py:694
  36.4 0.3 collective-permute-done.9.y_ref
  36.7 0.4 %last.1 = (f32[192,128]{1,0:T(8,128)S(1)}, f32[8,128]{1,0:T(8,128)S(1)}) custom-call(f32[152,128]{1,0:T(8,128)S(1)} %merge.11.got_ref, f32[48,128]{1,0:T(8,128)S(1)} %get-tuple-element.50.id_ref, f32[4,32,128]{2,1,0:T(8,128)S(1)} %get-tuple-element.72.ent_ref, f32[192,128]{1,0:T(8,128)S(1)} %get-tuple-element.73.mu_ref, ...), custom_call_target="tpu_custom_call" | custom-call | tf_op jit(solution)/shard_map/last/pallas_call | solution.py:719
  37.1 0.3 collective-permute-start.11
  37.4 0.7 %finish.1 = (f32[192,128]{1,0:T(8,128)}, f32[24,128]{1,0:T(8,128)}) custom-call(f32[192,128]{1,0:T(8,128)S(1)} %get-tuple-element.75.ml_ref, f32[24,128]{1,0:T(8,128)S(1)} %get-tuple-element.76.dual_ref, f32[24,128]{1,0:T(8,128)S(1)} %copy-done.3, f32[24,128]{1,0:T(8,128)S(1)} %image.3.rest_0_.image_ref, f32[24,128]{1,0:T(8,128)S(1)} %collective-permute-done.10.image2_ref), custom_call_target="tpu_custom_call" | custom-call | tf_op jit(solution)/shard_map/finish/pallas_call | solution.py:727
  38.1 0.2 collective-permute-done.11.sums2_ref
  38.3 0.6 %penalty.1 = f32[1,1]{1,0:T(1,128)} custom-call(f32[8,128]{1,0:T(8,128)S(1)} %get-tuple-element.74.pen_ref, f32[8,128]{1,0:T(8,128)S(1)} %get-tuple-element.79.sums_ref, f32[8,128]{1,0:T(8,128)S(1)} %collective-permute-done.11.sums2_ref), custom_call_target="tpu_custom_call" | custom-call | tf_op jit(solution)/shard_map/penalty/pallas_call | solution.py:735
  (26 shorter events, 0.1 us)
Async XLA Ops:
  0.6 5.8 %copy-start = (bf16[24,2,22528]{2,1,0:T(2,128)(2,1)S(1)}, bf16[24,2,22528]{2,1,0:T(2,128)(2,1)}, u32[]{:S(2)}) copy-start(bf16[24,2,22528]{2,1,0:T(2,128)(2,1)} %param.14) | copy-start | bytes 6488068
  0.6 5.8 %copy-start.1 = (f32[24,2,512]{2,1,0:T(2,128)S(1)}, f32[24,2,512]{2,1,0:T(2,128)}, u32[]{:S(2)}) copy-start(f32[24,2,512]{2,1,0:T(2,128)} %param.18) | copy-start | bytes 294916
  0.7 5.8 %copy-start.6 = (f32[24]{0:T(128)S(1)}, f32[24]{0:T(128)}, u32[]{:S(2)}) copy-start(f32[24]{0:T(128)} %param.13) | copy-start | bytes 292
  0.7 5.8 %copy-start.4 = (s32[24,2,2,2]{0,3,2,1:T(2,128)S(1)}, s32[24,2,2,2]{0,3,2,1:T(2,128)}, u32[]{:S(2)}) copy-start(s32[24,2,2,2]{0,3,2,1:T(2,128)} %param.11) | copy-start | bytes 2308
  0.7 5.8 %copy-start.5 = (s32[3,24]{1,0:T(4,128)S(1)}, s32[3,24]{1,0:T(4,128)}, u32[]{:S(2)}) copy-start(s32[3,24]{1,0:T(4,128)} %nodes_ref.1) | copy-start | bytes 868
  3.5 5.1 %collective-permute-start = (f32[96,128]{1,0:T(8,128)S(1)}, f32[96,128]{1,0:T(8,128)S(1)}, u32[]{:S(2)}, u32[]{:S(2)}) collective-permute-start(f32[96,128]{1,0:T(8,128)S(1)} %get-tuple-element.53.pieces_ref), channel_id=1, source_target_pairs={{2,0},{0,2},{3,1},{1,3},{6,4},{4,6},{7,5},{5,7},{10,8},{8,10},{11,... | collective-permute-start | bytes 147464 | tf_op jit(solution)/shard_map/ppermute | solution.py:535
  8.9 4.9 %collective-permute-start.1 = (f32[24,128]{1,0:T(8,128)S(1)}, f32[24,128]{1,0:T(8,128)S(1)}, u32[]{:S(2)}, u32[]{:S(2)}) collective-permute-start(f32[24,128]{1,0:T(8,128)S(1)} %get-tuple-element.56.x_ref), channel_id=1, source_target_pairs={{0,16},{4,20},{8,24},{12,28},{16,0},{20,4},{24,8},{28,12},{1,17},{... | collective-permute-start | bytes 36872 | tf_op jit(solution)/shard_map/ppermute | solution.py:542
  13.9 3.1 %copy-start.2 = (f32[24,128]{1,0:T(8,128)S(1)}, f32[24,128]{1,0:T(8,128)}, u32[]{:S(2)}) copy-start(f32[24,128]{1,0:T(8,128)} %dual_ref.1) | copy-start | bytes 36868
  13.9 3.1 %copy-start.3 = (f32[24,128]{1,0:T(8,128)S(1)}, f32[24,128]{1,0:T(8,128)}, u32[]{:S(2)}) copy-start(f32[24,128]{1,0:T(8,128)} %rhs_ref.3) | copy-start | bytes 36868
  13.9 4.0 %collective-permute-start.2 = (f32[40,128]{1,0:T(8,128)S(1)}, f32[40,128]{1,0:T(8,128)S(1)}, u32[]{:S(2)}, u32[]{:S(2)}) collective-permute-start(f32[40,128]{1,0:T(8,128)S(1)} %merge.6.x_ref), channel_id=1, source_target_pairs={{0,8},{4,12},{8,0},{12,4},{16,24},{20,28},{24,16},{28,20},{1,9},{5... | collective-permute-start | bytes 61448 | tf_op jit(solution)/shard_map/ppermute | solution.py:542
  15.8 1.2 %collective-permute-start.3 = (f32[24,128]{1,0:T(8,128)S(1)}, f32[24,128]{1,0:T(8,128)S(1)}, u32[]{:S(2)}, u32[]{:S(2)}) collective-permute-start(f32[24,128]{1,0:T(8,128)S(1)} %image.2.rest_0_.image_ref), channel_id=1, source_target_pairs={{0,1},{1,0},{2,3},{3,2},{4,5},{5,4},{6,7},{7,6},{8,9},{9,8},{10,11... | collective-permute-start | bytes 36872 | tf_op jit(solution)/shard_map/ppermute | solution.py:539
  17.9 4.1 %collective-permute-start.4 = (f32[88,128]{1,0:T(8,128)S(1)}, f32[88,128]{1,0:T(8,128)S(1)}, u32[]{:S(2)}, u32[]{:S(2)}) collective-permute-start(f32[88,128]{1,0:T(8,128)S(1)} %merge.7.x_ref), channel_id=1, source_target_pairs={{0,4},{4,0},{8,12},{12,8},{16,20},{20,16},{24,28},{28,24},{1,5},{5... | collective-permute-start | bytes 135176 | tf_op jit(solution)/shard_map/ppermute | solution.py:542
  19.6 4.1 %collective-permute-start.6 = (f32[96,128]{1,0:T(8,128)S(1)}, f32[96,128]{1,0:T(8,128)S(1)}, u32[]{:S(2)}, u32[]{:S(2)}) collective-permute-start(f32[96,128]{1,0:T(8,128)S(1)} %get-tuple-element.59.rest_0_.pieces_ref), channel_id=1, source_target_pairs={{2,0},{0,2},{3,1},{1,3},{6,4},{4,6},{7,5},{5,7},{10,8},{8,10},{11,... | collective-permute-start | bytes 147464 | tf_op jit(solution)/shard_map/ppermute | solution.py:535
  22.5 1.2 %collective-permute-start.5 = (f32[8,128]{1,0:T(8,128)S(1)}, f32[8,128]{1,0:T(8,128)S(1)}, u32[]{:S(2)}, u32[]{:S(2)}) collective-permute-start(f32[8,128]{1,0:T(8,128)S(1)} %get-tuple-element.64.sums_ref), channel_id=1, source_target_pairs={{0,1},{1,0},{2,3},{3,2},{4,5},{5,4},{6,7},{7,6},{8,9},{9,8},{10,11... | collective-permute-start | bytes 12296 | tf_op jit(solution)/shard_map/ppermute | solution.py:539
  24.1 4.7 %collective-permute-start.7 = (f32[24,128]{1,0:T(8,128)S(1)}, f32[24,128]{1,0:T(8,128)S(1)}, u32[]{:S(2)}, u32[]{:S(2)}) collective-permute-start(f32[24,128]{1,0:T(8,128)S(1)} %get-tuple-element.70.x_ref), channel_id=1, source_target_pairs={{0,16},{4,20},{8,24},{12,28},{16,0},{20,4},{24,8},{28,12},{1,17},{... | collective-permute-start | bytes 36872 | tf_op jit(solution)/shard_map/ppermute | solution.py:542
  28.8 3.8 %collective-permute-start.8 = (f32[40,128]{1,0:T(8,128)S(1)}, f32[40,128]{1,0:T(8,128)S(1)}, u32[]{:S(2)}, u32[]{:S(2)}) collective-permute-start(f32[40,128]{1,0:T(8,128)S(1)} %merge.9.x_ref), channel_id=1, source_target_pairs={{0,8},{4,12},{8,0},{12,4},{16,24},{20,28},{24,16},{28,20},{1,9},{5... | collective-permute-start | bytes 61448 | tf_op jit(solution)/shard_map/ppermute | solution.py:542
  32.6 4.1 %collective-permute-start.9 = (f32[80,128]{1,0:T(8,128)S(1)}, f32[80,128]{1,0:T(8,128)S(1)}, u32[]{:S(2)}, u32[]{:S(2)}) collective-permute-start(f32[80,128]{1,0:T(8,128)S(1)} %merge.10.x_ref), channel_id=1, source_target_pairs={{0,4},{4,0},{8,12},{12,8},{16,20},{20,16},{24,28},{28,24},{1,5},{5... | collective-permute-start | bytes 122888 | tf_op jit(solution)/shard_map/ppermute | solution.py:542
  34.3 3.2 %collective-permute-start.10 = (f32[24,128]{1,0:T(8,128)S(1)}, f32[24,128]{1,0:T(8,128)S(1)}, u32[]{:S(2)}, u32[]{:S(2)}) collective-permute-start(f32[24,128]{1,0:T(8,128)S(1)} %image.3.rest_0_.image_ref), channel_id=1, source_target_pairs={{0,1},{1,0},{2,3},{3,2},{4,5},{5,4},{6,7},{7,6},{8,9},{9,8},{10,11... | collective-permute-start | bytes 36872 | tf_op jit(solution)/shard_map/ppermute | solution.py:539
  37.1 1.2 %collective-permute-start.11 = (f32[8,128]{1,0:T(8,128)S(1)}, f32[8,128]{1,0:T(8,128)S(1)}, u32[]{:S(2)}, u32[]{:S(2)}) collective-permute-start(f32[8,128]{1,0:T(8,128)S(1)} %get-tuple-element.79.sums_ref), channel_id=1, source_target_pairs={{0,1},{1,0},{2,3},{3,2},{4,5},{5,4},{6,7},{7,6},{8,9},{9,8},{10,11... | collective-permute-start | bytes 12296 | tf_op jit(solution)/shard_map/ppermute | solution.py:539

commit v8 on v6

--- a/solution.py
+++ b/solution.py
@@ -447,7 +447,7 @@
 
 
 def penalty_kernel(pen_ref, sums_ref, sums2_ref, out_ref):
-    out_ref[...] = scaled(pen_ref[0:1, 0:1], sums_ref, [sums2_ref])
+    out_ref[0, 0] = scaled(pen_ref[0:1, 0:1], sums_ref, [sums2_ref])[0, 0]
 
 
 def bulk_kernel(S, primal_ref, cost_ref, out_ref):
@@ -736,7 +736,7 @@
         penalty_kernel,
         out_shape=shape(1, 1),
         in_specs=[VMEM] * 3,
-        out_specs=VMEM,
+        out_specs=SMEM,
         compiler_params=params(4),
         name="penalty",
     )(pen1, sums2, from_section(sums2))

time: 39.1 us -> 39.1 us (level)
  no operation moved by 1% of the time
where the time goes in v8:
time: 39.1 us; the launch traced here: 39 us
  starting transfers between devices  17.5 us (45%)
  Pallas kernels  17.2 us (44%)
  waiting for transfers between devices  3.42 us (9%)
  between operations  0.81 us (2%)
    ppermute x6, starting transfers between devices, partner(): return lax.ppermute(x, 'scen', [(i, i ^ apart) for i in range(scens)])  12.7 us
    ppermute x2, starting transfers between devices, from_rows(): lax.ppermute(x, 'rows', [((i + q) % R, i) for i in range(R)])  4.5 us
    pallas_call x2, Pallas kernels, place(): pl.pallas_call(functools.partial(place_kernel, *static, first, count, cut...  3.99 us
    pallas_call x2, Pallas kernels, image_of(): pl.pallas_call(functools.partial(image_kernel, S, J, NZ), out_shape=near(...  3.46 us
    pallas_call x1, Pallas kernels, local(): pl.pallas_call(functools.partial(pieces_kernel, S, J, NZ), out_shape=[nea...  2.77 us
    pallas_call x1, Pallas kernels, local(): pl.pallas_call(functools.partial(setup_kernel, *static), out_shape=[near(...  2.04 us
    ppermute x6, waiting for transfers between devices, partner(): return lax.ppermute(x, 'scen', [(i, i ^ apart) for i in range(scens)])  1.7 us
    ppermute x2, waiting for transfers between devices, from_rows(): lax.ppermute(x, 'rows', [((i + q) % R, i) for i in range(R)])  1.12 us
  transfers between devices with their start and end apart: 12, of which 7 were waited for; matrix products, arithmetic and copies ran while one was open for 0% of the time, Pallas kernels for 33%

profile of v8, /device:TPU:0, one launch (start us, length us, event | category | flops | bytes accessed | tf_op | source)
XLA Modules:
  0.0 39.0 jit_solution(16961534224915509171)
XLA Ops:
  0.7 2.8 %pieces.1 = (f32[96,128]{1,0:T(8,128)S(1)}, bf16[24,4,128,128]{3,2,1,0:T(8,128)(2,1)S(1)}, bf16[24,352,128]{2,1,0:T(8,128)(2,1)S(1)}) custom-call(bf16[24,4,128,128]{3,2,1,0:T(8,128)(2,1)} %bitcast.39, f32[24,128]{1,0:T(8,128)} %dual_ref.1, bf16[24,352,128]{2,1,0:T(8,128)(2,1)} %bitcast.40), custom_call_target="tpu_custom_call" | custom-call | tf_op jit(solution)/shard_map/pieces/pallas_call | solution.py:568
  3.5 3.0 %collective-permute-start = (f32[96,128]{1,0:T(8,128)S(1)}, f32[96,128]{1,0:T(8,128)S(1)}, u32[]{:S(2)}, u32[]{:S(2)}) collective-permute-start(f32[96,128]{1,0:T(8,128)S(1)} %get-tuple-element.53.pieces_ref), channel_id=1, source_target_pairs={{2,0},{0,2},{3,1},{1,3},{6,4},{4,6},{7,5},{5,7},{10,8},{8,10},{11,... | collective-permute-start | bytes 147464 | tf_op jit(solution)/shard_map/ppermute | solution.py:535
  6.5 2.0 %setup.1 = (f32[192,128]{1,0:T(8,128)S(1)}, f32[192,128]{1,0:T(8,128)S(1)}, f32[192,128]{1,0:T(8,128)S(1)}, f32[192,128]{1,0:T(8,128)S(1)}, f32[192,128]{1,0:T(8...) custom-call(s32[3,24]{1,0:T(4,128)S(1)} %copy-done.5, ...), custom_call_target="tpu_custom_call" | custom-call | tf_op jit(solution)/shard_map/setup/pallas_call | solution.py:584
  8.5 0.4 first.1
  8.9 3.2 %collective-permute-start.1 = (f32[24,128]{1,0:T(8,128)S(1)}, f32[24,128]{1,0:T(8,128)S(1)}, u32[]{:S(2)}, u32[]{:S(2)}) collective-permute-start(f32[24,128]{1,0:T(8,128)S(1)} %get-tuple-element.56.x_ref), channel_id=1, source_target_pairs={{0,16},{4,20},{8,24},{12,28},{16,0},{20,4},{24,8},{28,12},{1,17},{... | collective-permute-start | bytes 36872 | tf_op jit(solution)/shard_map/ppermute | solution.py:542
  12.1 1.7 %image.2.rest_0_.image_ref = f32[24,128]{1,0:T(8,128)S(1)} custom-call(bf16[24,4,128,128]{3,2,1,0:T(8,128)(2,1)S(1)} %get-tuple-element.57.lp_ref, f32[96,128]{1,0:T(8,128)S(1)} %get-tuple-element.58.step_ref), custom_call_target="tpu_custom_call" | custom-call | tf_op jit(solution)/shard_map/image/pallas_call | solution.py:620
  13.9 1.9 %collective-permute-start.2 = (f32[40,128]{1,0:T(8,128)S(1)}, f32[40,128]{1,0:T(8,128)S(1)}, u32[]{:S(2)}, u32[]{:S(2)}) collective-permute-start(f32[40,128]{1,0:T(8,128)S(1)} %merge.6.x_ref), channel_id=1, source_target_pairs={{0,8},{4,12},{8,0},{12,4},{16,24},{20,28},{24,16},{28,20},{1,9},{5... | collective-permute-start | bytes 61448 | tf_op jit(solution)/shard_map/ppermute | solution.py:542
  15.8 1.0 %bulk.1.rest_1_.bulk_ref = f32[24,352,128]{2,1,0:T(8,128)S(1)} custom-call(bf16[24,352,128]{2,1,0:T(8,128)(2,1)S(1)} %get-tuple-element.42.primal_ref, bf16[24,352,128]{2,1,0:T(8,128)(2,1)S(1)} %bitcast.32), custom_call_target="tpu_custom_call" | custom-call | tf_op jit(solution)/shard_map/bulk/pallas_call | solution.py:646
  16.7 0.2 collective-permute-done.3.image2_ref
  16.9 0.9 %dual.1 = (f32[24,128]{1,0:T(8,128)S(1)}, f32[96,128]{1,0:T(8,128)S(1)}) custom-call(bf16[24,4,128,128]{3,2,1,0:T(8,128)(2,1)S(1)} %get-tuple-element.57.lp_ref, f32[24,128]{1,0:T(8,128)S(1)} %copy-done.2, f32[24,128]{1,0:T(8,128)S(1)} %copy-done.3, f32[24,128]{1,0:T(8,128)S(1)} %image.2.rest_0_.image_ref, f32[24,128]{1,0:T(8,128)S(1)} %collective-permute-done.3.image2_ref), custom_call_target="tpu_custom_call" | custom-call | tf_op jit(solution)/shard_map/dual/pallas_call | solution.py:654
  17.9 1.7 %collective-permute-start.4 = (f32[88,128]{1,0:T(8,128)S(1)}, f32[88,128]{1,0:T(8,128)S(1)}, u32[]{:S(2)}, u32[]{:S(2)}) collective-permute-start(f32[88,128]{1,0:T(8,128)S(1)} %merge.7.x_ref), channel_id=1, source_target_pairs={{0,4},{4,0},{8,12},{12,8},{16,20},{20,16},{24,28},{28,24},{1,5},{5... | collective-permute-start | bytes 135176 | tf_op jit(solution)/shard_map/ppermute | solution.py:542
  19.6 1.5 %collective-permute-start.6 = (f32[96,128]{1,0:T(8,128)S(1)}, f32[96,128]{1,0:T(8,128)S(1)}, u32[]{:S(2)}, u32[]{:S(2)}) collective-permute-start(f32[96,128]{1,0:T(8,128)S(1)} %get-tuple-element.59.rest_0_.pieces_ref), channel_id=1, source_target_pairs={{2,0},{0,2},{3,1},{1,3},{6,4},{4,6},{7,5},{5,7},{10,8},{8,10},{11,... | collective-permute-start | bytes 147464 | tf_op jit(solution)/shard_map/ppermute | solution.py:535
  21.1 1.0 %collective-permute-done.4.y_ref = f32[88,128]{1,0:T(8,128)S(1)} collective-permute-done((f32[88,128]{1,0:T(8,128)S(1)}, f32[88,128]{1,0:T(8,128)S(1)}, u32[]{:S(2)}, u32[]{:S(2)}) %collective-permute-start.4) | collective-permute-done | bytes 45088 | tf_op jit(solution)/shard_map/ppermute | solution.py:542
  22.0 0.4 %nodes.1 = (f32[192,128]{1,0:T(8,128)S(1)}, f32[192,128]{1,0:T(8,128)S(1)}, f32[4,32,128]{2,1,0:T(8,128)S(1)}, f32[8,128]{1,0:T(8,128)S(1)}) custom-call(f32[152,128]{1,0:T(8,128)S(1)} %merge.8.got_ref, f32[48,128]{1,0:T(8,128)S(1)} %get-tuple-element.50.id_ref, f32[192,128]{1,0:T(8,128)S(1)} %get-tuple-element.60.mu_ref, ...), custom_call_target="tpu_custom_call" | custom-call | tf_op jit(solution)/shard_map/nodes/pallas_call | solution.py:668
  22.5 0.1 collective-permute-start.5
  22.5 1.1 %collective-permute-done.6.rest_0_ = f32[96,128]{1,0:T(8,128)S(1)} collective-permute-done((f32[96,128]{1,0:T(8,128)S(1)}, f32[96,128]{1,0:T(8,128)S(1)}, u32[]{:S(2)}, u32[]{:S(2)}) %collective-permute-start.6) | collective-permute-done | bytes 49184 | tf_op jit(solution)/shard_map/ppermute | solution.py:535
  23.7 0.0 collective-permute-done.5.sums2_ref
  23.7 0.4 %second.1 = (f32[192,128]{1,0:T(8,128)S(1)}, f32[192,128]{1,0:T(8,128)S(1)}, f32[192,128]{1,0:T(8,128)S(1)}, f32[24,128]{1,0:T(8,128)S(1)}, f32[96,128]{1,0:T(8,128)S(1)}, /*index=5*/f32[8,128]{1,0:T(8,128)S(1)}) custom-call(f32[192,128]{1,0:T(8,128)S(1)} %get-tuple-element.54.pp_ref, f32[192,128]{1,0:T(8,128)S(1)} %get-tuple-element.44.pc_ref, ...), custom_call_target="tpu_custom_call" | custom-call | tf_op jit(solution)/shard_map/second/pallas_call | solution.py:681
  24.1 2.7 %collective-permute-start.7 = (f32[24,128]{1,0:T(8,128)S(1)}, f32[24,128]{1,0:T(8,128)S(1)}, u32[]{:S(2)}, u32[]{:S(2)}) collective-permute-start(f32[24,128]{1,0:T(8,128)S(1)} %get-tuple-element.70.x_ref), channel_id=1, source_target_pairs={{0,16},{4,20},{8,24},{12,28},{16,0},{20,4},{24,8},{28,12},{1,17},{... | collective-permute-start | bytes 36872 | tf_op jit(solution)/shard_map/ppermute | solution.py:542
  26.9 1.7 %image.3.rest_0_.image_ref = f32[24,128]{1,0:T(8,128)S(1)} custom-call(bf16[24,4,128,128]{3,2,1,0:T(8,128)(2,1)S(1)} %get-tuple-element.57.lp_ref, f32[96,128]{1,0:T(8,128)S(1)} %get-tuple-element.71.step_ref), custom_call_target="tpu_custom_call" | custom-call | tf_op jit(solution)/shard_map/image/pallas_call | solution.py:620
  28.6 0.2 collective-permute-done.7.y_ref
  28.8 1.6 %collective-permute-start.8 = (f32[40,128]{1,0:T(8,128)S(1)}, f32[40,128]{1,0:T(8,128)S(1)}, u32[]{:S(2)}, u32[]{:S(2)}) collective-permute-start(f32[40,128]{1,0:T(8,128)S(1)} %merge.9.x_ref), channel_id=1, source_target_pairs={{0,8},{4,12},{8,0},{12,4},{16,24},{20,28},{24,16},{28,20},{1,9},{5... | collective-permute-start | bytes 61448 | tf_op jit(solution)/shard_map/ppermute | solution.py:542
  30.4 2.0 %place.2 = (f32[24,352,128]{2,1,0:T(8,128)S(1)}, f32[24,352,128]{2,1,0:T(8,128)}) custom-call(s32[2,2,2,24]{3,2,1,0:T(2,128)S(1)} %bitcast.35, f32[24,352,128]{2,1,0:T(8,128)S(1)} %bulk.1.rest_1_.bulk_ref, f32[192,128]{1,0:T(8,128)S(1)} %get-tuple-element.65.p_ref, f32[192,128]{1,0:T(8,128)S(1)} %get-tuple-element.66.h_ref), custom_call_target="tpu_custom_call", output_to_operand_aliasing={{0}: (1, {})} | custom-call | tf_op jit(solution)/shard_map/place/pallas_call | solution.py:694
  32.5 0.1 collective-permute-done.8.y_ref
  32.6 1.7 %collective-permute-start.9 = (f32[80,128]{1,0:T(8,128)S(1)}, f32[80,128]{1,0:T(8,128)S(1)}, u32[]{:S(2)}, u32[]{:S(2)}) collective-permute-start(f32[80,128]{1,0:T(8,128)S(1)} %merge.10.x_ref), channel_id=1, source_target_pairs={{0,4},{4,0},{8,12},{12,8},{16,20},{20,16},{24,28},{28,24},{1,5},{5... | collective-permute-start | bytes 122888 | tf_op jit(solution)/shard_map/ppermute | solution.py:542
  34.3 2.0 %place.3 = (f32[24,352,128]{2,1,0:T(8,128)S(1)}, f32[24,352,128]{2,1,0:T(8,128)}) custom-call(s32[2,2,2,24]{3,2,1,0:T(2,128)S(1)} %bitcast.36, f32[24,352,128]{2,1,0:T(8,128)S(1)} %get-tuple-element.67.bulk_ref, f32[192,128]{1,0:T(8,128)S(1)} %get-tuple-element.65.p_ref, ...), custom_call_target="tpu_custom_call", output_to_operand_aliasing={{0}: (1, {}), {1}: (4, {})} | custom-call | tf_op jit(solution)/shard_map/place/pallas_call | solution.py:694
  36.3 0.4 %collective-permute-done.9.y_ref = f32[80,128]{1,0:T(8,128)S(1)} collective-permute-done((f32[80,128]{1,0:T(8,128)S(1)}, f32[80,128]{1,0:T(8,128)S(1)}, u32[]{:S(2)}, u32[]{:S(2)}) %collective-permute-start.9) | collective-permute-done | bytes 40992 | tf_op jit(solution)/shard_map/ppermute | solution.py:542
  36.7 0.4 %last.1 = (f32[192,128]{1,0:T(8,128)S(1)}, f32[8,128]{1,0:T(8,128)S(1)}) custom-call(f32[152,128]{1,0:T(8,128)S(1)} %merge.11.got_ref, f32[48,128]{1,0:T(8,128)S(1)} %get-tuple-element.50.id_ref, f32[4,32,128]{2,1,0:T(8,128)S(1)} %get-tuple-element.72.ent_ref, f32[192,128]{1,0:T(8,128)S(1)} %get-tuple-element.73.mu_ref, ...), custom_call_target="tpu_custom_call" | custom-call | tf_op jit(solution)/shard_map/last/pallas_call | solution.py:719
  37.1 0.2 collective-permute-start.11
  37.3 0.7 %finish.1 = (f32[192,128]{1,0:T(8,128)}, f32[24,128]{1,0:T(8,128)}) custom-call(f32[192,128]{1,0:T(8,128)S(1)} %get-tuple-element.75.ml_ref, f32[24,128]{1,0:T(8,128)S(1)} %get-tuple-element.76.dual_ref, f32[24,128]{1,0:T(8,128)S(1)} %copy-done.3, f32[24,128]{1,0:T(8,128)S(1)} %image.3.rest_0_.image_ref, f32[24,128]{1,0:T(8,128)S(1)} %collective-permute-done.10.image2_ref), custom_call_target="tpu_custom_call" | custom-call | tf_op jit(solution)/shard_map/finish/pallas_call | solution.py:727
  38.0 0.4 collective-permute-done.11.sums2_ref
  38.3 0.6 %penalty.1 = f32[1,1]{1,0:T(1,128)} custom-call(f32[8,128]{1,0:T(8,128)S(1)} %get-tuple-element.74.pen_ref, f32[8,128]{1,0:T(8,128)S(1)} %get-tuple-element.79.sums_ref, f32[8,128]{1,0:T(8,128)S(1)} %collective-permute-done.11.sums2_ref), custom_call_target="tpu_custom_call" | custom-call | tf_op jit(solution)/shard_map/penalty/pallas_call | solution.py:735
  (26 shorter events, 0.1 us)
Async XLA Ops:
  0.6 5.8 %copy-start = (bf16[24,2,22528]{2,1,0:T(2,128)(2,1)S(1)}, bf16[24,2,22528]{2,1,0:T(2,128)(2,1)}, u32[]{:S(2)}) copy-start(bf16[24,2,22528]{2,1,0:T(2,128)(2,1)} %param.14) | copy-start | bytes 6488068
  0.6 5.8 %copy-start.1 = (f32[24,2,512]{2,1,0:T(2,128)S(1)}, f32[24,2,512]{2,1,0:T(2,128)}, u32[]{:S(2)}) copy-start(f32[24,2,512]{2,1,0:T(2,128)} %param.18) | copy-start | bytes 294916
  0.7 5.8 %copy-start.6 = (f32[24]{0:T(128)S(1)}, f32[24]{0:T(128)}, u32[]{:S(2)}) copy-start(f32[24]{0:T(128)} %param.13) | copy-start | bytes 292
  0.7 5.8 %copy-start.4 = (s32[24,2,2,2]{0,3,2,1:T(2,128)S(1)}, s32[24,2,2,2]{0,3,2,1:T(2,128)}, u32[]{:S(2)}) copy-start(s32[24,2,2,2]{0,3,2,1:T(2,128)} %param.11) | copy-start | bytes 2308
  0.7 5.8 %copy-start.5 = (s32[3,24]{1,0:T(4,128)S(1)}, s32[3,24]{1,0:T(4,128)}, u32[]{:S(2)}) copy-start(s32[3,24]{1,0:T(4,128)} %nodes_ref.1) | copy-start | bytes 868
  3.5 5.1 %collective-permute-start = (f32[96,128]{1,0:T(8,128)S(1)}, f32[96,128]{1,0:T(8,128)S(1)}, u32[]{:S(2)}, u32[]{:S(2)}) collective-permute-start(f32[96,128]{1,0:T(8,128)S(1)} %get-tuple-element.53.pieces_ref), channel_id=1, source_target_pairs={{2,0},{0,2},{3,1},{1,3},{6,4},{4,6},{7,5},{5,7},{10,8},{8,10},{11,... | collective-permute-start | bytes 147464 | tf_op jit(solution)/shard_map/ppermute | solution.py:535
  8.9 4.9 %collective-permute-start.1 = (f32[24,128]{1,0:T(8,128)S(1)}, f32[24,128]{1,0:T(8,128)S(1)}, u32[]{:S(2)}, u32[]{:S(2)}) collective-permute-start(f32[24,128]{1,0:T(8,128)S(1)} %get-tuple-element.56.x_ref), channel_id=1, source_target_pairs={{0,16},{4,20},{8,24},{12,28},{16,0},{20,4},{24,8},{28,12},{1,17},{... | collective-permute-start | bytes 36872 | tf_op jit(solution)/shard_map/ppermute | solution.py:542
  13.9 3.1 %copy-start.2 = (f32[24,128]{1,0:T(8,128)S(1)}, f32[24,128]{1,0:T(8,128)}, u32[]{:S(2)}) copy-start(f32[24,128]{1,0:T(8,128)} %dual_ref.1) | copy-start | bytes 36868
  13.9 3.1 %copy-start.3 = (f32[24,128]{1,0:T(8,128)S(1)}, f32[24,128]{1,0:T(8,128)}, u32[]{:S(2)}) copy-start(f32[24,128]{1,0:T(8,128)} %rhs_ref.3) | copy-start | bytes 36868
  13.9 4.0 %collective-permute-start.2 = (f32[40,128]{1,0:T(8,128)S(1)}, f32[40,128]{1,0:T(8,128)S(1)}, u32[]{:S(2)}, u32[]{:S(2)}) collective-permute-start(f32[40,128]{1,0:T(8,128)S(1)} %merge.6.x_ref), channel_id=1, source_target_pairs={{0,8},{4,12},{8,0},{12,4},{16,24},{20,28},{24,16},{28,20},{1,9},{5... | collective-permute-start | bytes 61448 | tf_op jit(solution)/shard_map/ppermute | solution.py:542
  15.8 1.2 %collective-permute-start.3 = (f32[24,128]{1,0:T(8,128)S(1)}, f32[24,128]{1,0:T(8,128)S(1)}, u32[]{:S(2)}, u32[]{:S(2)}) collective-permute-start(f32[24,128]{1,0:T(8,128)S(1)} %image.2.rest_0_.image_ref), channel_id=1, source_target_pairs={{0,1},{1,0},{2,3},{3,2},{4,5},{5,4},{6,7},{7,6},{8,9},{9,8},{10,11... | collective-permute-start | bytes 36872 | tf_op jit(solution)/shard_map/ppermute | solution.py:539
  17.9 4.1 %collective-permute-start.4 = (f32[88,128]{1,0:T(8,128)S(1)}, f32[88,128]{1,0:T(8,128)S(1)}, u32[]{:S(2)}, u32[]{:S(2)}) collective-permute-start(f32[88,128]{1,0:T(8,128)S(1)} %merge.7.x_ref), channel_id=1, source_target_pairs={{0,4},{4,0},{8,12},{12,8},{16,20},{20,16},{24,28},{28,24},{1,5},{5... | collective-permute-start | bytes 135176 | tf_op jit(solution)/shard_map/ppermute | solution.py:542
  19.6 4.1 %collective-permute-start.6 = (f32[96,128]{1,0:T(8,128)S(1)}, f32[96,128]{1,0:T(8,128)S(1)}, u32[]{:S(2)}, u32[]{:S(2)}) collective-permute-start(f32[96,128]{1,0:T(8,128)S(1)} %get-tuple-element.59.rest_0_.pieces_ref), channel_id=1, source_target_pairs={{2,0},{0,2},{3,1},{1,3},{6,4},{4,6},{7,5},{5,7},{10,8},{8,10},{11,... | collective-permute-start | bytes 147464 | tf_op jit(solution)/shard_map/ppermute | solution.py:535
  22.5 1.2 %collective-permute-start.5 = (f32[8,128]{1,0:T(8,128)S(1)}, f32[8,128]{1,0:T(8,128)S(1)}, u32[]{:S(2)}, u32[]{:S(2)}) collective-permute-start(f32[8,128]{1,0:T(8,128)S(1)} %get-tuple-element.64.sums_ref), channel_id=1, source_target_pairs={{0,1},{1,0},{2,3},{3,2},{4,5},{5,4},{6,7},{7,6},{8,9},{9,8},{10,11... | collective-permute-start | bytes 12296 | tf_op jit(solution)/shard_map/ppermute | solution.py:539
  24.1 4.7 %collective-permute-start.7 = (f32[24,128]{1,0:T(8,128)S(1)}, f32[24,128]{1,0:T(8,128)S(1)}, u32[]{:S(2)}, u32[]{:S(2)}) collective-permute-start(f32[24,128]{1,0:T(8,128)S(1)} %get-tuple-element.70.x_ref), channel_id=1, source_target_pairs={{0,16},{4,20},{8,24},{12,28},{16,0},{20,4},{24,8},{28,12},{1,17},{... | collective-permute-start | bytes 36872 | tf_op jit(solution)/shard_map/ppermute | solution.py:542
  28.8 3.8 %collective-permute-start.8 = (f32[40,128]{1,0:T(8,128)S(1)}, f32[40,128]{1,0:T(8,128)S(1)}, u32[]{:S(2)}, u32[]{:S(2)}) collective-permute-start(f32[40,128]{1,0:T(8,128)S(1)} %merge.9.x_ref), channel_id=1, source_target_pairs={{0,8},{4,12},{8,0},{12,4},{16,24},{20,28},{24,16},{28,20},{1,9},{5... | collective-permute-start | bytes 61448 | tf_op jit(solution)/shard_map/ppermute | solution.py:542
  32.6 4.1 %collective-permute-start.9 = (f32[80,128]{1,0:T(8,128)S(1)}, f32[80,128]{1,0:T(8,128)S(1)}, u32[]{:S(2)}, u32[]{:S(2)}) collective-permute-start(f32[80,128]{1,0:T(8,128)S(1)} %merge.10.x_ref), channel_id=1, source_target_pairs={{0,4},{4,0},{8,12},{12,8},{16,20},{20,16},{24,28},{28,24},{1,5},{5... | collective-permute-start | bytes 122888 | tf_op jit(solution)/shard_map/ppermute | solution.py:542
  34.3 3.0 %collective-permute-start.10 = (f32[24,128]{1,0:T(8,128)S(1)}, f32[24,128]{1,0:T(8,128)S(1)}, u32[]{:S(2)}, u32[]{:S(2)}) collective-permute-start(f32[24,128]{1,0:T(8,128)S(1)} %image.3.rest_0_.image_ref), channel_id=1, source_target_pairs={{0,1},{1,0},{2,3},{3,2},{4,5},{5,4},{6,7},{7,6},{8,9},{9,8},{10,11... | collective-permute-start | bytes 36872 | tf_op jit(solution)/shard_map/ppermute | solution.py:539
  37.1 1.2 %collective-permute-start.11 = (f32[8,128]{1,0:T(8,128)S(1)}, f32[8,128]{1,0:T(8,128)S(1)}, u32[]{:S(2)}, u32[]{:S(2)}) collective-permute-start(f32[8,128]{1,0:T(8,128)S(1)} %get-tuple-element.79.sums_ref), channel_id=1, source_target_pairs={{0,1},{1,0},{2,3},{3,2},{4,5},{5,4},{6,7},{7,6},{8,9},{9,8},{10,11... | collective-permute-start | bytes 12296 | tf_op jit(solution)/shard_map/ppermute | solution.py:539
